TPU v7x, 32 devices: a whole 2x2x4 slice. The times are simulated.
32 devices in a mesh: section: 2 (over y), dp: 16 (over z, x, core).
Axes of the slice: x: 2, y: 2, z: 4, core: 2. Of those that a mesh axis runs over, the one named last changes fastest.
Arguments:
- activations: bfloat16 [2, 2048, 8192], P('section', 'dp'), may hold values from -6 to 6
- cotangent: bfloat16 [2048, 8192], P('dp'), may hold values from -6 to 6
- token_ids: int32 [2048], P('dp'), may hold values from 0 to 30527, as said below
- gains: float32 [2, 8192], P('section'), may hold values from 0.1 to 1.9
- factors: bfloat16 [2, 4, 64, 128, 128], P('section'), may hold values from -0.5 to 0.5
- monarch_perm: int32 [2, 8192], P('section'), may hold values from 0 to 8191, each once within a row
Outputs:
- grad_acts: bfloat16 [2, 2048, 8192], P('section', 'dp')
- factor_grads: float32 [2, 4, 64, 128, 128], P('section', None, 'dp')
- gain_grads: float32 [2, 8192], P('section', 'dp')
Inputs may be any that keep to these rules, and one draw needn't show every extreme that they name: `token_ids`: 0 marks padding; in each device's block of 128 tokens the padding is a tail, possibly empty, of at most three quarters of the block; other ids lie in 1 to 30527. `monarch_perm`: each row is a permutation of 0 to 8191.
All inputs are finite; a program needn't handle non-finite values.
Results may differ from a plain program's by a relative error of at most 0.01.
Values may be sent and summed in bfloat16 or wider, within the bound.
No kernel may reach another device: no remote copies, remote signals or barrier semaphores. Data moves between devices by JAX's collectives and lax.ppermute only.
A program may use at most 192 MiB of HBM per device.

v0:
```python
import jax
import jax.numpy as jnp
from jax import lax
from jax.sharding import PartitionSpec as P

inv_sqrt_two = 0.7071067811865476
inv_sqrt_two_pi = 0.3989422804014327


def shifted(block, axis, distance):
    devices = range(lax.axis_size(axis))
    route = [(i - distance, i) for i in devices if i - distance in devices]
    return lax.ppermute(block, axis, route)


def block_mul(rows, factor):
    split = rows.reshape(rows.shape[0], factor.shape[0], factor.shape[1])
    out = jnp.einsum("rki,kij->rkj", split, factor, preferred_element_type=jnp.float32)
    return out.reshape(rows.shape[0], rows.shape[1])


def block_mul_t(rows, factor):
    split = rows.reshape(rows.shape[0], factor.shape[0], factor.shape[1])
    out = jnp.einsum("rkj,kij->rki", split, factor, preferred_element_type=jnp.float32)
    return out.reshape(rows.shape[0], rows.shape[1])


def block_grad(left, right, blocks, size):
    lsplit = left.reshape(left.shape[0], blocks, size)
    rsplit = right.reshape(right.shape[0], blocks, size)
    return jnp.einsum("rki,rkj->kij", lsplit, rsplit, preferred_element_type=jnp.float32)


def section_backward(x, grad_out, gamma, factor, perm, inverse):
    blocks, size = (factor.shape[1], factor.shape[2])
    xf = x.astype(jnp.float32)
    scale = lax.rsqrt(jnp.mean(xf * xf, axis=1, keepdims=True) + 1e-06)
    zed = xf * scale
    normed = (zed * gamma).astype(jnp.bfloat16)
    first = block_mul(normed, factor[0]).astype(jnp.bfloat16)
    first_p = jnp.take(first, perm, axis=1)
    pre = block_mul(first_p, factor[1])
    cdf = 0.5 * (1.0 + jax.scipy.special.erf(pre * inv_sqrt_two))
    hidden = (pre * cdf).astype(jnp.bfloat16)
    second = block_mul(hidden, factor[2]).astype(jnp.bfloat16)
    second_p = jnp.take(second, perm, axis=1)
    grad_three = block_grad(second_p, grad_out, blocks, size)
    grad_sp = block_mul_t(grad_out, factor[3]).astype(jnp.bfloat16)
    grad_second = jnp.take(grad_sp, inverse, axis=1)
    grad_two = block_grad(hidden, grad_second, blocks, size)
    grad_hidden = block_mul_t(grad_second, factor[2])
    slope = cdf + pre * jnp.exp(-0.5 * pre * pre) * inv_sqrt_two_pi
    grad_pre = (grad_hidden * slope).astype(jnp.bfloat16)
    grad_one = block_grad(first_p, grad_pre, blocks, size)
    grad_fp = block_mul_t(grad_pre, factor[1]).astype(jnp.bfloat16)
    grad_first = jnp.take(grad_fp, inverse, axis=1)
    grad_zero = block_grad(normed, grad_first, blocks, size)
    grad_normed = block_mul_t(grad_first, factor[0])
    grad_gamma = jnp.sum(grad_normed * zed, axis=0)
    grad_zed = grad_normed * gamma
    inner = jnp.mean(grad_zed * zed, axis=1, keepdims=True)
    grad_x = (grad_out.astype(jnp.float32) + scale * (grad_zed - zed * inner)).astype(jnp.bfloat16)
    return (grad_x, jnp.stack([grad_zero, grad_one, grad_two, grad_three]), grad_gamma)


def replica_sum(grads, grad_gamma):
    return (
        lax.psum_scatter(grads[None], "dp", scatter_dimension=2, tiled=True),
        lax.psum_scatter(grad_gamma[None], "dp", scatter_dimension=1, tiled=True),
    )


def on_device(activations, cotangent, token_ids, gains, factors, monarch_perm):
    x_all = activations[0]
    gamma = gains[0]
    factor = factors[0]
    perm = monarch_perm[0]
    width = perm.shape[0]
    inverse = jnp.zeros((width,), jnp.int32).at[perm].set(jnp.arange(width, dtype=jnp.int32))
    live = (token_ids != 0).astype(jnp.bfloat16)
    seeded = cotangent * live[:, None]
    sections = lax.axis_size("section")
    replicas = lax.axis_size("dp")
    here = lax.axis_index("section")
    micro = 1
    rows = x_all.shape[0] // micro
    ticks = micro + sections - 1
    carried = jnp.zeros((rows, width), jnp.bfloat16)
    out_grad = jnp.zeros_like(x_all)
    total_grads = jnp.zeros(factor.shape, jnp.float32)
    total_gamma = jnp.zeros((width,), jnp.float32)
    for tick in range(ticks):
        index = tick - (sections - 1 - here)
        valid = jnp.logical_and(index >= 0, index < micro)
        grad_out = jnp.where(here == sections - 1, seeded, carried)

        def active(operands):
            return section_backward(operands[0], operands[1], gamma, factor, perm, inverse)

        def resting(operands):
            return (
                jnp.zeros((rows, width), jnp.bfloat16),
                jnp.zeros(factor.shape, jnp.float32),
                jnp.zeros((width,), jnp.float32),
            )

        grad_x, grads, grad_gamma = lax.cond(valid, active, resting, (x_all, grad_out))
        out_grad = jnp.where(valid, grad_x, out_grad)
        if tick + 1 < ticks:
            carried = shifted(grad_x, "section", -1)
        total_grads = total_grads + grads
        total_gamma = total_gamma + grad_gamma
    shard_grads, shard_gamma = replica_sum(total_grads, total_gamma)
    return (out_grad[None], shard_grads / replicas, shard_gamma / replicas)


def solution(mesh):
    in_specs = (
        P("section", "dp", None),
        P("dp", None),
        P("dp"),
        P("section", None),
        P("section", None, None, None, None),
        P("section", None),
    )
    out_specs = (P("section", "dp", None), P("section", None, "dp", None, None), P("section", "dp"))
    return jax.shard_map(
        on_device, mesh=mesh, in_specs=in_specs, out_specs=out_specs, check_vma=False
    )
```

profile of v0, /device:TPU:0, one launch (start us, length us, event | category | flops | bytes accessed | tf_op | source)
XLA Modules:
  0.0 935.0 jit_solution(14036009690081980755)
XLA Ops:
  18.4 30.5 %scatter_custom_fusion = s32[8192]{0:T(1024)S(1)} fusion(s32[8192]{0:T(1024)S(1)} %bitcast.269, s32[8192]{0:T(1024)S(1)} %iota.3, s32[]{:T(128)} %constant.57.clone.1), kind=kCustom, calls=%fused_computation.146 | custom fusion | bytes 32772 | tf_op jit(solution)/shard_map/scatter | solution.py:79
  50.4 20.8 %conditional.2 = (bf16[128,8192]{0,1:T(8,128)(2,1)}, f32[4,64,128,128]{3,2,1,0:T(8,128)}, f32[8192]{0:T(1024)S(1)}, bf16[128,8192]{1,0:T(8,128)(2,1)}) conditional(s32[]{:T(128)} %convert_element_type.123, () %tuple.26, (pred[]{:T(512)}, bf16[128,8192]{0,1:T(8,128)(2,1)}, bf16[128,8192]{1,0:T(8,128)(2,1)}, bf16[128,8192]{0,1:T(8,128)(2,1)S(1)}, ...), branch_computations={%region_1.2_spmd, %region_2.7_spmd} | conditional | flops 3014811648 | bytes 369612288 | solution.py:107
  50.4 7.9 broadcast.116
  72.6 251.6 %collective-permute-done = bf16[128,8192]{0,1:T(8,128)(2,1)S(1)} collective-permute-done((bf16[128,8192]{0,1:T(8,128)(2,1)}, bf16[128,8192]{0,1:T(8,128)(2,1)S(1)}, u32[]{:S(2)}, u32[]{:S(2)}) %collective-permute-start) | collective-permute-done | bytes 2097184 | tf_op jit(solution)/shard_map/ppermute | solution.py:13
  324.1 223.9 %conditional.3 = (f32[4,64,128,128]{3,2,1,0:T(8,128)}, f32[8192]{0:T(1024)S(1)}, bf16[128,8192]{1,0:T(8,128)(2,1)}) conditional(s32[]{:T(128)} %convert_element_type.121, () %tuple.25, (pred[]{:T(512)}, bf16[128,8192]{0,1:T(8,128)(2,1)}, bf16[128,8192]{0,1:T(8,128)(2,1)S(1)}, bf16[128,8192]{0,1:T(8,128)(2,1)}, bf16[4,64,128,128]{3,2,1,0:T(8,128)(2,1)}, ...), branch_computations={%region_6.8_spmd, %region_7.12_spmd} | conditional | flops 3014811648 | bytes 398972576 | solution.py:107
  327.6 4.4 fusion.52
  332.0 12.0 %copy.81 = bf16[4,64,128,128]{2,3,1,0:T(8,128)(2,1)} copy(bf16[4,64,128,128]{3,2,1,0:T(8,128)(2,1)} %get-tuple-element.49) | data formatting | bytes 16777216 | tf_op jit(solution)/shard_map
  347.0 29.4 %gather_fusion.5 = bf16[8192,128]{1,0:T(8,128)(2,1)} fusion(bf16[128,8192]{0,1:T(8,128)(2,1)S(1)} %bitcast.225, s32[8192]{0:T(1024)S(1)} %get-tuple-element.108), kind=kCustom, calls=%fused_computation.5.clone | custom fusion | bytes 4227072 | tf_op jit(solution)/shard_map/cond/branch_1_fun/jit(_take)/gather | solution.py:41
  376.4 5.8 broadcast_select_fusion.8
  382.3 6.2 fusion.69
  391.8 29.4 %gather_fusion.4 = bf16[8192,128]{1,0:T(8,128)(2,1)} fusion(bf16[128,8192]{0,1:T(8,128)(2,1)S(1)} %bitcast.230, s32[8192]{0:T(1024)S(1)} %get-tuple-element.109), kind=kCustom, calls=%fused_computation.4.clone | custom fusion | bytes 4227072 | tf_op jit(solution)/shard_map/cond/branch_1_fun/jit(_take)/gather | solution.py:49
  421.2 6.0 broadcast_select_fusion.5
  427.2 4.4 fusion.65
  435.6 29.4 %gather_fusion.6 = bf16[8192,128]{1,0:T(8,128)(2,1)} fusion(bf16[128,8192]{0,1:T(8,128)(2,1)S(1)} %bitcast.231, s32[8192]{0:T(1024)S(1)} %get-tuple-element.109), kind=kCustom, calls=%fused_computation.6.clone | custom fusion | bytes 4227072 | tf_op jit(solution)/shard_map/cond/branch_1_fun/jit(_take)/gather | solution.py:56
  465.1 5.8 broadcast_select_fusion.6
  476.9 4.7 fusion.57
  481.6 4.3 copy.125
  485.9 4.4 convolution_bitcast_fusion.6
  500.7 29.4 %gather_fusion.7 = bf16[8192,128]{1,0:T(8,128)(2,1)} fusion(bf16[128,8192]{0,1:T(8,128)(2,1)S(1)} %bitcast.228, s32[8192]{0:T(1024)S(1)} %get-tuple-element.108), kind=kCustom, calls=%fused_computation.7.clone | custom fusion | bytes 4227072 | tf_op jit(solution)/shard_map/cond/branch_1_fun/jit(_take)/gather | solution.py:46
  530.2 6.0 broadcast_select_fusion.7
  539.6 8.1 pad_maximum_fusion.1
  550.8 19.2 %add_bitcast_fusion = f32[1,4,64,128,128]{4,3,2,1,0:T(8,128)} fusion(f32[4,64,128,128]{3,2,1,0:T(8,128)} %get-tuple-element.64, f32[4,64,128,128]{3,2,1,0:T(8,128)} %get-tuple-element.65), kind=kLoop, calls=%fused_computation.141 | loop fusion | flops 4194304 | bytes 50331648 | tf_op jit(solution)/shard_map/broadcast_in_dim | solution.py:68
  575.1 48.5 %reduce-scatter.7.cloned.1.call-done = f32[512,1]{1,0:T(8,128)} async-done(((f32[8192,1]{1,0:T(8,128)}), f32[512,1]{1,0:T(8,128)}) %reduce-scatter.7.cloned.1.call-update) | async-done | bytes 2064
  625.2 300.2 %all-reduce.3.cloned.1.call-done = f32[1,4,64,128,128]{4,3,2,1,0:T(8,128)} async-done(((f32[1,4,64,128,128]{4,3,2,1,0:T(8,128)}), f32[1,4,64,128,128]{4,3,2,1,0:T(8,128)}) %all-reduce.3.cloned.1.call-update) | async-done | bytes 16777232
  (87 shorter events, 61.7 us)
Async XLA Ops:
  7.2 616.4 %reduce-scatter.7.cloned.1.call-start = ((), (), s32[]{:S(2)}) async-start(), calls=%async_computation.1 | async-start | bytes 4456448
  7.2 4.1 copy-start.39
  11.3 3.2 copy-start.38
  14.6 35.8 %copy-start = (bf16[1,128,8192]{1,2,0:T(8,128)(2,1)}, bf16[1,128,8192]{1,2,0:T(8,128)(2,1)S(1)}, u32[]{:S(2)}) copy-start(bf16[1,128,8192]{1,2,0:T(8,128)(2,1)S(1)} %copy.92) | copy-start | bytes 6291460
  18.4 32.0 %copy-start.37 = (f32[1,8192]{1,0:T(1,128)S(1)}, f32[1,8192]{1,0:T(1,128)}, u32[]{:S(2)}) copy-start(f32[1,8192]{1,0:T(1,128)} %param.15) | copy-start | bytes 98308
  71.2 252.9 %collective-permute-start = (bf16[128,8192]{0,1:T(8,128)(2,1)}, bf16[128,8192]{0,1:T(8,128)(2,1)S(1)}, u32[]{:S(2)}, u32[]{:S(2)}) collective-permute-start(bf16[128,8192]{0,1:T(8,128)(2,1)} %get-tuple-element.62), channel_id=1, source_target_pairs={{16,0},{17,1},{18,2},{19,3},{20,4},{21,5},{22,6},{23,7},{24,8},{25... | collective-permute-start | bytes 6291464 | tf_op jit(solution)/shard_map/ppermute | solution.py:13
  324.1 7.9 copy-start.35
  324.1 3.5 copy-start.3
  382.2 6.3 copy-start.16
  382.3 6.3 copy-start.11
  382.3 6.2 copy-start.36
  421.2 6.0 copy-start.34
  427.2 4.5 copy-start.29
  431.7 4.0 copy-start.28
  470.9 3.3 copy-start.22
  470.9 3.3 copy-start.4
  481.6 4.3 copy-start.17
  485.9 4.4 copy-start.14
  485.9 4.4 copy-start.23
  490.3 3.6 copy-start.12
  490.3 3.6 copy-start.30
  530.2 6.0 copy-start.9
  536.2 3.5 copy-start.26
  550.8 374.6 %all-reduce.3.cloned.1.call-start = ((), (), s32[]{:S(2)}) async-start(), calls=%async_computation.2 | async-start | bytes 33554432
  (4 other events, 8.6 us)
Sparse Core Ops, SparseCore 0:
  550.9 72.5 reduce-scatter.6
  627.9 297.3 all-reduce.2
where the time goes:
time: 939 us; the launch traced here: 935 us
  waiting for transfers between devices  600 us (64%)
  local copies, waits for them, and re-layouts  191 us (20%)
  other arithmetic  76.2 us (8%)
  matrix products  40.2 us (4%)
  between operations  15.3 us (2%)
  loops' own time  10.4 us (1%)
    unnamed x4, waiting for transfers between devices  349 us
    ppermute x1, waiting for transfers between devices, shifted(): return lax.ppermute(block, axis, route)  252 us
    scatter x1, local copies, waits for them, and re-layouts, on_device(): jnp.zeros((width,), jnp.int32).at[perm]  30.5 us
    gather x1, local copies, waits for them, and re-layouts, section_backward(): second_p = jnp.take(second, perm, axis=1)  29.4 us
    gather x1, local copies, waits for them, and re-layouts, section_backward(): first_p = jnp.take(first, perm, axis=1)  29.4 us
    gather x1, local copies, waits for them, and re-layouts, section_backward(): grad_first = jnp.take(grad_fp, inverse, axis=1)  29.4 us
    gather x1, local copies, waits for them, and re-layouts, section_backward(): grad_second = jnp.take(grad_sp, inverse, axis=1)  29.4 us
    another operation x6, local copies, waits for them, and re-layouts  24.4 us
  transfers between devices with their start and end apart: 3, of which 3 were waited for; matrix products, arithmetic and copies ran while one was open for 3% of the time, Pallas kernels for 0%

commit v1 on v0

v1 whole, which is shorter than its diff:
```python
import functools

import jax
import jax.numpy as jnp
from jax import lax
from jax.experimental import pallas as pl
from jax.experimental.pallas import tpu as pltpu
from jax.sharding import PartitionSpec as P

F32 = jnp.float32
BF16 = jnp.bfloat16
inv_sqrt_two = 0.7071067811865476
inv_sqrt_two_pi = 0.3989422804014327
STEP = 8
VMEM_BYTES = 44 << 20


def dot(a, b, ca, cb):
    return lax.dot_general(a, b, (((ca,), (cb,)), ((), ())), preferred_element_type=F32)


def whole(*shape):
    return pl.BlockSpec(shape, lambda *_: (0,) * len(shape))


def call(body, name, grid, in_specs, out_specs, out_shape, scratch=(), prefetch=1):
    return pl.pallas_call(
        body,
        name=name,
        out_shape=out_shape,
        grid_spec=pltpu.PrefetchScalarGridSpec(
            num_scalar_prefetch=prefetch,
            grid=grid,
            in_specs=in_specs,
            out_specs=out_specs,
            scratch_shapes=scratch,
        ),
        compiler_params=pltpu.CompilerParams(vmem_limit_bytes=VMEM_BYTES),
    )


def rounded(v):
    return v.astype(BF16).astype(F32)


def normed_block(x, scale, gamma, cols):
    return (x[:, cols].astype(F32) * scale[...] * gamma[:, cols]).astype(BF16)


def gather_rows(perm, base, source, target, count):
    for i in range(count):
        target[pl.ds(i, 1), :] = source[pl.ds(perm[base + i], 1), :]


def scatter_rows(perm, base, source, target, count):
    for i in range(count):
        target[pl.ds(perm[base + i], 1), :] = source[pl.ds(i, 1), :]


def forward_first(perm, x, gamma, fac, ap_t, h_t, slope_t, scale, a_t, rows):
    phase, c = pl.program_id(0), pl.program_id(1)
    bs = fac.shape[2]
    blocks = x.shape[1] // bs

    @pl.when(jnp.logical_and(phase == 0, c == 0))
    def _():
        def add(k, acc):
            xk = x[:, pl.ds(pl.multiple_of(k * bs, bs), bs)].astype(F32)
            return acc + xk * xk

        acc = lax.fori_loop(0, blocks, add, jnp.zeros((x.shape[0], bs), F32), unroll=8)
        mean = jnp.sum(acc, axis=1, keepdims=True) / x.shape[1]
        scale[...] = jnp.broadcast_to(lax.rsqrt(mean + 1e-06), scale.shape)

    @pl.when(phase == 0)
    def _():
        for k in range(STEP):
            at = pl.multiple_of((c * STEP + k) * bs, bs)
            n = normed_block(x, scale, gamma, pl.ds(at, bs))
            a_t[pl.ds(at, bs), :] = rounded(dot(fac[0, k], n, 0, 1))

    @pl.when(phase == 1)
    def _():
        for k in range(STEP):
            at = pl.multiple_of((c * STEP + k) * bs, bs)
            gather_rows(perm, at, a_t, rows.at[k], bs)
            ap = rows[k].astype(BF16)
            ap_t[pl.ds(k * bs, bs), :] = ap
            pre = dot(fac[0, k], ap, 0, 0)
            cdf = 0.5 * (1.0 + lax.erf(pre * inv_sqrt_two))
            h_t[pl.ds(k * bs, bs), :] = (pre * cdf).astype(BF16)
            slope_t[pl.ds(k * bs, bs), :] = cdf + pre * jnp.exp(-0.5 * pre * pre) * inv_sqrt_two_pi


def forward_second(perm, h_t, fac, cp_t, c_t, rows):
    phase, c = pl.program_id(0), pl.program_id(1)
    bs = fac.shape[2]

    @pl.when(phase == 0)
    def _():
        for k in range(STEP):
            at = pl.multiple_of((c * STEP + k) * bs, bs)
            c_t[pl.ds(at, bs), :] = rounded(dot(fac[0, k], h_t[pl.ds(k * bs, bs), :], 0, 0))

    @pl.when(phase == 1)
    def _():
        for k in range(STEP):
            at = pl.multiple_of((c * STEP + k) * bs, bs)
            gather_rows(perm, at, c_t, rows.at[k], bs)
            cp_t[pl.ds(k * bs, bs), :] = rows[k].astype(BF16)


def backward_data(perm, cot, live, slope_t, fac, fac_one, x, scale, gamma, grad_x, gc_t, ga_t, gn, rows):
    phase, c = pl.program_id(0), pl.program_id(1)
    bs = fac.shape[2]
    blocks = x.shape[1] // bs

    def gy_block(cols):
        return (cot[:, cols].astype(F32) * live[...]).astype(BF16)

    @pl.when(phase == 0)
    def _():
        for k in range(STEP):
            at = pl.multiple_of((c * STEP + k) * bs, bs)
            rows[k] = rounded(dot(fac[0, k], gy_block(pl.ds(at, bs)), 1, 1))
            scatter_rows(perm, at, rows.at[k], gc_t, bs)

    @pl.when(phase == 1)
    def _():
        for k in range(STEP):
            at = pl.multiple_of((c * STEP + k) * bs, bs)
            gh = dot(fac[0, k], gc_t[pl.ds(at, bs), :].astype(BF16), 1, 0)
            gpre = (gh * slope_t[pl.ds(k * bs, bs), :]).astype(BF16)
            rows[k] = rounded(dot(fac_one[0, k], gpre, 1, 0))
            scatter_rows(perm, at, rows.at[k], ga_t, bs)

    @pl.when(phase == 2)
    def _():
        for k in range(STEP):
            at = pl.multiple_of((c * STEP + k) * bs, bs)
            gn[:, pl.ds(at, bs)] = dot(ga_t[pl.ds(at, bs), :].astype(BF16), fac[0, k], 0, 1)

    @pl.when(jnp.logical_and(phase == 2, c == pl.num_programs(1) - 1))
    def _():
        finish(lambda cols: gy_block(cols), x, scale, gamma, gn, grad_x, blocks, bs)


def finish(gy_block, x, scale, gamma, gn, grad_x, blocks, bs):
    def add(k, acc):
        cols = pl.ds(pl.multiple_of(k * bs, bs), bs)
        z = x[:, cols].astype(F32) * scale[...]
        return acc + gn[:, cols] * gamma[:, cols] * z

    acc = lax.fori_loop(0, blocks, add, jnp.zeros((x.shape[0], bs), F32), unroll=8)
    inner = jnp.broadcast_to(jnp.sum(acc, axis=1, keepdims=True) / x.shape[1], acc.shape)

    def emit(k, _):
        cols = pl.ds(pl.multiple_of(k * bs, bs), bs)
        z = x[:, cols].astype(F32) * scale[...]
        grad = gy_block(cols).astype(F32) + scale[...] * (gn[:, cols] * gamma[:, cols] - z * inner)
        grad_x[:, cols] = grad.astype(BF16)
        return 0

    lax.fori_loop(0, blocks, emit, 0, unroll=4)


def split_blocks(flags, own):
    for k in range(STEP // 2):
        group, within = divmod(k, own)
        base = group * 2 * own + within
        yield k, base + flags[0] * own, base + (1 - flags[0]) * own


def chosen_gy(flags, cot, live, moved, cols):
    seeded = (cot[:, cols].astype(F32) * live[...]).astype(BF16)
    return jnp.where(flags[1] == 1, seeded, moved[:, cols])


def backward_three(own, perm, flags, cot, live, moved, cp_t, fac, keep, send, gc_out, gc_t, rows):
    c = pl.program_id(0)
    bs = fac.shape[2]

    def gy_block(k):
        return chosen_gy(flags, cot, live, moved, pl.ds(pl.multiple_of((c * STEP + k) * bs, bs), bs))

    for k in range(STEP):
        rows[k] = rounded(dot(fac[0, k], gy_block(k), 1, 1))
        scatter_rows(perm, pl.multiple_of((c * STEP + k) * bs, bs), rows.at[k], gc_t, bs)
    for k, stays, goes in split_blocks(flags, own):
        for out, block in ((keep, stays), (send, goes)):
            left = cp_t[pl.ds(pl.multiple_of(block * bs, bs), bs), :]
            out[k] = dot(left, gy_block(block), 1, 0).astype(BF16)

    @pl.when(c == pl.num_programs(0) - 1)
    def _():
        gc_out[...] = gc_t[...].astype(BF16)


def backward_two_one(own, perm, flags, gc_t, h_t, ap_t, slope_t, fac_two, fac_one, keep_two, send_two, keep_one, send_one, ga_out, ga_t, gpre, rows):
    c = pl.program_id(0)
    bs = fac_two.shape[2]
    for k in range(STEP):
        here = pl.ds(k * bs, bs)
        gh = dot(fac_two[0, k], gc_t[here, :], 1, 0)
        gpre[here, :] = (gh * slope_t[here, :]).astype(BF16)
        rows[k] = rounded(dot(fac_one[0, k], gpre[here, :], 1, 0))
        scatter_rows(perm, pl.multiple_of((c * STEP + k) * bs, bs), rows.at[k], ga_t, bs)
    for k, stays, goes in split_blocks(flags, own):
        for two, one, block in ((keep_two, keep_one, stays), (send_two, send_one, goes)):
            at = pl.ds(pl.multiple_of(block * bs, bs), bs)
            two[k] = dot(h_t[at, :], gc_t[at, :], 1, 1).astype(BF16)
            one[k] = dot(ap_t[at, :], gpre[at, :], 1, 1).astype(BF16)

    @pl.when(c == pl.num_programs(0) - 1)
    def _():
        ga_out[...] = ga_t[...].astype(BF16)


def backward_zero(own, flags, ga_t, x, scale, gamma, keep, send):
    c = pl.program_id(0)
    bs = x.shape[1] // (pl.num_programs(0) * STEP)
    for k, stays, goes in split_blocks(flags, own):
        for out, block in ((keep, stays), (send, goes)):
            at = pl.multiple_of(block * bs, bs)
            n = normed_block(x, scale, gamma, pl.ds(pl.multiple_of(c * STEP * bs + at, bs), bs))
            out[k] = dot(ga_t[pl.ds(at, bs), :], n, 1, 0).astype(BF16)


def backward_last(flags, ga_t, cot, live, moved, x, scale, gamma, fac, grad_x, grad_gamma, gn):
    c = pl.program_id(0)
    bs = fac.shape[2]
    blocks = x.shape[1] // bs
    for k in range(STEP):
        cols = pl.ds(pl.multiple_of((c * STEP + k) * bs, bs), bs)
        value = dot(ga_t[pl.ds(k * bs, bs), :], fac[0, k], 0, 1)
        gn[:, cols] = value
        z = x[:, cols].astype(F32) * scale[...]
        grad_gamma[:, pl.ds(k * bs, bs)] = jnp.sum(value * z, axis=0, keepdims=True)

    @pl.when(c == pl.num_programs(0) - 1)
    def _():
        finish(lambda cols: chosen_gy(flags, cot, live, moved, cols), x, scale, gamma, gn, grad_x, blocks, bs)


def halved(keep, send, stage, own, me, replicas):
    came = lax.ppermute(send, "dp", [(i, i ^ (1 << stage)) for i in range(replicas)])
    if (2 << stage) == replicas:
        return keep.astype(F32) + came.astype(F32), None
    split = (keep.shape[0] // (2 * own), 2, own) + keep.shape[1:]
    bit = (me >> (stage + 1)) & 1

    def part(which):
        a = lax.dynamic_index_in_dim(keep.reshape(split), which, 1, keepdims=False)
        b = lax.dynamic_index_in_dim(came.reshape(split), which, 1, keepdims=False)
        total = (a.astype(F32) + b.astype(F32)).astype(keep.dtype)
        return total.reshape((split[0] * own,) + keep.shape[1:])

    return part(bit), part(1 - bit)


def summed(keep, send, own, me, replicas):
    for stage in range(replicas.bit_length() - 1):
        keep, send = halved(keep, send, stage, own, me, replicas)
    return keep / replicas


def on_device(replicas, sections, activations, cotangent, token_ids, gains, factors, monarch_perm):
    x = activations[0]
    gamma = gains
    fac = factors[0]
    perm = monarch_perm[0]
    tokens, width = x.shape
    blocks, bs = fac.shape[1], fac.shape[2]
    own = blocks // replicas
    steps = blocks // STEP
    here = lax.axis_index("section")
    me = lax.axis_index("dp")
    live = jnp.broadcast_to((token_ids != 0).astype(F32)[:, None], (tokens, bs))
    flags = jnp.stack([me & 1, (here == sections - 1).astype(jnp.int32)])

    tok = whole(tokens, width)
    sca = whole(tokens, bs)
    gam = whole(1, width)
    chunk = (STEP * bs, tokens)
    fblock = (1, STEP, bs, bs)
    f_at = lambda which: pl.BlockSpec(fblock, lambda c, *_: (which, c, 0, 0))
    c_at = pl.BlockSpec(chunk, lambda c, *_: (c, 0))
    feat = lambda dt: jax.ShapeDtypeStruct((width, tokens), dt)
    half = jax.ShapeDtypeStruct((blocks // 2, bs, bs), BF16)
    half_at = pl.BlockSpec((STEP // 2, bs, bs), lambda c, *_: (c, 0, 0))
    big = pltpu.VMEM((width, tokens), F32)
    rows = pltpu.VMEM((STEP, bs, tokens), F32)
    late = pl.BlockSpec(chunk, lambda ph, c, *_: (ph * c, 0))

    ap_t, h_t, slope_t, scale = call(
        forward_first,
        "forward_first",
        (2, steps),
        [tok, gam, pl.BlockSpec(fblock, lambda ph, c, *_: (ph, c, 0, 0))],
        [late, late, late, sca],
        [feat(BF16), feat(BF16), feat(F32), jax.ShapeDtypeStruct((tokens, bs), F32)],
        [big, rows],
    )(perm, x, gamma, fac)

    which = lambda ph: jnp.where(ph == 0, 3, jnp.where(ph == 1, 2, 0))
    mid = lambda ph, c: jnp.where(ph == 0, 0, jnp.where(ph == 1, c, steps - 1))
    grad_x = call(
        backward_data,
        "backward_data",
        (3, steps),
        [
            tok,
            sca,
            pl.BlockSpec(chunk, lambda ph, c, *_: (mid(ph, c), 0)),
            pl.BlockSpec(fblock, lambda ph, c, *_: (which(ph), c, 0, 0)),
            pl.BlockSpec(fblock, lambda ph, c, *_: (1, mid(ph, c), 0, 0)),
            tok,
            sca,
            gam,
        ],
        tok,
        jax.ShapeDtypeStruct((tokens, width), BF16),
        [big, big, pltpu.VMEM((tokens, width), F32), rows],
    )(perm, cotangent, live, slope_t, fac, fac, x, scale, gamma)
    moved = lax.ppermute(grad_x, "section", [(i, i - 1) for i in range(1, sections)])

    cp_t = call(
        forward_second,
        "forward_second",
        (2, steps),
        [
            pl.BlockSpec(chunk, lambda ph, c, *_: (jnp.where(ph == 0, c, steps - 1), 0)),
            pl.BlockSpec(fblock, lambda ph, c, *_: (2, jnp.where(ph == 0, c, steps - 1), 0, 0)),
        ],
        late,
        feat(BF16),
        [big, rows],
    )(perm, h_t, fac)

    keep_three, send_three, gc_t = call(
        functools.partial(backward_three, own),
        "backward_three",
        (steps,),
        [tok, sca, tok, c_at, f_at(3)],
        [half_at, half_at, whole(width, tokens)],
        [half, half, feat(BF16)],
        [big, rows],
        prefetch=2,
    )(perm, flags, cotangent, live, moved, cp_t, fac)
    keep_two, send_two, keep_one, send_one, ga_t = call(
        functools.partial(backward_two_one, own),
        "backward_two_one",
        (steps,),
        [c_at, c_at, c_at, c_at, f_at(2), f_at(1)],
        [half_at] * 4 + [whole(width, tokens)],
        [half] * 4 + [feat(BF16)],
        [big, pltpu.VMEM(chunk, BF16), rows],
        prefetch=2,
    )(perm, flags, gc_t, h_t, ap_t, slope_t, fac, fac)
    keep_zero, send_zero = call(
        functools.partial(backward_zero, own),
        "backward_zero",
        (steps,),
        [c_at, tok, sca, gam],
        [half_at, half_at],
        [half, half],
    )(flags, ga_t, x, scale, gamma)
    out_grad, grad_gamma = call(
        backward_last,
        "backward_last",
        (steps,),
        [c_at, tok, sca, tok, tok, sca, gam, f_at(0)],
        [tok, pl.BlockSpec((1, STEP * bs), lambda c, *_: (0, c))],
        [jax.ShapeDtypeStruct((tokens, width), BF16), jax.ShapeDtypeStruct((1, width), F32)],
        [pltpu.VMEM((tokens, width), F32)],
    )(flags, ga_t, cotangent, live, moved, x, scale, gamma, fac)

    total = [
        summed(keep, send, own, me, replicas)
        for keep, send in ((keep_zero, send_zero), (keep_one, send_one), (keep_two, send_two), (keep_three, send_three))
    ]
    total[0] = jnp.swapaxes(total[0], 1, 2)
    pieces = grad_gamma.reshape(replicas // 2, 2, width // replicas)
    gamma_keep = lax.dynamic_index_in_dim(pieces, me & 1, 1, keepdims=False)
    gamma_send = lax.dynamic_index_in_dim(pieces, 1 - (me & 1), 1, keepdims=False)
    gamma_total = summed(gamma_keep, gamma_send, 1, me, replicas)
    return (out_grad[None], jnp.stack(total)[None], gamma_total)


def solution(mesh):
    replicas, sections = mesh.shape["dp"], mesh.shape["section"]
    in_specs = (
        P("section", "dp", None),
        P("dp", None),
        P("dp"),
        P("section", None),
        P("section", None, None, None, None),
        P("section", None),
    )
    out_specs = (P("section", "dp", None), P("section", None, "dp", None, None), P("section", "dp"))
    return jax.shard_map(
        functools.partial(on_device, replicas, sections),
        mesh=mesh,
        in_specs=in_specs,
        out_specs=out_specs,
        check_vma=False,
    )
```

time: 939 us -> 252 us (0.27)
  waiting for transfers between devices: 600 us -> 76.1 us
  local copies, waits for them, and re-layouts: 191 us -> 10.9 us
  Pallas kernels: 0 us -> 118 us
  other arithmetic: 76.2 us -> 14.6 us
  matrix products: 40.2 us -> 0 us
  starting transfers between devices: 1.37 us -> 30.1 us
  between operations: 15.3 us -> 0.92 us
  loops' own time: 10.4 us -> 0 us
    unnamed x4 -> x0, waiting for transfers between devices: 349 us -> none
    ppermute x1 -> x21, waiting for transfers between devices: 252 us -> 76.1 us  [the longest x20 43.5 us: halved(): lax.ppermute(send, 'dp', [(i, i ^ 1 << stage) for i in range(replicas)])]
    pallas_call x0 -> x7, Pallas kernels: none -> 118 us  [the longest x1 36.2 us: on_device(): call(backward_data, 'backward_data', (3, steps), [tok, sca, pl.BlockSpec(...]
    gather x4 -> x0, local copies, waits for them, and re-layouts: 118 us -> none  [the longest x1 29.4 us: section_backward(): second_p = jnp.take(second, perm, axis=1)]
    dot_general x11 -> x0, matrix products: 40.2 us -> none  [the longest x4 14.7 us: block_mul_t(): jnp.einsum('rkj,kij->rki', split, factor, preferred_element_type=jnp.floa...]
    scatter x1 -> x0, local copies, waits for them, and re-layouts: 30.5 us -> none  [on_device(): jnp.zeros((width,), jnp.int32).at[perm]]
    ppermute x1 -> x21, starting transfers between devices: 1.29 us -> 30.1 us  [the longest x20 28.7 us: halved(): lax.ppermute(send, 'dp', [(i, i ^ 1 << stage) for i in range(replicas)])]
    another operation x6 -> x1, local copies, waits for them, and re-layouts: 24.4 us -> 0.13 us  [on_device(): return (out_grad[None], jnp.stack(total)[None], gamma_total)]
  transfers between devices with their start and end apart: 3 -> 21, of which waited for: 3 -> 13; matrix products, arithmetic and copies ran while one was open for 3% -> 5% of each run, Pallas kernels for 0% -> 11%
where the time goes in v1:
time: 252 us; the launch traced here: 251 us
  Pallas kernels  118 us (47%)
  waiting for transfers between devices  76.1 us (30%)
  starting transfers between devices  30.1 us (12%)
  other arithmetic  14.6 us (6%)
  local copies, waits for them, and re-layouts  10.9 us (4%)
    ppermute x20, waiting for transfers between devices, halved(): lax.ppermute(send, 'dp', [(i, i ^ 1 << stage) for i in range(replicas)])  43.5 us
    pallas_call x1, Pallas kernels, on_device(): call(backward_data, 'backward_data', (3, steps), [tok, sca, pl.BlockSpec(...  36.2 us
    ppermute x1, waiting for transfers between devices, on_device(): lax.ppermute(grad_x, 'section', [(i, i - 1) for i in range(1, sections)])  32.6 us
    ppermute x20, starting transfers between devices, halved(): lax.ppermute(send, 'dp', [(i, i ^ 1 << stage) for i in range(replicas)])  28.7 us
    pallas_call x1, Pallas kernels, on_device(): call(forward_first, 'forward_first', (2, steps), [tok, gam, pl.BlockSpec(...  18.6 us
    pallas_call x1, Pallas kernels, on_device(): call(functools.partial(backward_two_one, own), 'backward_two_one', (steps...  15.3 us
    pallas_call x1, Pallas kernels, on_device(): call(functools.partial(backward_three, own), 'backward_three', (steps,),...  15.3 us
    pallas_call x1, Pallas kernels, on_device(): call(forward_second, 'forward_second', (2, steps), [pl.BlockSpec(chunk, l...  14.6 us
  transfers between devices with their start and end apart: 21, of which 13 were waited for; matrix products, arithmetic and copies ran while one was open for 5% of the time, Pallas kernels for 11%

profile of v1, /device:TPU:0, one launch (start us, length us, event | category | flops | bytes accessed | tf_op | source)
XLA Modules:
  0.0 250.7 jit_solution(14578891639795168198)
XLA Ops:
  4.4 18.6 %forward_first.1 = (bf16[8192,128]{1,0:T(8,128)(2,1)S(1)}, bf16[8192,128]{1,0:T(8,128)(2,1)S(1)}, f32[8192,128]{1,0:T(8,128)}, f32[128,128]{1,0:T(8,128)S(1)}) custom-call(s32[8192]{0:T(1024)S(1)} %bitcast.134, bf16[128,8192]{1,0:T(8,128)(2,1)S(1)} %bitcast.126, f32[1,8192]{1,0:T(1,128)S(1)} %copy-done.15, bf16[4,64,128,128]{3,2,1,0:T(8,128)(2,1)} %bitcast.139), custom_call_target="tpu_custom_call" | custom-call | tf_op jit(solution)/shard_map/forward_first/pallas_call | solution.py:295
  24.4 36.2 %backward_data.1 = bf16[128,8192]{1,0:T(8,128)(2,1)} custom-call(s32[8192]{0:T(1024)S(1)} %bitcast.135, bf16[128,8192]{1,0:T(8,128)(2,1)S(1)} %copy-done.2, f32[128,128]{1,0:T(8,128)S(1)} %broadcast_in_dim.12.live, f32[8192,128]{1,0:T(8,128)} %get-tuple-element.19.slope_t, bf16[4,64,128,128]{3,2,1,0:T(8,128)(2,1)} %bitcast.140, ...), custom_call_target="tpu_custom_call" | custom-call | tf_op jit(solution)/shard_map/backward_data/pallas_call | solution.py:307
  62.1 14.6 %forward_second.1.cp_t = bf16[8192,128]{1,0:T(8,128)(2,1)S(1)} custom-call(s32[8192]{0:T(1024)S(1)} %bitcast.136, bf16[8192,128]{1,0:T(8,128)(2,1)S(1)} %get-tuple-element.21.h_t, bf16[4,64,128,128]{3,2,1,0:T(8,128)(2,1)} %bitcast.142), custom_call_target="tpu_custom_call" | custom-call | tf_op jit(solution)/shard_map/forward_second/pallas_call | solution.py:327
  78.2 32.6 %collective-permute-done.moved = bf16[128,8192]{1,0:T(8,128)(2,1)} collective-permute-done((bf16[128,8192]{1,0:T(8,128)(2,1)}, bf16[128,8192]{1,0:T(8,128)(2,1)}, u32[]{:S(2)}, u32[]{:S(2)}) %collective-permute-start) | collective-permute-done | bytes 2097184 | tf_op jit(solution)/shard_map/ppermute | solution.py:325
  110.8 15.3 %backward_three.1 = (bf16[32,128,128]{2,1,0:T(8,128)(2,1)S(1)}, bf16[32,128,128]{2,1,0:T(8,128)(2,1)}, bf16[8192,128]{1,0:T(8,128)(2,1)S(1)}) custom-call(s32[8192]{0:T(1024)S(1)} %bitcast.137, s32[2]{0:T(128)S(1)} %pad_add_fusion.flags, bf16[128,8192]{1,0:T(8,128)(2,1)S(1)} %copy-done.2, f32[128,128]{1,0:T(8,128)S(1)} %broadcast_in_dim.12.live, ...), custom_call_target="tpu_custom_call" | custom-call | tf_op jit(solution)/shard_map/backward_three/pallas_call | solution.py:340
  126.1 15.3 %backward_two_one.1 = (bf16[32,128,128]{2,1,0:T(8,128)(2,1)S(1)}, bf16[32,128,128]{2,1,0:T(8,128)(2,1)}, bf16[32,128,128]{2,1,0:T(8,128)(2,1)S(1)}, bf16[32,128,128]{2,1,0:T(8,128)(2,1)}, bf16[8192,128]{1,0:T(8,128)(2,1)S(1)}) custom-call(s32[8192]{0:T(1024)S(1)} %bitcast.138, s32[2]{0:T(128)S(1)} %pad_add_fusion.flags, ...), custom_call_target="tpu_custom_call" | custom-call | tf_op jit(solution)/shard_map/backward_two_one/pallas_call | solution.py:350
  141.4 5.0 %backward_zero.1 = (bf16[32,128,128]{2,1,0:T(8,128)(2,1)S(1)}, bf16[32,128,128]{2,1,0:T(8,128)(2,1)}) custom-call(s32[2]{0:T(128)S(1)} %pad_add_fusion.flags, bf16[8192,128]{1,0:T(8,128)(2,1)S(1)} %get-tuple-element.24.ga_t, bf16[128,8192]{1,0:T(8,128)(2,1)S(1)} %bitcast.128, f32[128,128]{1,0:T(8,128)S(1)} %get-tuple-element.20.scale, f32[1,8192]{1,0:T(1,128)S(1)} %copy-done.16), custom_call_target="tpu_custom_call" | custom-call | tf_op jit(solution)/shard_map/backward_zero/pallas_call | solution.py:360
  151.6 13.1 %backward_last.1 = (bf16[128,8192]{1,0:T(8,128)(2,1)}, f32[1,8192]{1,0:T(1,128)S(1)}) custom-call(s32[2]{0:T(128)S(1)} %pad_add_fusion.flags, bf16[8192,128]{1,0:T(8,128)(2,1)S(1)} %copy-done.5, bf16[128,8192]{1,0:T(8,128)(2,1)S(1)} %copy-done.3, f32[128,128]{1,0:T(8,128)S(1)} %broadcast_in_dim.12.live, bf16[128,8192]{1,0:T(8,128)(2,1)} %collective-permute-done.moved, ...), custom_call_target="tpu_custom_call" | custom-call | tf_op jit(solution)/shard_map/backward_last/pallas_call | solution.py:368
  167.4 2.4 collective-permute-start.18
  171.4 4.1 %add_convert_fusion.5 = (bf16[4,1,4,128,128]{4,3,2,1,0:T(8,128)(2,1)S(1)}, bf16[4,1,4,128,128]{4,3,2,1,0:T(8,128)(2,1)}, bf16[4,1,4,128,128]{4,3,2,1,0:T(8,128)(2,1)}, bf16[4,1,4,128,128]{4,3,2,1,0:T(8,128)(2,1)S(1)}) fusion(bf16[4,2,4,128,128]{4,3,2,1,0:T(8,128)(2,1)} %bitcast.18, s32[]{:T(128)S(6)} %select_n.85, bf16[4,2,4,128,128]{4,3,2,1,0:T(8,128)(2,1)} %bitcast.132, ...), kind=kLoop, calls=%fused_computation.6 | loop fusion | flops 4194304 | bytes 6291464 | tf_op jit(solution)/shard_map/convert_element_type | solution.py:255
  179.8 3.3 %add_convert_fusion.1 = (bf16[4,1,4,128,128]{4,3,2,1,0:T(8,128)(2,1)S(1)}, bf16[4,1,4,128,128]{4,3,2,1,0:T(8,128)(2,1)}, bf16[4,1,4,128,128]{4,3,2,1,0:T(8,128)(2,1)}, bf16[4,1,4,128,128]{4,3,2,1,0:T(8,128)(2,1)S(1)}) fusion(bf16[4,2,4,128,128]{4,3,2,1,0:T(8,128)(2,1)} %bitcast.38, s32[]{:T(128)S(6)} %select_n.85, ...), kind=kLoop, calls=%fused_computation.2 | loop fusion | flops 4194304 | bytes 6291464 | tf_op jit(solution)/shard_map/convert_element_type | solution.py:255
  184.6 2.7 %collective-permute-start.20 = (f32[1,512]{1,0:T(1,128)S(1)}, f32[1,512]{1,0:T(1,128)S(1)}, u32[]{:S(2)}, u32[]{:S(2)}) collective-permute-start(f32[1,512]{1,0:T(1,128)S(1)} %fusion.29), channel_id=1, source_target_pairs={{0,8},{1,9},{2,10},{3,11},{4,12},{5,13},{6,14},{7,15},{8,0},{9,1},... | collective-permute-start | bytes 6152 | tf_op jit(solution)/shard_map/ppermute | solution.py:246
  191.9 2.2 collective-permute-start.3
  194.1 7.9 %collective-permute-done.6 = bf16[16,128,128]{2,1,0:T(8,128)(2,1)} collective-permute-done((bf16[16,128,128]{2,1,0:T(8,128)(2,1)}, bf16[16,128,128]{2,1,0:T(8,128)(2,1)}, u32[]{:S(2)}, u32[]{:S(2)}) %collective-permute-start.6) | collective-permute-done | bytes 524320 | tf_op jit(solution)/shard_map/ppermute | solution.py:246
  203.2 2.2 collective-permute-start.7
  205.4 7.9 %collective-permute-done.10 = bf16[16,128,128]{2,1,0:T(8,128)(2,1)} collective-permute-done((bf16[16,128,128]{2,1,0:T(8,128)(2,1)}, bf16[16,128,128]{2,1,0:T(8,128)(2,1)}, u32[]{:S(2)}, u32[]{:S(2)}) %collective-permute-start.10) | collective-permute-done | bytes 524320 | tf_op jit(solution)/shard_map/ppermute | solution.py:246
  216.6 6.0 %collective-permute-done.14 = bf16[16,128,128]{2,1,0:T(8,128)(2,1)S(1)} collective-permute-done((bf16[16,128,128]{2,1,0:T(8,128)(2,1)}, bf16[16,128,128]{2,1,0:T(8,128)(2,1)S(1)}, u32[]{:S(2)}, u32[]{:S(2)}) %collective-permute-start.14) | collective-permute-done | bytes 524320 | tf_op jit(solution)/shard_map/ppermute | solution.py:246
  224.7 2.6 %collective-permute-start.4 = (bf16[4,128,128]{2,1,0:T(8,128)(2,1)S(1)}, bf16[4,128,128]{2,1,0:T(8,128)(2,1)S(1)}, u32[]{:S(2)}, u32[]{:S(2)}) collective-permute-start(bf16[4,128,128]{2,1,0:T(8,128)(2,1)S(1)} %fusion.9), channel_id=1, source_target_pairs={{0,8},{1,9},{2,10},{3,11},{4,12},{5,13},{6,14},{7,15},{8,0},{9,1},... | collective-permute-start | bytes 393224 | tf_op jit(solution)/shard_map/ppermute | solution.py:246
  227.9 2.6 %collective-permute-start.12 = (bf16[4,128,128]{2,1,0:T(8,128)(2,1)S(1)}, bf16[4,128,128]{2,1,0:T(8,128)(2,1)S(1)}, u32[]{:S(2)}, u32[]{:S(2)}) collective-permute-start(bf16[4,128,128]{2,1,0:T(8,128)(2,1)S(1)} %fusion.13), channel_id=1, source_target_pairs={{0,8},{1,9},{2,10},{3,11},{4,12},{5,13},{6,14},{7,15},{8,0},{9,1},... | collective-permute-start | bytes 393224 | tf_op jit(solution)/shard_map/ppermute | solution.py:246
  230.5 2.6 %collective-permute-done.15 = bf16[8,128,128]{2,1,0:T(8,128)(2,1)S(1)} collective-permute-done((bf16[8,128,128]{2,1,0:T(8,128)(2,1)S(1)}, bf16[8,128,128]{2,1,0:T(8,128)(2,1)S(1)}, u32[]{:S(2)}, u32[]{:S(2)}) %collective-permute-start.15) | collective-permute-done | bytes 262176 | tf_op jit(solution)/shard_map/ppermute | solution.py:246
  233.2 2.2 collective-permute-start.16
  235.4 7.5 %collective-permute-done.4 = bf16[4,128,128]{2,1,0:T(8,128)(2,1)S(1)} collective-permute-done((bf16[4,128,128]{2,1,0:T(8,128)(2,1)S(1)}, bf16[4,128,128]{2,1,0:T(8,128)(2,1)S(1)}, u32[]{:S(2)}, u32[]{:S(2)}) %collective-permute-start.4) | collective-permute-done | bytes 131104 | tf_op jit(solution)/shard_map/ppermute | solution.py:246
  243.1 2.6 %collective-permute-done.8 = bf16[4,128,128]{2,1,0:T(8,128)(2,1)S(1)} collective-permute-done((bf16[4,128,128]{2,1,0:T(8,128)(2,1)S(1)}, bf16[4,128,128]{2,1,0:T(8,128)(2,1)S(1)}, u32[]{:S(2)}, u32[]{:S(2)}) %collective-permute-start.8) | collective-permute-done | bytes 131104 | tf_op jit(solution)/shard_map/ppermute | solution.py:246
  245.7 2.4 collective-permute-done.12
  (92 shorter events, 37.8 us)
Async XLA Ops:
  4.4 20.0 %copy-start.2 = (bf16[128,8192]{1,0:T(8,128)(2,1)S(1)}, bf16[128,8192]{1,0:T(8,128)(2,1)}, u32[]{:S(2)}) copy-start(bf16[128,8192]{1,0:T(8,128)(2,1)} %cot.5) | copy-start | bytes 6291460
  24.3 37.7 %copy-start.6 = (bf16[8192,128]{1,0:T(8,128)(2,1)}, bf16[8192,128]{1,0:T(8,128)(2,1)S(1)}, u32[]{:S(2)}) copy-start(bf16[8192,128]{1,0:T(8,128)(2,1)S(1)} %get-tuple-element.21.h_t) | copy-start | bytes 6291460
  60.6 50.2 %collective-permute-start = (bf16[128,8192]{1,0:T(8,128)(2,1)}, bf16[128,8192]{1,0:T(8,128)(2,1)}, u32[]{:S(2)}, u32[]{:S(2)}) collective-permute-start(bf16[128,8192]{1,0:T(8,128)(2,1)} %backward_data.1), channel_id=1, source_target_pairs={{16,0},{17,1},{18,2},{19,3},{20,4},{21,5},{22,6},{23,7},{24,8},{25... | collective-permute-start | bytes 6291464 | tf_op jit(solution)/shard_map/ppermute | solution.py:325
  62.1 48.7 %copy-start.14 = (s32[1,8192]{1,0:T(1,128)S(1)}, s32[1,8192]{1,0:T(1,128)}, u32[]{:S(2)}) copy-start(s32[1,8192]{1,0:T(1,128)} %param.11) | copy-start | bytes 98308
  147.4 24.0 %collective-permute-start.1 = (bf16[32,128,128]{2,1,0:T(8,128)(2,1)}, bf16[32,128,128]{2,1,0:T(8,128)(2,1)}, u32[]{:S(2)}, u32[]{:S(2)}) collective-permute-start(bf16[32,128,128]{2,1,0:T(8,128)(2,1)} %get-tuple-element.27), channel_id=1, source_target_pairs={{0,1},{1,0},{2,3},{3,2},{4,5},{5,4},{6,7},{7,6},{8,9},{9,8},{10,11... | collective-permute-start | bytes 3145736 | tf_op jit(solution)/shard_map/ppermute | solution.py:246
  147.4 24.0 %collective-permute-start.5 = (bf16[32,128,128]{2,1,0:T(8,128)(2,1)}, bf16[32,128,128]{2,1,0:T(8,128)(2,1)}, u32[]{:S(2)}, u32[]{:S(2)}) collective-permute-start(bf16[32,128,128]{2,1,0:T(8,128)(2,1)} %get-tuple-element.29), channel_id=1, source_target_pairs={{0,1},{1,0},{2,3},{3,2},{4,5},{5,4},{6,7},{7,6},{8,9},{9,8},{10,11... | collective-permute-start | bytes 3145736 | tf_op jit(solution)/shard_map/ppermute | solution.py:246
  147.9 31.9 %collective-permute-start.9 = (bf16[32,128,128]{2,1,0:T(8,128)(2,1)}, bf16[32,128,128]{2,1,0:T(8,128)(2,1)}, u32[]{:S(2)}, u32[]{:S(2)}) collective-permute-start(bf16[32,128,128]{2,1,0:T(8,128)(2,1)} %get-tuple-element.31), channel_id=1, source_target_pairs={{0,1},{1,0},{2,3},{3,2},{4,5},{5,4},{6,7},{7,6},{8,9},{9,8},{10,11... | collective-permute-start | bytes 3145736 | tf_op jit(solution)/shard_map/ppermute | solution.py:246
  147.9 31.9 %collective-permute-start.13 = (bf16[32,128,128]{2,1,0:T(8,128)(2,1)}, bf16[32,128,128]{2,1,0:T(8,128)(2,1)}, u32[]{:S(2)}, u32[]{:S(2)}) collective-permute-start(bf16[32,128,128]{2,1,0:T(8,128)(2,1)} %get-tuple-element.33), channel_id=1, source_target_pairs={{0,1},{1,0},{2,3},{3,2},{4,5},{5,4},{6,7},{7,6},{8,9},{9,8},{10,11... | collective-permute-start | bytes 3145736 | tf_op jit(solution)/shard_map/ppermute | solution.py:246
  166.1 1.2 collective-permute-start.17
  167.4 4.0 %collective-permute-start.18 = (f32[4,512]{1,0:T(4,128)S(1)}, f32[4,512]{1,0:T(4,128)S(1)}, u32[]{:S(2)}, u32[]{:S(2)}) collective-permute-start(f32[4,512]{1,0:T(4,128)S(1)} %bitcast.167), channel_id=1, source_target_pairs={{0,2},{1,3},{2,0},{3,1},{4,6},{5,7},{6,4},{7,5},{8,10},{9,11},{10,... | collective-permute-start | bytes 24584 | tf_op jit(solution)/shard_map/ppermute | solution.py:246
  175.6 15.2 %collective-permute-start.2 = (bf16[16,128,128]{2,1,0:T(8,128)(2,1)}, bf16[16,128,128]{2,1,0:T(8,128)(2,1)}, u32[]{:S(2)}, u32[]{:S(2)}) collective-permute-start(bf16[16,128,128]{2,1,0:T(8,128)(2,1)} %bitcast.9), channel_id=1, source_target_pairs={{0,2},{1,3},{2,0},{3,1},{4,6},{5,7},{6,4},{7,5},{8,10},{9,11},{10,... | collective-permute-start | bytes 1572872 | tf_op jit(solution)/shard_map/ppermute | solution.py:246
  177.6 7.0 %collective-permute-start.19 = (f32[2,512]{1,0:T(2,128)S(1)}, f32[2,512]{1,0:T(2,128)S(1)}, u32[]{:S(2)}, u32[]{:S(2)}) collective-permute-start(f32[2,512]{1,0:T(2,128)S(1)} %bitcast.168), channel_id=1, source_target_pairs={{0,4},{1,5},{2,6},{3,7},{4,0},{5,1},{6,2},{7,3},{8,12},{9,13},{10,... | collective-permute-start | bytes 12296 | tf_op jit(solution)/shard_map/ppermute | solution.py:246
  179.3 22.7 %collective-permute-start.6 = (bf16[16,128,128]{2,1,0:T(8,128)(2,1)}, bf16[16,128,128]{2,1,0:T(8,128)(2,1)}, u32[]{:S(2)}, u32[]{:S(2)}) collective-permute-start(bf16[16,128,128]{2,1,0:T(8,128)(2,1)} %bitcast.20), channel_id=1, source_target_pairs={{0,2},{1,3},{2,0},{3,1},{4,6},{5,7},{6,4},{7,5},{8,10},{9,11},{10,... | collective-permute-start | bytes 1572872 | tf_op jit(solution)/shard_map/ppermute | solution.py:246
  183.1 30.1 %collective-permute-start.10 = (bf16[16,128,128]{2,1,0:T(8,128)(2,1)}, bf16[16,128,128]{2,1,0:T(8,128)(2,1)}, u32[]{:S(2)}, u32[]{:S(2)}) collective-permute-start(bf16[16,128,128]{2,1,0:T(8,128)(2,1)} %bitcast.30), channel_id=1, source_target_pairs={{0,2},{1,3},{2,0},{3,1},{4,6},{5,7},{6,4},{7,5},{8,10},{9,11},{10,... | collective-permute-start | bytes 1572872 | tf_op jit(solution)/shard_map/ppermute | solution.py:246
  184.6 4.5 %collective-permute-start.20 = (f32[1,512]{1,0:T(1,128)S(1)}, f32[1,512]{1,0:T(1,128)S(1)}, u32[]{:S(2)}, u32[]{:S(2)}) collective-permute-start(f32[1,512]{1,0:T(1,128)S(1)} %fusion.29), channel_id=1, source_target_pairs={{0,8},{1,9},{2,10},{3,11},{4,12},{5,13},{6,14},{7,15},{8,0},{9,1},... | collective-permute-start | bytes 6152 | tf_op jit(solution)/shard_map/ppermute | solution.py:246
  187.3 35.3 %collective-permute-start.14 = (bf16[16,128,128]{2,1,0:T(8,128)(2,1)}, bf16[16,128,128]{2,1,0:T(8,128)(2,1)S(1)}, u32[]{:S(2)}, u32[]{:S(2)}) collective-permute-start(bf16[16,128,128]{2,1,0:T(8,128)(2,1)} %bitcast.152), channel_id=1, source_target_pairs={{0,2},{1,3},{2,0},{3,1},{4,6},{5,7},{6,4},{7,5},{8,10},{9,11},{10,... | collective-permute-start | bytes 1572872 | tf_op jit(solution)/shard_map/ppermute | solution.py:246
  191.9 32.7 %collective-permute-start.3 = (bf16[8,128,128]{2,1,0:T(8,128)(2,1)S(1)}, bf16[8,128,128]{2,1,0:T(8,128)(2,1)S(1)}, u32[]{:S(2)}, u32[]{:S(2)}) collective-permute-start(bf16[8,128,128]{2,1,0:T(8,128)(2,1)S(1)} %bitcast.161), channel_id=1, source_target_pairs={{0,4},{1,5},{2,6},{3,7},{4,0},{5,1},{6,2},{7,3},{8,12},{9,13},{10,... | collective-permute-start | bytes 786440 | tf_op jit(solution)/shard_map/ppermute | solution.py:246
  203.2 24.2 %collective-permute-start.7 = (bf16[8,128,128]{2,1,0:T(8,128)(2,1)S(1)}, bf16[8,128,128]{2,1,0:T(8,128)(2,1)S(1)}, u32[]{:S(2)}, u32[]{:S(2)}) collective-permute-start(bf16[8,128,128]{2,1,0:T(8,128)(2,1)S(1)} %bitcast.162), channel_id=1, source_target_pairs={{0,4},{1,5},{2,6},{3,7},{4,0},{5,1},{6,2},{7,3},{8,12},{9,13},{10,... | collective-permute-start | bytes 786440 | tf_op jit(solution)/shard_map/ppermute | solution.py:246
  214.4 13.4 %collective-permute-start.11 = (bf16[8,128,128]{2,1,0:T(8,128)(2,1)S(1)}, bf16[8,128,128]{2,1,0:T(8,128)(2,1)S(1)}, u32[]{:S(2)}, u32[]{:S(2)}) collective-permute-start(bf16[8,128,128]{2,1,0:T(8,128)(2,1)S(1)} %bitcast.163), channel_id=1, source_target_pairs={{0,4},{1,5},{2,6},{3,7},{4,0},{5,1},{6,2},{7,3},{8,12},{9,13},{10,... | collective-permute-start | bytes 786440 | tf_op jit(solution)/shard_map/ppermute | solution.py:246
  222.8 10.4 %collective-permute-start.15 = (bf16[8,128,128]{2,1,0:T(8,128)(2,1)S(1)}, bf16[8,128,128]{2,1,0:T(8,128)(2,1)S(1)}, u32[]{:S(2)}, u32[]{:S(2)}) collective-permute-start(bf16[8,128,128]{2,1,0:T(8,128)(2,1)S(1)} %bitcast.164), channel_id=1, source_target_pairs={{0,4},{1,5},{2,6},{3,7},{4,0},{5,1},{6,2},{7,3},{8,12},{9,13},{10,... | collective-permute-start | bytes 786440 | tf_op jit(solution)/shard_map/ppermute | solution.py:246
  224.7 18.1 %collective-permute-start.4 = (bf16[4,128,128]{2,1,0:T(8,128)(2,1)S(1)}, bf16[4,128,128]{2,1,0:T(8,128)(2,1)S(1)}, u32[]{:S(2)}, u32[]{:S(2)}) collective-permute-start(bf16[4,128,128]{2,1,0:T(8,128)(2,1)S(1)} %fusion.9), channel_id=1, source_target_pairs={{0,8},{1,9},{2,10},{3,11},{4,12},{5,13},{6,14},{7,15},{8,0},{9,1},... | collective-permute-start | bytes 393224 | tf_op jit(solution)/shard_map/ppermute | solution.py:246
  227.4 18.3 %collective-permute-start.8 = (bf16[4,128,128]{2,1,0:T(8,128)(2,1)S(1)}, bf16[4,128,128]{2,1,0:T(8,128)(2,1)S(1)}, u32[]{:S(2)}, u32[]{:S(2)}) collective-permute-start(bf16[4,128,128]{2,1,0:T(8,128)(2,1)S(1)} %fusion.11), channel_id=1, source_target_pairs={{0,8},{1,9},{2,10},{3,11},{4,12},{5,13},{6,14},{7,15},{8,0},{9,1},... | collective-permute-start | bytes 393224 | tf_op jit(solution)/shard_map/ppermute | solution.py:246
  227.9 20.3 %collective-permute-start.12 = (bf16[4,128,128]{2,1,0:T(8,128)(2,1)S(1)}, bf16[4,128,128]{2,1,0:T(8,128)(2,1)S(1)}, u32[]{:S(2)}, u32[]{:S(2)}) collective-permute-start(bf16[4,128,128]{2,1,0:T(8,128)(2,1)S(1)} %fusion.13), channel_id=1, source_target_pairs={{0,8},{1,9},{2,10},{3,11},{4,12},{5,13},{6,14},{7,15},{8,0},{9,1},... | collective-permute-start | bytes 393224 | tf_op jit(solution)/shard_map/ppermute | solution.py:246
  233.2 16.4 %collective-permute-start.16 = (bf16[4,128,128]{2,1,0:T(8,128)(2,1)S(1)}, bf16[4,128,128]{2,1,0:T(8,128)(2,1)S(1)}, u32[]{:S(2)}, u32[]{:S(2)}) collective-permute-start(bf16[4,128,128]{2,1,0:T(8,128)(2,1)S(1)} %fusion.15), channel_id=1, source_target_pairs={{0,8},{1,9},{2,10},{3,11},{4,12},{5,13},{6,14},{7,15},{8,0},{9,1},... | collective-permute-start | bytes 393224 | tf_op jit(solution)/shard_map/ppermute | solution.py:246
  (14 other events, 64.2 us)

commit v2 on v1

v2 whole, which is shorter than its diff:
```python
import functools

import jax
import jax.numpy as jnp
from jax import lax
from jax.experimental import pallas as pl
from jax.experimental.pallas import tpu as pltpu
from jax.sharding import PartitionSpec as P

F32 = jnp.float32
BF16 = jnp.bfloat16
inv_sqrt_two = 0.7071067811865476
inv_sqrt_two_pi = 0.3989422804014327
STEP = 16
UNROLL = 8
EXTRA = 16
VMEM_BYTES = 56 << 20


def dot(a, b, ca, cb):
    return lax.dot_general(a, b, (((ca,), (cb,)), ((), ())), preferred_element_type=F32)


def whole(*shape):
    return pl.BlockSpec(shape, lambda *_: (0,) * len(shape))


def call(body, name, grid, in_specs, out_specs, out_shape, scratch=(), prefetch=1):
    return pl.pallas_call(
        body,
        name=name,
        out_shape=out_shape,
        grid_spec=pltpu.PrefetchScalarGridSpec(
            num_scalar_prefetch=prefetch,
            grid=grid,
            in_specs=in_specs,
            out_specs=out_specs,
            scratch_shapes=scratch,
        ),
        compiler_params=pltpu.CompilerParams(vmem_limit_bytes=VMEM_BYTES),
    )


def each_block(body, count=STEP, unroll=UNROLL):
    def some(i, carry):
        for u in range(unroll):
            body(i * unroll + u, u)
        return carry

    lax.fori_loop(0, count // unroll, some, 0)


def at_block(k, bs):
    return pl.ds(pl.multiple_of(k * bs, bs), bs)


def rounded(v):
    return v.astype(BF16).astype(F32)


def zed_block(x, scale, cols):
    return x[:, cols].astype(F32) * scale[...]


def gather_rows(perm, base, source, target, count):
    for i in range(count):
        target[pl.ds(i, 1), :] = source[pl.ds(perm[base + i], 1), :]


def scatter_rows(perm, base, source, target, count):
    for i in range(count):
        target[pl.ds(perm[base + i], 1), :] = source[pl.ds(i, 1), :]


def seeded_block(cot, live, cols):
    return (cot[:, cols].astype(F32) * live[...]).astype(BF16)


def gradient(gy, gn, gamma, z, scale, inner):
    return (gy.astype(F32) + scale[...] * (gn * gamma - z * inner[...])).astype(BF16)


def first_pass(perm, x, cot, live, gamma, fac_a, fac_b, ap_t, h_t, slope_t, scale, grad_x, a_t, gc_t, ga_t, gn, acc, rows, rows_b):
    phase, c = pl.program_id(0), pl.program_id(1)
    bs = fac_a.shape[2]
    blocks = x.shape[1] // bs

    @pl.when(jnp.logical_and(phase == 0, c == 0))
    def _():
        def add(k, total):
            xk = x[:, at_block(k, bs)].astype(F32)
            return total + xk * xk

        total = lax.fori_loop(0, blocks, add, jnp.zeros((x.shape[0], bs), F32), unroll=8)
        mean = jnp.sum(total, axis=1, keepdims=True) / x.shape[1]
        scale[...] = jnp.broadcast_to(lax.rsqrt(mean + 1e-06), scale.shape)
        acc[...] = jnp.zeros(acc.shape, F32)

    @pl.when(phase == 0)
    def _():
        def one(k, u):
            block = c * STEP + k
            cols = at_block(block, bs)
            n = (zed_block(x, scale, cols) * gamma[:, cols]).astype(BF16)
            a_t[cols, :] = rounded(dot(fac_a[0, k], n, 0, 1))
            rows[u] = rounded(dot(fac_b[0, k], seeded_block(cot, live, at_block(k, bs)), 1, 1))
            scatter_rows(perm, block * bs, rows.at[u], gc_t, bs)

        each_block(one)

    @pl.when(phase == 1)
    def _():
        def one(k, u):
            block = c * STEP + k
            here = at_block(k, bs)
            gather_rows(perm, block * bs, a_t, rows.at[u], bs)
            ap = rows[u].astype(BF16)
            ap_t[here, :] = ap
            pre = dot(fac_a[0, k], ap, 0, 0)
            cdf = 0.5 * (1.0 + lax.erf(pre * inv_sqrt_two))
            h_t[here, :] = (pre * cdf).astype(BF16)
            slope = cdf + pre * jnp.exp(-0.5 * pre * pre) * inv_sqrt_two_pi
            slope_t[here, :] = slope
            gh = dot(fac_b[0, k], gc_t[at_block(block, bs), :].astype(BF16), 1, 0)
            rows_b[u] = rounded(dot(fac_a[0, k], (gh * slope).astype(BF16), 1, 0))
            scatter_rows(perm, block * bs, rows_b.at[u], ga_t, bs)

        each_block(one)

    @pl.when(phase == 2)
    def _():
        def one(k, u):
            cols = at_block(c * STEP + k, bs)
            value = dot(ga_t[cols, :].astype(BF16), fac_a[0, k], 0, 1)
            gn[:, cols] = value
            acc[...] += value * gamma[:, cols] * zed_block(x, scale, cols)

        each_block(one)

    @pl.when(jnp.logical_and(phase == 2, c == pl.num_programs(1) - 1))
    def _():
        mean = jnp.sum(acc[...], axis=1, keepdims=True) / x.shape[1]
        acc[...] = jnp.broadcast_to(mean, acc.shape)

    @pl.when(phase == 3)
    def _():
        def one(k, u):
            here = at_block(k, bs)
            cols = at_block(c * STEP + k, bs)
            z = zed_block(x, scale, cols)
            grad_x[:, here] = gradient(seeded_block(cot, live, here), gn[:, cols], gamma[:, cols], z, scale, acc)

        each_block(one, unroll=4)


def forward_second(perm, h_t, fac, cp_t, c_t, rows):
    phase, c = pl.program_id(0), pl.program_id(1)
    bs = fac.shape[2]

    @pl.when(phase == 0)
    def _():
        each_block(
            lambda k, u: c_t.__setitem__(
                (at_block(c * STEP + k, bs), slice(None)), rounded(dot(fac[0, k], h_t[at_block(k, bs), :], 0, 0))
            )
        )

    @pl.when(phase == 1)
    def _():
        def one(k, u):
            gather_rows(perm, (c * STEP + k) * bs, c_t, rows.at[u], bs)
            cp_t[at_block(k, bs), :] = rows[u].astype(BF16)

        each_block(one)


def each_split(flags, own, body):
    for k in range(STEP // 2):
        group, within = divmod(k, own)
        base = group * 2 * own + within
        body(0, k, base + flags[0] * own)
        body(1, k, base + (1 - flags[0]) * own)


def chosen_gy(flags, cot, live, moved, cols):
    return jnp.where(flags[1] == 1, seeded_block(cot, live, cols), moved[:, cols])


def grad_three(own, flags, cot, live, moved, cp_t, keep, send):
    bs = live.shape[1]
    outs = (keep, send)

    def one(goes, k, block):
        at = at_block(block, bs)
        outs[goes][k] = dot(cp_t[at, :], chosen_gy(flags, cot, live, moved, at), 1, 0).astype(BF16)

    each_split(flags, own, one)


def back_three(perm, flags, cot, live, moved, fac, gc_out, gc_t, rows):
    c = pl.program_id(0)
    bs = fac.shape[2]

    def one(k, u):
        rows[u] = rounded(dot(fac[0, k], chosen_gy(flags, cot, live, moved, at_block(k, bs)), 1, 1))
        scatter_rows(perm, (c * STEP + k) * bs, rows.at[u], gc_t, bs)

    each_block(one)

    @pl.when(c == pl.num_programs(0) - 1)
    def _():
        gc_out[...] = gc_t[...].astype(BF16)


def back_two_one(own, perm, flags, gc_t, h_t, ap_t, slope_t, fac_two, fac_one, keep, send, ga_out, ga_t, gpre, rows):
    c = pl.program_id(0)
    bs = fac_two.shape[2]
    outs = (keep, send)

    def one(k, u):
        here = at_block(k, bs)
        gh = dot(fac_two[0, k], gc_t[here, :], 1, 0)
        gpre[here, :] = (gh * slope_t[here, :]).astype(BF16)
        rows[u] = rounded(dot(fac_one[0, k], gpre[here, :], 1, 0))
        scatter_rows(perm, (c * STEP + k) * bs, rows.at[u], ga_t, bs)

    each_block(one)

    def grads(goes, k, block):
        at = at_block(block, bs)
        outs[goes][0, k] = dot(h_t[at, :], gc_t[at, :], 1, 1).astype(BF16)
        outs[goes][1, k] = dot(ap_t[at, :], gpre[at, :], 1, 1).astype(BF16)

    each_split(flags, own, grads)

    @pl.when(c == pl.num_programs(0) - 1)
    def _():
        ga_out[...] = ga_t[...].astype(BF16)


def back_zero(own, flags, ga_t, x, scale, gamma, fac, keep, send, gn, inner, acc):
    c = pl.program_id(0)
    bs = fac.shape[2]
    outs = (keep, send)

    @pl.when(c == 0)
    def _():
        acc[...] = jnp.zeros(acc.shape, F32)

    def one(goes, k, block):
        at = at_block(block, bs)
        z = zed_block(x, scale, at)
        zg = z * gamma[:, at]
        outs[goes][k, pl.ds(0, bs), :] = dot(ga_t[at, :], zg.astype(BF16), 1, 0).astype(BF16)
        value = dot(ga_t[at, :], fac[0, block], 0, 1)
        gn[:, at] = value
        total = jnp.sum(value * z, axis=0, keepdims=True)
        outs[goes][k, pl.ds(bs, EXTRA), :] = jnp.broadcast_to(total, (EXTRA, bs)).astype(BF16)
        acc[...] += value * zg

    each_split(flags, own, one)

    @pl.when(c == pl.num_programs(0) - 1)
    def _():
        mean = jnp.sum(acc[...], axis=1, keepdims=True) / (x.shape[1] * pl.num_programs(0))
        inner[...] = jnp.broadcast_to(mean, inner.shape)


def back_last(flags, gn, cot, live, moved, x, scale, gamma, inner, grad_x):
    bs = live.shape[1]

    def one(k, u):
        cols = at_block(k, bs)
        z = zed_block(x, scale, cols)
        gy = chosen_gy(flags, cot, live, moved, cols)
        grad_x[:, cols] = gradient(gy, gn[:, cols], gamma[:, cols], z, scale, inner)

    each_block(one, unroll=4)


class Halving:
    def __init__(self, keep, send, order, own, me, replicas):
        self.keep, self.send, self.order = keep, send, list(order)
        self.left = list(range(replicas.bit_length() - 1))[::-1]
        self.left.remove(self.order[0])
        self.own, self.me, self.replicas = own, me, replicas

    def go(self):
        bit = self.order.pop(0)
        self.came = lax.ppermute(self.send, "dp", [(i, i ^ (1 << bit)) for i in range(self.replicas)])
        return self

    def add(self):
        if not self.order:
            self.keep = self.keep.astype(F32) + self.came.astype(F32)
            return self
        bit = self.order[0]
        place = self.left.index(bit)
        shape = (2**place, 2, 2 ** (len(self.left) - 1 - place) * self.own) + self.keep.shape[1:]
        mine = (self.me >> bit) & 1
        keep, came = self.keep.reshape(shape), self.came.reshape(shape)

        def part(which):
            a = lax.dynamic_index_in_dim(keep, which, 1, keepdims=False)
            b = lax.dynamic_index_in_dim(came, which, 1, keepdims=False)
            total = (a.astype(F32) + b.astype(F32)).astype(self.keep.dtype)
            return total.reshape((shape[0] * shape[2],) + shape[3:])

        self.left.remove(bit)
        self.send, self.keep = part(1 - mine), part(mine)
        return self

    def finish(self):
        while self.order:
            self.go().add()
        return self.keep / self.replicas


def on_device(replicas, sections, activations, cotangent, token_ids, gains, factors, monarch_perm):
    x = activations[0]
    gamma = gains
    fac = factors[0]
    perm = monarch_perm[0]
    tokens, width = x.shape
    blocks, bs = fac.shape[1], fac.shape[2]
    own = blocks // replicas
    steps = blocks // STEP
    here = lax.axis_index("section")
    me = lax.axis_index("dp")
    live = jnp.broadcast_to((token_ids != 0).astype(F32)[:, None], (tokens, bs))
    flags = jnp.stack([me & 1, (here == sections - 1).astype(jnp.int32)])
    bits = list(range(replicas.bit_length() - 1))
    other = bits[:1] + bits[2:3] + bits[1:2] + bits[3:]

    tok = whole(tokens, width)
    sca = whole(tokens, bs)
    gam = whole(1, width)
    chunk = (STEP * bs, tokens)
    wide = (tokens, STEP * bs)
    fblock = (1, STEP, bs, bs)
    f_at = lambda which: pl.BlockSpec(fblock, lambda c, *_: (which, c, 0, 0))
    c_at = pl.BlockSpec(chunk, lambda c, *_: (c, 0))
    w_at = pl.BlockSpec(wide, lambda c, *_: (0, c))
    g_at = pl.BlockSpec((1, STEP * bs), lambda c, *_: (0, c))
    feat = lambda dt: jax.ShapeDtypeStruct((width, tokens), dt)
    row = lambda dt: jax.ShapeDtypeStruct((tokens, width), dt)
    small = jax.ShapeDtypeStruct((tokens, bs), F32)
    half = lambda n=0, lead=(): jax.ShapeDtypeStruct(lead + (blocks // 2, bs + n, bs), BF16)
    half_at = pl.BlockSpec((STEP // 2, bs, bs), lambda c, *_: (c, 0, 0))
    more_at = pl.BlockSpec((STEP // 2, bs + EXTRA, bs), lambda c, *_: (c, 0, 0))
    two_at = pl.BlockSpec((2, STEP // 2, bs, bs), lambda c, *_: (0, c, 0, 0))
    big = pltpu.VMEM((width, tokens), F32)
    rows = pltpu.VMEM((UNROLL, bs, tokens), F32)
    last = steps - 1

    def phased(*picks):
        def at(ph, c):
            out = c if picks[-1] is None else picks[-1]
            for i in range(len(picks) - 2, -1, -1):
                out = jnp.where(ph == i, c if picks[i] is None else picks[i], out)
            return out

        return at

    pick = lambda values: lambda ph: jnp.where(ph == 0, values[0], jnp.where(ph == 1, values[1], values[2]))
    a_which, a_at = pick((0, 1, 0)), phased(None, None, None, last)
    b_which, b_at = pick((3, 2, 2)), phased(None, None, last, last)
    cot_at, out_at, mid_at = phased(None, last, last, None), phased(0, 0, 0, None), phased(0, None, last, last)
    mid = pl.BlockSpec(chunk, lambda ph, c, *_: (mid_at(ph, c), 0))
    ap_t, h_t, slope_t, scale, grad_x = call(
        first_pass,
        "first_pass",
        (4, steps),
        [
            tok,
            pl.BlockSpec(wide, lambda ph, c, *_: (0, cot_at(ph, c))),
            sca,
            gam,
            pl.BlockSpec(fblock, lambda ph, c, *_: (a_which(ph), a_at(ph, c), 0, 0)),
            pl.BlockSpec(fblock, lambda ph, c, *_: (b_which(ph), b_at(ph, c), 0, 0)),
        ],
        [mid, mid, mid, sca, pl.BlockSpec(wide, lambda ph, c, *_: (0, out_at(ph, c)))],
        [feat(BF16), feat(BF16), feat(F32), small, row(BF16)],
        [big, big, big, pltpu.VMEM((tokens, width), F32), pltpu.VMEM((tokens, bs), F32), rows, rows],
    )(perm, x, cotangent, live, gamma, fac, fac)
    moved = lax.ppermute(grad_x, "section", [(i, i - 1) for i in range(1, sections)])

    early, rest = phased(None, last), phased(0, None)
    cp_t = call(
        forward_second,
        "forward_second",
        (2, steps),
        [
            pl.BlockSpec(chunk, lambda ph, c, *_: (early(ph, c), 0)),
            pl.BlockSpec(fblock, lambda ph, c, *_: (2, early(ph, c), 0, 0)),
        ],
        pl.BlockSpec(chunk, lambda ph, c, *_: (rest(ph, c), 0)),
        feat(BF16),
        [big, rows],
    )(perm, h_t, fac)

    start = lambda keep, send, order: Halving(keep, send, order, own, me, replicas)
    keep, send = call(
        functools.partial(grad_three, own),
        "grad_three",
        (steps,),
        [w_at, sca, w_at, c_at],
        [half_at, half_at],
        [half(), half()],
    )(flags, cotangent, live, moved, cp_t)
    three = start(keep, send, bits).go()
    gc_t = call(
        back_three,
        "back_three",
        (steps,),
        [w_at, sca, w_at, f_at(3)],
        whole(width, tokens),
        feat(BF16),
        [big, rows],
        prefetch=2,
    )(perm, flags, cotangent, live, moved, fac)
    gc_t, three.keep, three.came = lax.optimization_barrier((gc_t, three.keep, three.came))
    three.add()
    gc_t, three.keep, three.send = lax.optimization_barrier((gc_t, three.keep, three.send))
    three.go()
    keep, send, ga_t = call(
        functools.partial(back_two_one, own),
        "back_two_one",
        (steps,),
        [c_at, c_at, c_at, c_at, f_at(2), f_at(1)],
        [two_at, two_at, whole(width, tokens)],
        [half(0, (2,)), half(0, (2,)), feat(BF16)],
        [big, pltpu.VMEM(chunk, BF16), rows],
        prefetch=2,
    )(perm, flags, gc_t, h_t, ap_t, slope_t, fac, fac)
    came = lax.ppermute(send, "dp", [(i, i ^ 1) for i in range(replicas)])
    keep_zero, send_zero, gn, inner = call(
        functools.partial(back_zero, own),
        "back_zero",
        (steps,),
        [c_at, w_at, sca, g_at, f_at(0)],
        [more_at, more_at, w_at, sca],
        [half(EXTRA), half(EXTRA), row(F32), small],
        [pltpu.VMEM((tokens, bs), F32)],
    )(flags, ga_t, x, scale, gamma, fac)
    zero = start(keep_zero, send_zero, bits).go()
    gn, keep, came, three.keep, three.came = lax.optimization_barrier((gn, keep, came, three.keep, three.came))
    two, one = start(keep[0], None, other), start(keep[1], None, bits)
    for each, i in ((two, 0), (one, 1)):
        each.order.pop(0)
        each.came = came[i]
        each.add()
    three.add()
    gn, two.keep, two.send, one.keep, one.send, three.keep, three.send = lax.optimization_barrier(
        (gn, two.keep, two.send, one.keep, one.send, three.keep, three.send)
    )
    three.go()
    one.go()
    two.go()
    out_grad = call(
        back_last,
        "back_last",
        (steps,),
        [w_at, w_at, sca, w_at, w_at, sca, g_at, sca],
        w_at,
        row(BF16),
    )(flags, gn, cotangent, live, moved, x, scale, gamma, inner)
    zero.add()
    for each in (three, one, two):
        each.add()
    total = [each.finish() for each in (zero, one, two, three)]
    grad_gamma = total[0][:, bs, :].reshape(1, own * bs)
    total[0] = jnp.swapaxes(total[0][:, :bs, :], 1, 2)
    return (out_grad[None], jnp.stack(total)[None], grad_gamma)


def solution(mesh):
    replicas, sections = mesh.shape["dp"], mesh.shape["section"]
    in_specs = (
        P("section", "dp", None),
        P("dp", None),
        P("dp"),
        P("section", None),
        P("section", None, None, None, None),
        P("section", None),
    )
    out_specs = (P("section", "dp", None), P("section", None, "dp", None, None), P("section", "dp"))
    return jax.shard_map(
        functools.partial(on_device, replicas, sections),
        mesh=mesh,
        in_specs=in_specs,
        out_specs=out_specs,
        check_vma=False,
    )
```

time: 252 us -> 243 us (0.964)
  starting transfers between devices: 30.1 us -> 19.1 us
  waiting for transfers between devices: 76.1 us -> 85 us
  local copies, waits for them, and re-layouts: 10.9 us -> 6.45 us
    ppermute x20 -> x15, starting transfers between devices: 28.7 us -> 17.6 us  [the longest x14 17.6 us: go(): lax.ppermute(self.send, 'dp', [(i, i ^ 1 << bit) for i in range(self.repl...]
    unnamed x37 -> x6, local copies, waits for them, and re-layouts: 10 us -> 1.79 us
    ppermute x20 -> x15, waiting for transfers between devices: 43.5 us -> 50.8 us  [the longest x14 50.8 us: go(): lax.ppermute(self.send, 'dp', [(i, i ^ 1 << bit) for i in range(self.repl...]
    slice x0 -> x2, local copies, waits for them, and re-layouts: none -> 3.41 us  [the longest x1 2.68 us: on_device(): two, one = (start(keep[0], None, other), start(keep[1], None, bits))]
    convert_element_type x6 -> x9, other arithmetic: 11.1 us -> 8.46 us  [part(): total = (a.astype(F32) + b.astype(F32)).astype(self.keep.dtype)]
  transfers between devices with their start and end apart: 21 -> 16, of which waited for: 13 -> 10; matrix products, arithmetic and copies ran while one was open for 5% -> 6% of each run, Pallas kernels for 11% -> 16%
where the time goes in v2:
time: 243 us; the launch traced here: 242 us
  Pallas kernels  118 us (49%)
  waiting for transfers between devices  85 us (35%)
  starting transfers between devices  19.1 us (8%)
  other arithmetic  12.9 us (5%)
  local copies, waits for them, and re-layouts  6.45 us (3%)
    ppermute x14, waiting for transfers between devices, go(): lax.ppermute(self.send, 'dp', [(i, i ^ 1 << bit) for i in range(self.repl...  50.8 us
    pallas_call x1, Pallas kernels, on_device(): call(first_pass, 'first_pass', (4, steps), [tok, pl.BlockSpec(wide, lambd...  46.1 us
    ppermute x1, waiting for transfers between devices, on_device(): lax.ppermute(grad_x, 'section', [(i, i - 1) for i in range(1, sections)])  34.1 us
    pallas_call x1, Pallas kernels, on_device(): call(functools.partial(back_two_one, own), 'back_two_one', (steps,), [c_a...  19.5 us
    ppermute x14, starting transfers between devices, go(): lax.ppermute(self.send, 'dp', [(i, i ^ 1 << bit) for i in range(self.repl...  17.6 us
    pallas_call x1, Pallas kernels, on_device(): call(back_three, 'back_three', (steps,), [w_at, sca, w_at, f_at(3)], whol...  15.5 us
    pallas_call x1, Pallas kernels, on_device(): call(forward_second, 'forward_second', (2, steps), [pl.BlockSpec(chunk, l...  13.9 us
    pallas_call x1, Pallas kernels, on_device(): call(functools.partial(back_zero, own), 'back_zero', (steps,), [c_at, w_a...  8.53 us
  transfers between devices with their start and end apart: 16, of which 10 were waited for; matrix products, arithmetic and copies ran while one was open for 6% of the time, Pallas kernels for 16%

profile of v2, /device:TPU:0, one launch (start us, length us, event | category | flops | bytes accessed | tf_op | source)
XLA Modules:
  0.0 242.0 jit_solution(1265512882937727693)
XLA Ops:
  2.0 46.1 %first_pass.1 = (bf16[8192,128]{1,0:T(8,128)(2,1)}, bf16[8192,128]{1,0:T(8,128)(2,1)}, f32[8192,128]{1,0:T(8,128)}, f32[128,128]{1,0:T(8,128)}, bf16[128,8192]{1,0:T(8,128)(2,1)}) custom-call(s32[8192]{0:T(1024)} %bitcast.114, bf16[128,8192]{1,0:T(8,128)(2,1)} %bitcast.95, bf16[128,8192]{1,0:T(8,128)(2,1)} %cot.7, f32[128,128]{1,0:T(8,128)} %broadcast_in_dim.12.live, ...), custom_call_target="tpu_custom_call" | custom-call | tf_op jit(solution)/shard_map/first_pass/pallas_call | solution.py:370
  49.6 13.9 %forward_second.1.cp_t = bf16[8192,128]{1,0:T(8,128)(2,1)} custom-call(s32[8192]{0:T(1024)} %bitcast.115, bf16[8192,128]{1,0:T(8,128)(2,1)} %get-tuple-element.36.h_t, bf16[4,64,128,128]{3,2,1,0:T(8,128)(2,1)} %bitcast.90), custom_call_target="tpu_custom_call" | custom-call | tf_op jit(solution)/shard_map/forward_second/pallas_call | solution.py:389
  64.1 34.1 %collective-permute-done.moved = bf16[128,8192]{1,0:T(8,128)(2,1)S(1)} collective-permute-done((bf16[128,8192]{1,0:T(8,128)(2,1)}, bf16[128,8192]{1,0:T(8,128)(2,1)S(1)}, u32[]{:S(2)}, u32[]{:S(2)}) %collective-permute-start) | collective-permute-done | bytes 2097184 | tf_op jit(solution)/shard_map/ppermute | solution.py:386
  99.5 6.1 %grad_three.1 = (bf16[32,128,128]{2,1,0:T(8,128)(2,1)}, bf16[32,128,128]{2,1,0:T(8,128)(2,1)}) custom-call(s32[2]{0:T(128)} %pad_add_fusion.flags, bf16[128,8192]{1,0:T(8,128)(2,1)} %cot.7, f32[128,128]{1,0:T(8,128)} %broadcast_in_dim.12.live, bf16[128,8192]{1,0:T(8,128)(2,1)} %copy-done, bf16[8192,128]{1,0:T(8,128)(2,1)} %forward_second.1.cp_t), custom_call_target="tpu_custom_call" | custom-call | tf_op jit(solution)/shard_map/grad_three/pallas_call | solution.py:403
  105.7 15.5 %back_three.1.gc_t = bf16[8192,128]{1,0:T(8,128)(2,1)} custom-call(s32[8192]{0:T(1024)} %bitcast.116, s32[2]{0:T(128)} %pad_add_fusion.flags, bf16[128,8192]{1,0:T(8,128)(2,1)} %cot.7, f32[128,128]{1,0:T(8,128)} %broadcast_in_dim.12.live, bf16[128,8192]{1,0:T(8,128)(2,1)} %copy-done, bf16[4,64,128,128]{3,2,1,0:T(8,128)(2,1)} %bitcast.91), custom_call_target="tpu_custom_call" | custom-call | tf_op jit(solution)/shard_map/back_three/pallas_call | solution.py:412
  122.4 19.5 %back_two_one.1 = (bf16[2,32,128,128]{3,2,1,0:T(8,128)(2,1)}, bf16[2,32,128,128]{3,2,1,0:T(8,128)(2,1)}, bf16[8192,128]{1,0:T(8,128)(2,1)}) custom-call(s32[8192]{0:T(1024)} %bitcast.117, s32[2]{0:T(128)} %pad_add_fusion.flags, bf16[8192,128]{1,0:T(8,128)(2,1)} %back_three.1.gc_t, bf16[8192,128]{1,0:T(8,128)(2,1)} %get-tuple-element.36.h_t, ...), custom_call_target="tpu_custom_call" | custom-call | tf_op jit(solution)/shard_map/back_two_one/pallas_call | solution.py:426
  141.9 8.5 %back_zero.1 = (bf16[32,144,128]{2,1,0:T(8,128)(2,1)}, bf16[32,144,128]{2,1,0:T(8,128)(2,1)}, f32[128,8192]{1,0:T(8,128)}, f32[128,128]{1,0:T(8,128)}) custom-call(s32[2]{0:T(128)} %pad_add_fusion.flags, bf16[8192,128]{1,0:T(8,128)(2,1)} %get-tuple-element.45.ga_t, bf16[128,8192]{1,0:T(8,128)(2,1)} %bitcast.96, f32[128,128]{1,0:T(8,128)} %get-tuple-element.46.scale, ...), custom_call_target="tpu_custom_call" | custom-call | tf_op jit(solution)/shard_map/back_zero/pallas_call | solution.py:437
  151.1 3.5 %collective-permute-done.4 = bf16[32,144,128]{2,1,0:T(8,128)(2,1)S(1)} collective-permute-done((bf16[32,144,128]{2,1,0:T(8,128)(2,1)}, bf16[32,144,128]{2,1,0:T(8,128)(2,1)S(1)}, u32[]{:S(2)}, u32[]{:S(2)}) %collective-permute-start.4) | collective-permute-done | bytes 1179680 | tf_op jit(solution)/shard_map/ppermute | solution.py:290
  154.6 2.4 add_convert_fusion.1
  157.0 2.4 collective-permute-start.5
  159.9 13.8 %collective-permute-done.5 = bf16[16,144,128]{2,1,0:T(8,128)(2,1)S(1)} collective-permute-done((bf16[16,144,128]{2,1,0:T(8,128)(2,1)}, bf16[16,144,128]{2,1,0:T(8,128)(2,1)S(1)}, u32[]{:S(2)}, u32[]{:S(2)}) %collective-permute-start.5) | collective-permute-done | bytes 589856 | tf_op jit(solution)/shard_map/ppermute | solution.py:290
  175.3 2.1 collective-permute-start.6
  177.3 11.5 %collective-permute-done.6 = bf16[8,144,128]{1,2,0:T(8,128)(2,1)S(1)} collective-permute-done((bf16[8,144,128]{1,2,0:T(8,128)(2,1)}, bf16[8,144,128]{1,2,0:T(8,128)(2,1)S(1)}, u32[]{:S(2)}, u32[]{:S(2)}) %collective-permute-start.6) | collective-permute-done | bytes 294944 | tf_op jit(solution)/shard_map/ppermute | solution.py:290
  189.6 2.6 %collective-permute-start.7 = (bf16[4,144,128]{1,2,0:T(8,128)(2,1)}, bf16[4,144,128]{1,2,0:T(8,128)(2,1)}, u32[]{:S(2)}, u32[]{:S(2)}) collective-permute-start(bf16[4,144,128]{1,2,0:T(8,128)(2,1)} %fusion.2), channel_id=1, source_target_pairs={{0,8},{1,9},{2,10},{3,11},{4,12},{5,13},{6,14},{7,15},{8,0},{9,1},... | collective-permute-start | bytes 442376 | tf_op jit(solution)/shard_map/ppermute | solution.py:290
  192.2 2.7 %fusion.15 = (bf16[1,32,128,128]{3,2,1,0:T(8,128)(2,1)S(1)}, bf16[1,32,128,128]{3,2,1,0:T(8,128)(2,1)S(1)}, bf16[1,32,128,128]{3,2,1,0:T(8,128)(2,1)S(1)}, bf16[1,32,128,128]{3,2,1,0:T(8,128)(2,1)S(1)}) fusion(bf16[2,32,128,128]{3,2,1,0:T(8,128)(2,1)} %get-tuple-element.53, bf16[2,32,128,128]{3,2,1,0:T(8,128)(2,1)} %collective-permute-done.2), kind=kLoop, calls=%fused_computation.50 | loop fusion | bytes 8388608 | tf_op jit(solution)/shard_map/slice | solution.py:448
  196.4 1.9 add_convert_fusion.16
  201.8 8.2 %back_last.1 = bf16[128,8192]{1,0:T(8,128)(2,1)} custom-call(s32[2]{0:T(128)} %pad_add_fusion.flags, f32[128,8192]{1,0:T(8,128)} %get-tuple-element.57.gn, bf16[128,8192]{1,0:T(8,128)(2,1)} %cot.7, f32[128,128]{1,0:T(8,128)} %broadcast_in_dim.12.live, bf16[128,8192]{1,0:T(8,128)(2,1)} %copy-done, bf16[128,8192]{1,0:T(8,128)(2,1)} %bitcast.97, ...), custom_call_target="tpu_custom_call" | custom-call | tf_op jit(solution)/shard_map/back_last/pallas_call | solution.py:460
  211.3 1.6 collective-permute-start.9
  213.6 6.6 %collective-permute-done.14 = bf16[8,128,128]{2,1,0:T(8,128)(2,1)S(1)} collective-permute-done((bf16[8,128,128]{2,1,0:T(8,128)(2,1)}, bf16[8,128,128]{2,1,0:T(8,128)(2,1)S(1)}, u32[]{:S(2)}, u32[]{:S(2)}) %collective-permute-start.14) | collective-permute-done | bytes 262176 | tf_op jit(solution)/shard_map/ppermute | solution.py:290
  221.5 1.6 collective-permute-start.12
  223.1 3.1 %collective-permute-done.9 = bf16[8,128,128]{2,1,0:T(8,128)(2,1)S(1)} collective-permute-done((bf16[8,128,128]{2,1,0:T(8,128)(2,1)S(1)}, bf16[8,128,128]{2,1,0:T(8,128)(2,1)S(1)}, u32[]{:S(2)}, u32[]{:S(2)}) %collective-permute-start.9) | collective-permute-done | bytes 262176 | tf_op jit(solution)/shard_map/ppermute | solution.py:290
  226.8 2.1 collective-permute-done.15
  231.0 5.8 %collective-permute-done.10 = bf16[4,128,128]{2,1,0:T(8,128)(2,1)S(1)} collective-permute-done((bf16[4,128,128]{2,1,0:T(8,128)(2,1)S(1)}, bf16[4,128,128]{2,1,0:T(8,128)(2,1)S(1)}, u32[]{:S(2)}, u32[]{:S(2)}) %collective-permute-start.10) | collective-permute-done | bytes 131104 | tf_op jit(solution)/shard_map/ppermute | solution.py:290
  236.8 4.1 %collective-permute-done.13 = bf16[4,128,128]{2,1,0:T(8,128)(2,1)S(1)} collective-permute-done((bf16[4,128,128]{2,1,0:T(8,128)(2,1)S(1)}, bf16[4,128,128]{2,1,0:T(8,128)(2,1)S(1)}, u32[]{:S(2)}, u32[]{:S(2)}) %collective-permute-start.13) | collective-permute-done | bytes 131104 | tf_op jit(solution)/shard_map/ppermute | solution.py:290
  (46 shorter events, 21.6 us)
Async XLA Ops:
  48.1 50.1 %collective-permute-start = (bf16[128,8192]{1,0:T(8,128)(2,1)}, bf16[128,8192]{1,0:T(8,128)(2,1)S(1)}, u32[]{:S(2)}, u32[]{:S(2)}) collective-permute-start(bf16[128,8192]{1,0:T(8,128)(2,1)} %get-tuple-element.35), channel_id=1, source_target_pairs={{16,0},{17,1},{18,2},{19,3},{20,4},{21,5},{22,6},{23,7},{24,8},{25... | collective-permute-start | bytes 6291464 | tf_op jit(solution)/shard_map/ppermute | solution.py:386
  98.2 1.4 copy-start
  105.7 15.5 %collective-permute-start.1 = (bf16[32,128,128]{2,1,0:T(8,128)(2,1)}, bf16[32,128,128]{2,1,0:T(8,128)(2,1)S(1)}, u32[]{:S(2)}, u32[]{:S(2)}) collective-permute-start(bf16[32,128,128]{2,1,0:T(8,128)(2,1)} %get-tuple-element.38), channel_id=1, source_target_pairs={{0,1},{1,0},{2,3},{3,2},{4,5},{5,4},{6,7},{7,6},{8,9},{9,8},{10,11... | collective-permute-start | bytes 3145736 | tf_op jit(solution)/shard_map/ppermute | solution.py:290
  105.7 15.5 %copy-start.1 = (bf16[32,128,128]{2,1,0:T(8,128)(2,1)S(1)}, bf16[32,128,128]{2,1,0:T(8,128)(2,1)}, u32[]{:S(2)}) copy-start(bf16[32,128,128]{2,1,0:T(8,128)(2,1)} %get-tuple-element.40) | copy-start | bytes 3145732
  150.4 4.2 %collective-permute-start.4 = (bf16[32,144,128]{2,1,0:T(8,128)(2,1)}, bf16[32,144,128]{2,1,0:T(8,128)(2,1)S(1)}, u32[]{:S(2)}, u32[]{:S(2)}) collective-permute-start(bf16[32,144,128]{2,1,0:T(8,128)(2,1)} %get-tuple-element.60), channel_id=1, source_target_pairs={{0,1},{1,0},{2,3},{3,2},{4,5},{5,4},{6,7},{7,6},{8,9},{9,8},{10,11... | collective-permute-start | bytes 3538952 | tf_op jit(solution)/shard_map/ppermute | solution.py:290
  151.0 41.2 %collective-permute-start.2 = (bf16[2,32,128,128]{3,2,1,0:T(8,128)(2,1)}, bf16[2,32,128,128]{3,2,1,0:T(8,128)(2,1)}, u32[]{:S(2)}, u32[]{:S(2)}) collective-permute-start(bf16[2,32,128,128]{3,2,1,0:T(8,128)(2,1)} %get-tuple-element.49), channel_id=1, source_target_pairs={{0,1},{1,0},{2,3},{3,2},{4,5},{5,4},{6,7},{7,6},{8,9},{9,8},{10,11... | collective-permute-start | bytes 6291464 | tf_op jit(solution)/shard_map/ppermute | solution.py:436
  157.0 16.7 %collective-permute-start.5 = (bf16[16,144,128]{2,1,0:T(8,128)(2,1)}, bf16[16,144,128]{2,1,0:T(8,128)(2,1)S(1)}, u32[]{:S(2)}, u32[]{:S(2)}) collective-permute-start(bf16[16,144,128]{2,1,0:T(8,128)(2,1)} %bitcast.25), channel_id=1, source_target_pairs={{0,2},{1,3},{2,0},{3,1},{4,6},{5,7},{6,4},{7,5},{8,10},{9,11},{10,... | collective-permute-start | bytes 1769480 | tf_op jit(solution)/shard_map/ppermute | solution.py:290
  159.3 32.8 %collective-permute-start.3 = (bf16[16,128,128]{2,1,0:T(8,128)(2,1)}, bf16[16,128,128]{2,1,0:T(8,128)(2,1)}, u32[]{:S(2)}, u32[]{:S(2)}) collective-permute-start(bf16[16,128,128]{2,1,0:T(8,128)(2,1)} %bitcast.8), channel_id=1, source_target_pairs={{0,2},{1,3},{2,0},{3,1},{4,6},{5,7},{6,4},{7,5},{8,10},{9,11},{10,... | collective-permute-start | bytes 1572872 | tf_op jit(solution)/shard_map/ppermute | solution.py:290
  175.3 13.5 %collective-permute-start.6 = (bf16[8,144,128]{1,2,0:T(8,128)(2,1)}, bf16[8,144,128]{1,2,0:T(8,128)(2,1)S(1)}, u32[]{:S(2)}, u32[]{:S(2)}) collective-permute-start(bf16[8,144,128]{1,2,0:T(8,128)(2,1)} %bitcast.27), channel_id=1, source_target_pairs={{0,4},{1,5},{2,6},{3,7},{4,0},{5,1},{6,2},{7,3},{8,12},{9,13},{10,... | collective-permute-start | bytes 884744 | tf_op jit(solution)/shard_map/ppermute | solution.py:290
  189.6 20.4 %collective-permute-start.7 = (bf16[4,144,128]{1,2,0:T(8,128)(2,1)}, bf16[4,144,128]{1,2,0:T(8,128)(2,1)}, u32[]{:S(2)}, u32[]{:S(2)}) collective-permute-start(bf16[4,144,128]{1,2,0:T(8,128)(2,1)} %fusion.2), channel_id=1, source_target_pairs={{0,8},{1,9},{2,10},{3,11},{4,12},{5,13},{6,14},{7,15},{8,0},{9,1},... | collective-permute-start | bytes 442376 | tf_op jit(solution)/shard_map/ppermute | solution.py:290
  198.3 12.8 %collective-permute-start.8 = (bf16[16,128,128]{2,1,0:T(8,128)(2,1)}, bf16[16,128,128]{2,1,0:T(8,128)(2,1)S(1)}, u32[]{:S(2)}, u32[]{:S(2)}) collective-permute-start(bf16[16,128,128]{2,1,0:T(8,128)(2,1)} %bitcast.16), channel_id=1, source_target_pairs={{0,2},{1,3},{2,0},{3,1},{4,6},{5,7},{6,4},{7,5},{8,10},{9,11},{10,... | collective-permute-start | bytes 1572872 | tf_op jit(solution)/shard_map/ppermute | solution.py:290
  199.8 21.5 %collective-permute-start.11 = (bf16[16,128,128]{2,1,0:T(8,128)(2,1)S(1)}, bf16[16,128,128]{2,1,0:T(8,128)(2,1)S(1)}, u32[]{:S(2)}, u32[]{:S(2)}) collective-permute-start(bf16[16,128,128]{2,1,0:T(8,128)(2,1)S(1)} %bitcast.120), channel_id=1, source_target_pairs={{0,4},{1,5},{2,6},{3,7},{4,0},{5,1},{6,2},{7,3},{8,12},{9,13},{10,... | collective-permute-start | bytes 1572872 | tf_op jit(solution)/shard_map/ppermute | solution.py:290
  201.4 18.8 %collective-permute-start.14 = (bf16[8,128,128]{2,1,0:T(8,128)(2,1)}, bf16[8,128,128]{2,1,0:T(8,128)(2,1)S(1)}, u32[]{:S(2)}, u32[]{:S(2)}) collective-permute-start(bf16[8,128,128]{2,1,0:T(8,128)(2,1)} %bitcast.129), channel_id=1, source_target_pairs={{0,4},{1,5},{2,6},{3,7},{4,0},{5,1},{6,2},{7,3},{8,12},{9,13},{10,... | collective-permute-start | bytes 786440 | tf_op jit(solution)/shard_map/ppermute | solution.py:290
  211.3 15.0 %collective-permute-start.9 = (bf16[8,128,128]{2,1,0:T(8,128)(2,1)S(1)}, bf16[8,128,128]{2,1,0:T(8,128)(2,1)S(1)}, u32[]{:S(2)}, u32[]{:S(2)}) collective-permute-start(bf16[8,128,128]{2,1,0:T(8,128)(2,1)S(1)} %bitcast.130), channel_id=1, source_target_pairs={{0,4},{1,5},{2,6},{3,7},{4,0},{5,1},{6,2},{7,3},{8,12},{9,13},{10,... | collective-permute-start | bytes 786440 | tf_op jit(solution)/shard_map/ppermute | solution.py:290
  220.2 8.6 %collective-permute-start.15 = (bf16[4,128,128]{2,1,0:T(8,128)(2,1)S(1)}, bf16[4,128,128]{2,1,0:T(8,128)(2,1)S(1)}, u32[]{:S(2)}, u32[]{:S(2)}) collective-permute-start(bf16[4,128,128]{2,1,0:T(8,128)(2,1)S(1)} %fusion.10), channel_id=1, source_target_pairs={{0,8},{1,9},{2,10},{3,11},{4,12},{5,13},{6,14},{7,15},{8,0},{9,1},... | collective-permute-start | bytes 393224 | tf_op jit(solution)/shard_map/ppermute | solution.py:290
  221.5 7.9 %collective-permute-start.12 = (bf16[8,128,128]{2,1,0:T(8,128)(2,1)S(1)}, bf16[8,128,128]{2,1,0:T(8,128)(2,1)S(1)}, u32[]{:S(2)}, u32[]{:S(2)}) collective-permute-start(bf16[8,128,128]{2,1,0:T(8,128)(2,1)S(1)} %bitcast.131), channel_id=1, source_target_pairs={{0,2},{1,3},{2,0},{3,1},{4,6},{5,7},{6,4},{7,5},{8,10},{9,11},{10,... | collective-permute-start | bytes 786440 | tf_op jit(solution)/shard_map/ppermute | solution.py:290
  226.3 10.5 %collective-permute-start.10 = (bf16[4,128,128]{2,1,0:T(8,128)(2,1)S(1)}, bf16[4,128,128]{2,1,0:T(8,128)(2,1)S(1)}, u32[]{:S(2)}, u32[]{:S(2)}) collective-permute-start(bf16[4,128,128]{2,1,0:T(8,128)(2,1)S(1)} %fusion.12), channel_id=1, source_target_pairs={{0,8},{1,9},{2,10},{3,11},{4,12},{5,13},{6,14},{7,15},{8,0},{9,1},... | collective-permute-start | bytes 393224 | tf_op jit(solution)/shard_map/ppermute | solution.py:290
  229.4 11.4 %collective-permute-start.13 = (bf16[4,128,128]{2,1,0:T(8,128)(2,1)S(1)}, bf16[4,128,128]{2,1,0:T(8,128)(2,1)S(1)}, u32[]{:S(2)}, u32[]{:S(2)}) collective-permute-start(bf16[4,128,128]{2,1,0:T(8,128)(2,1)S(1)} %fusion.14), channel_id=1, source_target_pairs={{0,8},{1,9},{2,10},{3,11},{4,12},{5,13},{6,14},{7,15},{8,0},{9,1},... | collective-permute-start | bytes 393224 | tf_op jit(solution)/shard_map/ppermute | solution.py:290

commit v3 on v2

--- a/solution.py
+++ b/solution.py
@@ -14,7 +14,6 @@
 STEP = 16
 UNROLL = 8
 EXTRA = 16
-VMEM_BYTES = 56 << 20
 
 
 def dot(a, b, ca, cb):
@@ -25,7 +24,7 @@
     return pl.BlockSpec(shape, lambda *_: (0,) * len(shape))
 
 
-def call(body, name, grid, in_specs, out_specs, out_shape, scratch=(), prefetch=1):
+def call(body, name, grid, in_specs, out_specs, out_shape, scratch=(), prefetch=1, vmem=50):
     return pl.pallas_call(
         body,
         name=name,
@@ -37,7 +36,7 @@
             out_specs=out_specs,
             scratch_shapes=scratch,
         ),
-        compiler_params=pltpu.CompilerParams(vmem_limit_bytes=VMEM_BYTES),
+        compiler_params=pltpu.CompilerParams(vmem_limit_bytes=vmem << 20),
     )
 
 
@@ -212,10 +211,12 @@
         gc_out[...] = gc_t[...].astype(BF16)
 
 
-def back_two_one(own, perm, flags, gc_t, h_t, ap_t, slope_t, fac_two, fac_one, keep, send, ga_out, ga_t, gpre, rows):
+def back_two_one(
+    own, perm, flags, gc_t, h_t, ap_t, slope_t, fac_two, fac_one, keep_two, send_two, keep_one, send_one, ga_out, ga_t, gpre, rows
+):
     c = pl.program_id(0)
     bs = fac_two.shape[2]
-    outs = (keep, send)
+    twos, ones = (keep_two, send_two), (keep_one, send_one)
 
     def one(k, u):
         here = at_block(k, bs)
@@ -228,8 +229,8 @@
 
     def grads(goes, k, block):
         at = at_block(block, bs)
-        outs[goes][0, k] = dot(h_t[at, :], gc_t[at, :], 1, 1).astype(BF16)
-        outs[goes][1, k] = dot(ap_t[at, :], gpre[at, :], 1, 1).astype(BF16)
+        twos[goes][k] = dot(h_t[at, :], gc_t[at, :], 1, 1).astype(BF16)
+        ones[goes][k] = dot(ap_t[at, :], gpre[at, :], 1, 1).astype(BF16)
 
     each_split(flags, own, grads)
 
@@ -251,7 +252,7 @@
         at = at_block(block, bs)
         z = zed_block(x, scale, at)
         zg = z * gamma[:, at]
-        outs[goes][k, pl.ds(0, bs), :] = dot(ga_t[at, :], zg.astype(BF16), 1, 0).astype(BF16)
+        outs[goes][k, pl.ds(0, bs), :] = dot(zg.astype(BF16), ga_t[at, :], 0, 1).astype(BF16)
         value = dot(ga_t[at, :], fac[0, block], 0, 1)
         gn[:, at] = value
         total = jnp.sum(value * z, axis=0, keepdims=True)
@@ -284,6 +285,7 @@
         self.left = list(range(replicas.bit_length() - 1))[::-1]
         self.left.remove(self.order[0])
         self.own, self.me, self.replicas = own, me, replicas
+        self.came = None
 
     def go(self):
         bit = self.order.pop(0)
@@ -292,7 +294,7 @@
 
     def add(self):
         if not self.order:
-            self.keep = self.keep.astype(F32) + self.came.astype(F32)
+            self.keep, self.send, self.came = self.keep.astype(F32) + self.came.astype(F32), None, None
             return self
         bit = self.order[0]
         place = self.left.index(bit)
@@ -308,12 +310,27 @@
 
         self.left.remove(bit)
         self.send, self.keep = part(1 - mine), part(mine)
+        self.came = None
         return self
 
     def finish(self):
+        if self.came is not None:
+            self.add()
         while self.order:
             self.go().add()
         return self.keep / self.replicas
+
+
+def met(*halvings, then):
+    state = [(h.keep, h.send if h.came is None else h.came) for h in halvings]
+    state, then = lax.optimization_barrier((state, then))
+    for h, (keep, rest) in zip(halvings, state):
+        h.keep = keep
+        if h.came is None:
+            h.send = rest
+        else:
+            h.came = rest
+    return then
 
 
 def on_device(replicas, sections, activations, cotangent, token_ids, gains, factors, monarch_perm):
@@ -382,6 +399,7 @@
         [mid, mid, mid, sca, pl.BlockSpec(wide, lambda ph, c, *_: (0, out_at(ph, c)))],
         [feat(BF16), feat(BF16), feat(F32), small, row(BF16)],
         [big, big, big, pltpu.VMEM((tokens, width), F32), pltpu.VMEM((tokens, bs), F32), rows, rows],
+        vmem=50,
     )(perm, x, cotangent, live, gamma, fac, fac)
     moved = lax.ppermute(grad_x, "section", [(i, i - 1) for i in range(1, sections)])
 
@@ -419,21 +437,27 @@
         [big, rows],
         prefetch=2,
     )(perm, flags, cotangent, live, moved, fac)
-    gc_t, three.keep, three.came = lax.optimization_barrier((gc_t, three.keep, three.came))
+    (gc_t,) = met(three, then=[gc_t])
     three.add()
-    gc_t, three.keep, three.send = lax.optimization_barrier((gc_t, three.keep, three.send))
+    (gc_t,) = met(three, then=[gc_t])
     three.go()
-    keep, send, ga_t = call(
+    keep_two, send_two, keep_one, send_one, ga_t = call(
         functools.partial(back_two_one, own),
         "back_two_one",
         (steps,),
         [c_at, c_at, c_at, c_at, f_at(2), f_at(1)],
-        [two_at, two_at, whole(width, tokens)],
-        [half(0, (2,)), half(0, (2,)), feat(BF16)],
+        [half_at] * 4 + [whole(width, tokens)],
+        [half()] * 4 + [feat(BF16)],
         [big, pltpu.VMEM(chunk, BF16), rows],
         prefetch=2,
     )(perm, flags, gc_t, h_t, ap_t, slope_t, fac, fac)
-    came = lax.ppermute(send, "dp", [(i, i ^ 1) for i in range(replicas)])
+    two, one = start(keep_two, send_two, other), start(keep_one, send_one, bits)
+    ga_t, one.keep, one.send, two.keep, two.send = met(three, then=[ga_t, one.keep, one.send, two.keep, two.send])
+    three.add()
+    (ga_t,) = met(three, then=[ga_t])
+    one.go()
+    two.go()
+    three.go()
     keep_zero, send_zero, gn, inner = call(
         functools.partial(back_zero, own),
         "back_zero",
@@ -443,20 +467,14 @@
         [half(EXTRA), half(EXTRA), row(F32), small],
         [pltpu.VMEM((tokens, bs), F32)],
     )(flags, ga_t, x, scale, gamma, fac)
-    zero = start(keep_zero, send_zero, bits).go()
-    gn, keep, came, three.keep, three.came = lax.optimization_barrier((gn, keep, came, three.keep, three.came))
-    two, one = start(keep[0], None, other), start(keep[1], None, bits)
-    for each, i in ((two, 0), (one, 1)):
-        each.order.pop(0)
-        each.came = came[i]
+    zero = start(keep_zero, send_zero, bits)
+    gn, zero.keep, zero.send = met(one, two, three, then=[gn, zero.keep, zero.send])
+    zero.go()
+    for each in (one, two, three):
         each.add()
-    three.add()
-    gn, two.keep, two.send, one.keep, one.send, three.keep, three.send = lax.optimization_barrier(
-        (gn, two.keep, two.send, one.keep, one.send, three.keep, three.send)
-    )
-    three.go()
-    one.go()
-    two.go()
+    (gn,) = met(one, two, three, then=[gn])
+    for each in (one, two, three):
+        each.go()
     out_grad = call(
         back_last,
         "back_last",
@@ -465,12 +483,15 @@
         w_at,
         row(BF16),
     )(flags, gn, cotangent, live, moved, x, scale, gamma, inner)
+    (out_grad,) = met(zero, then=[out_grad])
     zero.add()
-    for each in (three, one, two):
+    (out_grad,) = met(zero, one, two, three, then=[out_grad])
+    zero.go()
+    for each in (one, two, three):
         each.add()
     total = [each.finish() for each in (zero, one, two, three)]
     grad_gamma = total[0][:, bs, :].reshape(1, own * bs)
-    total[0] = jnp.swapaxes(total[0][:, :bs, :], 1, 2)
+    total[0] = total[0][:, :bs, :]
     return (out_grad[None], jnp.stack(total)[None], grad_gamma)
 
 

time: 243 us -> 221 us (0.909)
  waiting for transfers between devices: 85 us -> 68.8 us
  Pallas kernels: 118 us -> 112 us
  starting transfers between devices: 19.1 us -> 22.3 us
    ppermute x14 -> x16, waiting for transfers between devices: 50.8 us -> 34.4 us  [go(): lax.ppermute(self.send, 'dp', [(i, i ^ 1 << bit) for i in range(self.repl...]
    unnamed x6 -> x18, local copies, waits for them, and re-layouts: 1.79 us -> 5.62 us
    slice x2 -> x0, local copies, waits for them, and re-layouts: 3.41 us -> none  [the longest x1 2.68 us: on_device(): two, one = (start(keep[0], None, other), start(keep[1], None, bits))]
    ppermute x14 -> x16, starting transfers between devices: 17.6 us -> 20.8 us  [go(): lax.ppermute(self.send, 'dp', [(i, i ^ 1 << bit) for i in range(self.repl...]
  transfers between devices with their start and end apart: 16 -> 17, of which waited for: 10 -> 7; matrix products, arithmetic and copies ran while one was open for 6% -> 3% of each run, Pallas kernels for 16% -> 28%
where the time goes in v3:
time: 221 us; the launch traced here: 220 us
  Pallas kernels  112 us (51%)
  waiting for transfers between devices  68.8 us (31%)
  starting transfers between devices  22.3 us (10%)
  other arithmetic  10.6 us (5%)
  local copies, waits for them, and re-layouts  6.29 us (3%)
    pallas_call x1, Pallas kernels, on_device(): call(first_pass, 'first_pass', (4, steps), [tok, pl.BlockSpec(wide, lambd...  45.6 us
    ppermute x16, waiting for transfers between devices, go(): lax.ppermute(self.send, 'dp', [(i, i ^ 1 << bit) for i in range(self.repl...  34.4 us
    ppermute x1, waiting for transfers between devices, on_device(): lax.ppermute(grad_x, 'section', [(i, i - 1) for i in range(1, sections)])  34.4 us
    ppermute x16, starting transfers between devices, go(): lax.ppermute(self.send, 'dp', [(i, i ^ 1 << bit) for i in range(self.repl...  20.8 us
    pallas_call x1, Pallas kernels, on_device(): call(functools.partial(back_two_one, own), 'back_two_one', (steps,), [c_a...  19.3 us
    pallas_call x1, Pallas kernels, on_device(): call(back_three, 'back_three', (steps,), [w_at, sca, w_at, f_at(3)], whol...  13.8 us
    pallas_call x1, Pallas kernels, on_device(): call(forward_second, 'forward_second', (2, steps), [pl.BlockSpec(chunk, l...  12.9 us
    convert_element_type x9, other arithmetic, part(): total = (a.astype(F32) + b.astype(F32)).astype(self.keep.dtype)  8.47 us
  transfers between devices with their start and end apart: 17, of which 7 were waited for; matrix products, arithmetic and copies ran while one was open for 3% of the time, Pallas kernels for 28%

profile of v3, /device:TPU:0, one launch (start us, length us, event | category | flops | bytes accessed | tf_op | source)
XLA Modules:
  0.0 220.4 jit_solution(6078321849819230903)
XLA Ops:
  2.9 45.6 %first_pass.1 = (bf16[8192,128]{1,0:T(8,128)(2,1)S(1)}, bf16[8192,128]{1,0:T(8,128)(2,1)}, f32[8192,128]{1,0:T(8,128)}, f32[128,128]{1,0:T(8,128)S(1)}, bf16[128,8192]{1,0:T(8,128)(2,1)}) custom-call(s32[8192]{0:T(1024)S(1)} %bitcast.89, bf16[128,8192]{1,0:T(8,128)(2,1)} %bitcast.100, bf16[128,8192]{1,0:T(8,128)(2,1)} %cot.7, ...), custom_call_target="tpu_custom_call" | custom-call | tf_op jit(solution)/shard_map/first_pass/pallas_call | solution.py:387
  51.4 12.9 %forward_second.1.cp_t = bf16[8192,128]{1,0:T(8,128)(2,1)S(1)} custom-call(s32[8192]{0:T(1024)S(1)} %bitcast.90, bf16[8192,128]{1,0:T(8,128)(2,1)} %get-tuple-element.64.h_t, bf16[4,64,128,128]{3,2,1,0:T(8,128)(2,1)} %bitcast.95), custom_call_target="tpu_custom_call" | custom-call | tf_op jit(solution)/shard_map/forward_second/pallas_call | solution.py:407
  65.7 34.4 %collective-permute-done.moved = bf16[128,8192]{1,0:T(8,128)(2,1)} collective-permute-done((bf16[128,8192]{1,0:T(8,128)(2,1)}, bf16[128,8192]{1,0:T(8,128)(2,1)}, u32[]{:S(2)}, u32[]{:S(2)}) %collective-permute-start) | collective-permute-done | bytes 2097184 | tf_op jit(solution)/shard_map/ppermute | solution.py:404
  100.1 4.8 %grad_three.1 = (bf16[32,128,128]{2,1,0:T(8,128)(2,1)S(1)}, bf16[32,128,128]{2,1,0:T(8,128)(2,1)S(1)}) custom-call(s32[2]{0:T(128)S(1)} %pad_add_fusion.flags, bf16[128,8192]{1,0:T(8,128)(2,1)} %cot.7, f32[128,128]{1,0:T(8,128)S(1)} %broadcast_in_dim.12.live, bf16[128,8192]{1,0:T(8,128)(2,1)} %collective-permute-done.moved, bf16[8192,128]{1,0:T(8,128)(2,1)} %copy-done.2), custom_call_target="tpu_custom_call" | custom-call | tf_op jit(solution)/shard_map/grad_three/pallas_call | solution.py:421
  105.0 13.8 %back_three.1.gc_t = bf16[8192,128]{1,0:T(8,128)(2,1)S(1)} custom-call(s32[8192]{0:T(1024)S(1)} %bitcast.91, s32[2]{0:T(128)S(1)} %pad_add_fusion.flags, bf16[128,8192]{1,0:T(8,128)(2,1)} %cot.7, f32[128,128]{1,0:T(8,128)S(1)} %broadcast_in_dim.12.live, bf16[128,8192]{1,0:T(8,128)(2,1)} %collective-permute-done.moved, bf16[4,64,128,128]{3,2,1,0:T(8,128)(2,1)} %bitcast.96), custom_call_target="tpu_custom_call" | custom-call | tf_op jit(solution)/shard_map/back_three/pallas_call | solution.py:430
  121.4 2.3 %collective-permute-start.2 = (bf16[16,128,128]{2,1,0:T(8,128)(2,1)S(1)}, bf16[16,128,128]{2,1,0:T(8,128)(2,1)S(1)}, u32[]{:S(2)}, u32[]{:S(2)}) collective-permute-start(bf16[16,128,128]{2,1,0:T(8,128)(2,1)S(1)} %bitcast.117), channel_id=1, source_target_pairs={{0,2},{1,3},{2,0},{3,1},{4,6},{5,7},{6,4},{7,5},{8,10},{9,11},{10,... | collective-permute-start | bytes 1572872 | tf_op jit(solution)/shard_map/ppermute | solution.py:292
  123.7 19.3 %back_two_one.1 = (bf16[32,128,128]{2,1,0:T(8,128)(2,1)S(1)}, bf16[32,128,128]{2,1,0:T(8,128)(2,1)}, bf16[32,128,128]{2,1,0:T(8,128)(2,1)S(1)}, bf16[32,128,128]{2,1,0:T(8,128)(2,1)}, bf16[8192,128]{1,0:T(8,128)(2,1)}) custom-call(s32[8192]{0:T(1024)S(1)} %bitcast.92, s32[2]{0:T(128)S(1)} %pad_add_fusion.flags, bf16[8192,128]{1,0:T(8,128)(2,1)} %copy-done.1, ...), custom_call_target="tpu_custom_call" | custom-call | tf_op jit(solution)/shard_map/back_two_one/pallas_call | solution.py:444
  144.4 1.6 collective-permute-start.5
  146.0 7.9 %back_zero.1 = (bf16[32,144,128]{2,1,0:T(8,128)(2,1)S(1)}, bf16[32,144,128]{2,1,0:T(8,128)(2,1)}, f32[128,8192]{1,0:T(8,128)}, f32[128,128]{1,0:T(8,128)S(1)}) custom-call(s32[2]{0:T(128)S(1)} %pad_add_fusion.flags, bf16[8192,128]{1,0:T(8,128)(2,1)} %get-tuple-element.89.ga_t, bf16[128,8192]{1,0:T(8,128)(2,1)} %bitcast.101, ...), custom_call_target="tpu_custom_call" | custom-call | tf_op jit(solution)/shard_map/back_zero/pallas_call | solution.py:461
  155.1 1.6 add_convert_fusion.4
  156.7 1.7 add_convert_fusion.2
  159.6 2.6 %collective-permute-start.9 = (bf16[4,128,128]{2,1,0:T(8,128)(2,1)S(1)}, bf16[4,128,128]{2,1,0:T(8,128)(2,1)S(1)}, u32[]{:S(2)}, u32[]{:S(2)}) collective-permute-start(bf16[4,128,128]{2,1,0:T(8,128)(2,1)S(1)} %get-tuple-element.112), channel_id=1, source_target_pairs={{0,8},{1,9},{2,10},{3,11},{4,12},{5,13},{6,14},{7,15},{8,0},{9,1},... | collective-permute-start | bytes 393224 | tf_op jit(solution)/shard_map/ppermute | solution.py:292
  162.2 7.3 %back_last.1 = bf16[128,8192]{1,0:T(8,128)(2,1)} custom-call(s32[2]{0:T(128)S(1)} %pad_add_fusion.flags, f32[128,8192]{1,0:T(8,128)} %get-tuple-element.103.gn, bf16[128,8192]{1,0:T(8,128)(2,1)S(1)} %copy-done, f32[128,128]{1,0:T(8,128)S(1)} %broadcast_in_dim.12.live, bf16[128,8192]{1,0:T(8,128)(2,1)} %collective-permute-done.moved, ...), custom_call_target="tpu_custom_call" | custom-call | tf_op jit(solution)/shard_map/back_last/pallas_call | solution.py:478
  171.1 2.9 %collective-permute-done.9 = bf16[4,128,128]{2,1,0:T(8,128)(2,1)S(1)} collective-permute-done((bf16[4,128,128]{2,1,0:T(8,128)(2,1)S(1)}, bf16[4,128,128]{2,1,0:T(8,128)(2,1)S(1)}, u32[]{:S(2)}, u32[]{:S(2)}) %collective-permute-start.9) | collective-permute-done | bytes 131104 | tf_op jit(solution)/shard_map/ppermute | solution.py:292
  173.9 1.9 collective-permute-done.8
  178.2 2.7 %collective-permute-start.13 = (bf16[8,128,128]{2,1,0:T(8,128)(2,1)S(1)}, bf16[8,128,128]{2,1,0:T(8,128)(2,1)S(1)}, u32[]{:S(2)}, u32[]{:S(2)}) collective-permute-start(bf16[8,128,128]{2,1,0:T(8,128)(2,1)S(1)} %bitcast.125), channel_id=1, source_target_pairs={{0,4},{1,5},{2,6},{3,7},{4,0},{5,1},{6,2},{7,3},{8,12},{9,13},{10,... | collective-permute-start | bytes 786440 | tf_op jit(solution)/shard_map/ppermute | solution.py:292
  180.9 15.1 %collective-permute-done.15 = bf16[8,128,128]{2,1,0:T(8,128)(2,1)S(1)} collective-permute-done((bf16[8,128,128]{2,1,0:T(8,128)(2,1)S(1)}, bf16[8,128,128]{2,1,0:T(8,128)(2,1)S(1)}, u32[]{:S(2)}, u32[]{:S(2)}) %collective-permute-start.15) | collective-permute-done | bytes 262176 | tf_op jit(solution)/shard_map/ppermute | solution.py:292
  196.1 1.6 collective-permute-start.16
  197.8 1.7 collective-permute-start.11
  199.6 2.4 %collective-permute-start.14 = (bf16[4,128,128]{2,1,0:T(8,128)(2,1)S(1)}, bf16[4,128,128]{2,1,0:T(8,128)(2,1)S(1)}, u32[]{:S(2)}, u32[]{:S(2)}) collective-permute-start(bf16[4,128,128]{2,1,0:T(8,128)(2,1)S(1)} %fusion.10), channel_id=1, source_target_pairs={{0,8},{1,9},{2,10},{3,11},{4,12},{5,13},{6,14},{7,15},{8,0},{9,1},... | collective-permute-start | bytes 393224 | tf_op jit(solution)/shard_map/ppermute | solution.py:292
  202.0 3.8 %collective-permute-done.16 = bf16[4,128,128]{2,1,0:T(8,128)(2,1)S(1)} collective-permute-done((bf16[4,128,128]{2,1,0:T(8,128)(2,1)S(1)}, bf16[4,128,128]{2,1,0:T(8,128)(2,1)S(1)}, u32[]{:S(2)}, u32[]{:S(2)}) %collective-permute-start.16) | collective-permute-done | bytes 131104 | tf_op jit(solution)/shard_map/ppermute | solution.py:292
  205.8 4.2 %collective-permute-done.11 = bf16[8,144,128]{2,1,0:T(8,128)(2,1)S(1)} collective-permute-done((bf16[8,144,128]{2,1,0:T(8,128)(2,1)S(1)}, bf16[8,144,128]{2,1,0:T(8,128)(2,1)S(1)}, u32[]{:S(2)}, u32[]{:S(2)}) %collective-permute-start.11) | collective-permute-done | bytes 294944 | tf_op jit(solution)/shard_map/ppermute | solution.py:292
  210.1 2.0 collective-permute-start.12
  212.1 6.5 %collective-permute-done.12 = bf16[4,144,128]{2,1,0:T(8,128)(2,1)S(1)} collective-permute-done((bf16[4,144,128]{2,1,0:T(8,128)(2,1)S(1)}, bf16[4,144,128]{2,1,0:T(8,128)(2,1)S(1)}, u32[]{:S(2)}, u32[]{:S(2)}) %collective-permute-start.12) | collective-permute-done | bytes 147488 | tf_op jit(solution)/shard_map/ppermute | solution.py:292
  (57 shorter events, 19.1 us)
Async XLA Ops:
  2.9 48.5 %copy-start.5 = (s32[1,8192]{1,0:T(1,128)S(1)}, s32[1,8192]{1,0:T(1,128)}, u32[]{:S(2)}) copy-start(s32[1,8192]{1,0:T(1,128)} %param.11) | copy-start | bytes 98308
  48.5 1.4 copy-start.3
  49.9 50.2 %collective-permute-start = (bf16[128,8192]{1,0:T(8,128)(2,1)}, bf16[128,8192]{1,0:T(8,128)(2,1)}, u32[]{:S(2)}, u32[]{:S(2)}) collective-permute-start(bf16[128,8192]{1,0:T(8,128)(2,1)} %get-tuple-element.63), channel_id=1, source_target_pairs={{16,0},{17,1},{18,2},{19,3},{20,4},{21,5},{22,6},{23,7},{24,8},{25... | collective-permute-start | bytes 6291464 | tf_op jit(solution)/shard_map/ppermute | solution.py:404
  64.3 1.4 copy-start.2
  104.9 15.3 %collective-permute-start.1 = (bf16[32,128,128]{2,1,0:T(8,128)(2,1)S(1)}, bf16[32,128,128]{2,1,0:T(8,128)(2,1)S(1)}, u32[]{:S(2)}, u32[]{:S(2)}) collective-permute-start(bf16[32,128,128]{2,1,0:T(8,128)(2,1)S(1)} %get-tuple-element.66), channel_id=1, source_target_pairs={{0,1},{1,0},{2,3},{3,2},{4,5},{5,4},{6,7},{7,6},{8,9},{9,8},{10,11... | collective-permute-start | bytes 3145736 | tf_op jit(solution)/shard_map/ppermute | solution.py:292
  118.8 1.4 copy-start.1
  121.4 21.6 %collective-permute-start.2 = (bf16[16,128,128]{2,1,0:T(8,128)(2,1)S(1)}, bf16[16,128,128]{2,1,0:T(8,128)(2,1)S(1)}, u32[]{:S(2)}, u32[]{:S(2)}) collective-permute-start(bf16[16,128,128]{2,1,0:T(8,128)(2,1)S(1)} %bitcast.117), channel_id=1, source_target_pairs={{0,2},{1,3},{2,0},{3,1},{4,6},{5,7},{6,4},{7,5},{8,10},{9,11},{10,... | collective-permute-start | bytes 1572872 | tf_op jit(solution)/shard_map/ppermute | solution.py:292
  123.7 19.9 %copy-start.8 = (bf16[4,1,4,128,128]{4,3,2,1,0:T(8,128)(2,1)S(1)}, bf16[4,1,4,128,128]{4,3,2,1,0:T(8,128)(2,1)}, u32[]{:S(2)}) copy-start(bf16[4,1,4,128,128]{4,3,2,1,0:T(8,128)(2,1)} %get-tuple-element.130) | copy-start | bytes 1572868
  123.7 22.3 %copy-start.7 = (f32[1,8192]{1,0:T(1,128)S(1)}, f32[1,8192]{1,0:T(1,128)}, u32[]{:S(2)}) copy-start(f32[1,8192]{1,0:T(1,128)} %gamma.5) | copy-start | bytes 98308
  143.0 10.9 %collective-permute-start.3 = (bf16[32,128,128]{2,1,0:T(8,128)(2,1)}, bf16[32,128,128]{2,1,0:T(8,128)(2,1)}, u32[]{:S(2)}, u32[]{:S(2)}) collective-permute-start(bf16[32,128,128]{2,1,0:T(8,128)(2,1)} %get-tuple-element.81), channel_id=1, source_target_pairs={{0,1},{1,0},{2,3},{3,2},{4,5},{5,4},{6,7},{7,6},{8,9},{9,8},{10,11... | collective-permute-start | bytes 3145736 | tf_op jit(solution)/shard_map/ppermute | solution.py:292
  143.2 10.6 %collective-permute-start.4 = (bf16[32,128,128]{2,1,0:T(8,128)(2,1)}, bf16[32,128,128]{2,1,0:T(8,128)(2,1)}, u32[]{:S(2)}, u32[]{:S(2)}) collective-permute-start(bf16[32,128,128]{2,1,0:T(8,128)(2,1)} %get-tuple-element.83), channel_id=1, source_target_pairs={{0,1},{1,0},{2,3},{3,2},{4,5},{5,4},{6,7},{7,6},{8,9},{9,8},{10,11... | collective-permute-start | bytes 3145736 | tf_op jit(solution)/shard_map/ppermute | solution.py:292
  144.4 9.4 %collective-permute-start.5 = (bf16[8,128,128]{2,1,0:T(8,128)(2,1)S(1)}, bf16[8,128,128]{2,1,0:T(8,128)(2,1)}, u32[]{:S(2)}, u32[]{:S(2)}) collective-permute-start(bf16[8,128,128]{2,1,0:T(8,128)(2,1)S(1)} %bitcast.127), channel_id=1, source_target_pairs={{0,4},{1,5},{2,6},{3,7},{4,0},{5,1},{6,2},{7,3},{8,12},{9,13},{10,... | collective-permute-start | bytes 786440 | tf_op jit(solution)/shard_map/ppermute | solution.py:292
  153.8 15.7 %collective-permute-start.6 = (bf16[32,144,128]{2,1,0:T(8,128)(2,1)}, bf16[32,144,128]{2,1,0:T(8,128)(2,1)}, u32[]{:S(2)}, u32[]{:S(2)}) collective-permute-start(bf16[32,144,128]{2,1,0:T(8,128)(2,1)} %get-tuple-element.95), channel_id=1, source_target_pairs={{0,1},{1,0},{2,3},{3,2},{4,5},{5,4},{6,7},{7,6},{8,9},{9,8},{10,11... | collective-permute-start | bytes 3538952 | tf_op jit(solution)/shard_map/ppermute | solution.py:292
  156.7 5.5 %copy-start = (bf16[128,8192]{1,0:T(8,128)(2,1)S(1)}, bf16[128,8192]{1,0:T(8,128)(2,1)}, u32[]{:S(2)}) copy-start(bf16[128,8192]{1,0:T(8,128)(2,1)} %cot.7) | copy-start | bytes 6291460
  158.4 15.5 %collective-permute-start.7 = (bf16[16,128,128]{2,1,0:T(8,128)(2,1)S(1)}, bf16[16,128,128]{2,1,0:T(8,128)(2,1)S(1)}, u32[]{:S(2)}, u32[]{:S(2)}) collective-permute-start(bf16[16,128,128]{2,1,0:T(8,128)(2,1)S(1)} %bitcast.113), channel_id=1, source_target_pairs={{0,2},{1,3},{2,0},{3,1},{4,6},{5,7},{6,4},{7,5},{8,10},{9,11},{10,... | collective-permute-start | bytes 1572872 | tf_op jit(solution)/shard_map/ppermute | solution.py:292
  159.0 16.8 %collective-permute-start.8 = (bf16[16,128,128]{2,1,0:T(8,128)(2,1)S(1)}, bf16[16,128,128]{2,1,0:T(8,128)(2,1)S(1)}, u32[]{:S(2)}, u32[]{:S(2)}) collective-permute-start(bf16[16,128,128]{2,1,0:T(8,128)(2,1)S(1)} %bitcast.116), channel_id=1, source_target_pairs={{0,4},{1,5},{2,6},{3,7},{4,0},{5,1},{6,2},{7,3},{8,12},{9,13},{10,... | collective-permute-start | bytes 1572872 | tf_op jit(solution)/shard_map/ppermute | solution.py:292
  159.6 14.4 %collective-permute-start.9 = (bf16[4,128,128]{2,1,0:T(8,128)(2,1)S(1)}, bf16[4,128,128]{2,1,0:T(8,128)(2,1)S(1)}, u32[]{:S(2)}, u32[]{:S(2)}) collective-permute-start(bf16[4,128,128]{2,1,0:T(8,128)(2,1)S(1)} %get-tuple-element.112), channel_id=1, source_target_pairs={{0,8},{1,9},{2,10},{3,11},{4,12},{5,13},{6,14},{7,15},{8,0},{9,1},... | collective-permute-start | bytes 393224 | tf_op jit(solution)/shard_map/ppermute | solution.py:292
  175.8 21.8 %collective-permute-start.10 = (bf16[16,144,128]{2,1,0:T(8,128)(2,1)S(1)}, bf16[16,144,128]{2,1,0:T(8,128)(2,1)S(1)}, u32[]{:S(2)}, u32[]{:S(2)}) collective-permute-start(bf16[16,144,128]{2,1,0:T(8,128)(2,1)S(1)} %bitcast.111), channel_id=1, source_target_pairs={{0,2},{1,3},{2,0},{3,1},{4,6},{5,7},{6,4},{7,5},{8,10},{9,11},{10,... | collective-permute-start | bytes 1769480 | tf_op jit(solution)/shard_map/ppermute | solution.py:292
  177.5 18.6 %collective-permute-start.15 = (bf16[8,128,128]{2,1,0:T(8,128)(2,1)S(1)}, bf16[8,128,128]{2,1,0:T(8,128)(2,1)S(1)}, u32[]{:S(2)}, u32[]{:S(2)}) collective-permute-start(bf16[8,128,128]{2,1,0:T(8,128)(2,1)S(1)} %bitcast.126), channel_id=1, source_target_pairs={{0,2},{1,3},{2,0},{3,1},{4,6},{5,7},{6,4},{7,5},{8,10},{9,11},{10,... | collective-permute-start | bytes 786440 | tf_op jit(solution)/shard_map/ppermute | solution.py:292
  178.2 21.3 %collective-permute-start.13 = (bf16[8,128,128]{2,1,0:T(8,128)(2,1)S(1)}, bf16[8,128,128]{2,1,0:T(8,128)(2,1)S(1)}, u32[]{:S(2)}, u32[]{:S(2)}) collective-permute-start(bf16[8,128,128]{2,1,0:T(8,128)(2,1)S(1)} %bitcast.125), channel_id=1, source_target_pairs={{0,4},{1,5},{2,6},{3,7},{4,0},{5,1},{6,2},{7,3},{8,12},{9,13},{10,... | collective-permute-start | bytes 786440 | tf_op jit(solution)/shard_map/ppermute | solution.py:292
  196.1 9.7 %collective-permute-start.16 = (bf16[4,128,128]{2,1,0:T(8,128)(2,1)S(1)}, bf16[4,128,128]{2,1,0:T(8,128)(2,1)S(1)}, u32[]{:S(2)}, u32[]{:S(2)}) collective-permute-start(bf16[4,128,128]{2,1,0:T(8,128)(2,1)S(1)} %fusion.12), channel_id=1, source_target_pairs={{0,8},{1,9},{2,10},{3,11},{4,12},{5,13},{6,14},{7,15},{8,0},{9,1},... | collective-permute-start | bytes 393224 | tf_op jit(solution)/shard_map/ppermute | solution.py:292
  197.8 12.2 %collective-permute-start.11 = (bf16[8,144,128]{2,1,0:T(8,128)(2,1)S(1)}, bf16[8,144,128]{2,1,0:T(8,128)(2,1)S(1)}, u32[]{:S(2)}, u32[]{:S(2)}) collective-permute-start(bf16[8,144,128]{2,1,0:T(8,128)(2,1)S(1)} %bitcast.120), channel_id=1, source_target_pairs={{0,4},{1,5},{2,6},{3,7},{4,0},{5,1},{6,2},{7,3},{8,12},{9,13},{10,... | collective-permute-start | bytes 884744 | tf_op jit(solution)/shard_map/ppermute | solution.py:292
  199.6 12.4 %collective-permute-start.14 = (bf16[4,128,128]{2,1,0:T(8,128)(2,1)S(1)}, bf16[4,128,128]{2,1,0:T(8,128)(2,1)S(1)}, u32[]{:S(2)}, u32[]{:S(2)}) collective-permute-start(bf16[4,128,128]{2,1,0:T(8,128)(2,1)S(1)} %fusion.10), channel_id=1, source_target_pairs={{0,8},{1,9},{2,10},{3,11},{4,12},{5,13},{6,14},{7,15},{8,0},{9,1},... | collective-permute-start | bytes 393224 | tf_op jit(solution)/shard_map/ppermute | solution.py:292
  210.1 8.6 %collective-permute-start.12 = (bf16[4,144,128]{2,1,0:T(8,128)(2,1)S(1)}, bf16[4,144,128]{2,1,0:T(8,128)(2,1)S(1)}, u32[]{:S(2)}, u32[]{:S(2)}) collective-permute-start(bf16[4,144,128]{2,1,0:T(8,128)(2,1)S(1)} %fusion.6), channel_id=1, source_target_pairs={{0,8},{1,9},{2,10},{3,11},{4,12},{5,13},{6,14},{7,15},{8,0},{9,1},... | collective-permute-start | bytes 442376 | tf_op jit(solution)/shard_map/ppermute | solution.py:292
  (2 other events, 1.5 us)

commit v4 on v3

--- a/solution.py
+++ b/solution.py
@@ -24,10 +24,11 @@
     return pl.BlockSpec(shape, lambda *_: (0,) * len(shape))
 
 
-def call(body, name, grid, in_specs, out_specs, out_shape, scratch=(), prefetch=1, vmem=50):
+def call(body, name, grid, in_specs, out_specs, out_shape, scratch=(), prefetch=1, vmem=50, aliases=None):
     return pl.pallas_call(
         body,
         name=name,
+        input_output_aliases=aliases or {},
         out_shape=out_shape,
         grid_spec=pltpu.PrefetchScalarGridSpec(
             num_scalar_prefetch=prefetch,
@@ -71,6 +72,59 @@
         target[pl.ds(perm[base + i], 1), :] = source[pl.ds(i, 1), :]
 
 
+def scattered(make, perm, first, target, even, odd, bs):
+    def move(k, source):
+        scatter_rows(perm, (first + k) * bs, source, target, bs)
+
+    even[...] = make(0)
+
+    def pair(i, carry):
+        k = 2 * i
+        odd[...] = make(k + 1)
+        move(k, even)
+        even[...] = make(k + 2)
+        move(k + 1, odd)
+        return carry
+
+    lax.fori_loop(0, STEP // 2 - 1, pair, 0)
+    odd[...] = make(STEP - 1)
+    move(STEP - 2, even)
+    move(STEP - 1, odd)
+
+
+def gathered_scattered(make, perm, first, source, target, even_in, odd_in, even_out, odd_out, bs):
+    def fetch(k, into):
+        gather_rows(perm, (first + k) * bs, source, into, bs)
+
+    def move(k, out):
+        scatter_rows(perm, (first + k) * bs, out, target, bs)
+
+    fetch(0, even_in)
+    fetch(1, odd_in)
+    even_out[...] = make(0, even_in)
+
+    def pair(i, carry):
+        k = 2 * i
+        odd_out[...] = make(k + 1, odd_in)
+        fetch(k + 2, even_in)
+        move(k, even_out)
+        even_out[...] = make(k + 2, even_in)
+        fetch(k + 3, odd_in)
+        move(k + 1, odd_out)
+        return carry
+
+    lax.fori_loop(0, STEP // 2 - 1, pair, 0)
+    odd_out[...] = make(STEP - 1, odd_in)
+    move(STEP - 2, even_out)
+    move(STEP - 1, odd_out)
+
+
+def put_split(stage, flags, own, k, value):
+    device = lax.div(k, own)
+    goes = lax.bitwise_xor(lax.bitwise_and(device, 1), flags[0])
+    stage[goes, lax.div(device, 2) * own + lax.rem(k, own)] = value.astype(BF16)
+
+
 def seeded_block(cot, live, cols):
     return (cot[:, cols].astype(F32) * live[...]).astype(BF16)
 
@@ -79,7 +133,9 @@
     return (gy.astype(F32) + scale[...] * (gn * gamma - z * inner[...])).astype(BF16)
 
 
-def first_pass(perm, x, cot, live, gamma, fac_a, fac_b, ap_t, h_t, slope_t, scale, grad_x, a_t, gc_t, ga_t, gn, acc, rows, rows_b):
+def first_pass(
+    perm, x, cot, live, gamma, fac_a, fac_b, ap_t, h_t, slope_t, scale, grad_a, grad_b, a_t, gc_t, ga_t, gn, acc, r0, r1, r2, r3
+):
     phase, c = pl.program_id(0), pl.program_id(1)
     bs = fac_a.shape[2]
     blocks = x.shape[1] // bs
@@ -97,34 +153,29 @@
 
     @pl.when(phase == 0)
     def _():
-        def one(k, u):
-            block = c * STEP + k
-            cols = at_block(block, bs)
+        def make(k):
+            cols = at_block(c * STEP + k, bs)
             n = (zed_block(x, scale, cols) * gamma[:, cols]).astype(BF16)
             a_t[cols, :] = rounded(dot(fac_a[0, k], n, 0, 1))
-            rows[u] = rounded(dot(fac_b[0, k], seeded_block(cot, live, at_block(k, bs)), 1, 1))
-            scatter_rows(perm, block * bs, rows.at[u], gc_t, bs)
-
-        each_block(one)
+            return rounded(dot(fac_b[0, k], seeded_block(cot, live, at_block(k, bs)), 1, 1))
+
+        scattered(make, perm, c * STEP, gc_t, r0, r1, bs)
 
     @pl.when(phase == 1)
     def _():
-        def one(k, u):
-            block = c * STEP + k
+        def make(k, rows):
             here = at_block(k, bs)
-            gather_rows(perm, block * bs, a_t, rows.at[u], bs)
-            ap = rows[u].astype(BF16)
+            ap = rows[...].astype(BF16)
             ap_t[here, :] = ap
             pre = dot(fac_a[0, k], ap, 0, 0)
             cdf = 0.5 * (1.0 + lax.erf(pre * inv_sqrt_two))
             h_t[here, :] = (pre * cdf).astype(BF16)
             slope = cdf + pre * jnp.exp(-0.5 * pre * pre) * inv_sqrt_two_pi
             slope_t[here, :] = slope
-            gh = dot(fac_b[0, k], gc_t[at_block(block, bs), :].astype(BF16), 1, 0)
-            rows_b[u] = rounded(dot(fac_a[0, k], (gh * slope).astype(BF16), 1, 0))
-            scatter_rows(perm, block * bs, rows_b.at[u], ga_t, bs)
-
-        each_block(one)
+            gh = dot(fac_b[0, k], gc_t[at_block(c * STEP + k, bs), :].astype(BF16), 1, 0)
+            return rounded(dot(fac_a[0, k], (gh * slope).astype(BF16), 1, 0))
+
+        gathered_scattered(make, perm, c * STEP, a_t, ga_t, r0, r1, r2, r3, bs)
 
     @pl.when(phase == 2)
     def _():
@@ -141,15 +192,18 @@
         mean = jnp.sum(acc[...], axis=1, keepdims=True) / x.shape[1]
         acc[...] = jnp.broadcast_to(mean, acc.shape)
 
-    @pl.when(phase == 3)
-    def _():
+    def emit(out):
         def one(k, u):
             here = at_block(k, bs)
             cols = at_block(c * STEP + k, bs)
             z = zed_block(x, scale, cols)
-            grad_x[:, here] = gradient(seeded_block(cot, live, here), gn[:, cols], gamma[:, cols], z, scale, acc)
+            out[:, here] = gradient(seeded_block(cot, live, here), gn[:, cols], gamma[:, cols], z, scale, acc)
 
         each_block(one, unroll=4)
+
+    last = pl.num_programs(1) - 1
+    pl.when(jnp.logical_and(phase == 3, c < last))(lambda: emit(grad_a))
+    pl.when(jnp.logical_and(phase == 3, c == last))(lambda: emit(grad_b))
 
 
 def forward_second(perm, h_t, fac, cp_t, c_t, rows):
@@ -181,58 +235,42 @@
         body(1, k, base + (1 - flags[0]) * own)
 
 
-def chosen_gy(flags, cot, live, moved, cols):
-    return jnp.where(flags[1] == 1, seeded_block(cot, live, cols), moved[:, cols])
-
-
-def grad_three(own, flags, cot, live, moved, cp_t, keep, send):
-    bs = live.shape[1]
-    outs = (keep, send)
-
-    def one(goes, k, block):
-        at = at_block(block, bs)
-        outs[goes][k] = dot(cp_t[at, :], chosen_gy(flags, cot, live, moved, at), 1, 0).astype(BF16)
-
-    each_split(flags, own, one)
-
-
-def back_three(perm, flags, cot, live, moved, fac, gc_out, gc_t, rows):
-    c = pl.program_id(0)
+def back_three(own, skipped, perm, flags, cot, live, moved, cp_t, fac, *refs):
+    *given, keep, send, gy_out, gc_t, stage, even, odd = refs
     bs = fac.shape[2]
-
-    def one(k, u):
-        rows[u] = rounded(dot(fac[0, k], chosen_gy(flags, cot, live, moved, at_block(k, bs)), 1, 1))
-        scatter_rows(perm, (c * STEP + k) * bs, rows.at[u], gc_t, bs)
-
-    each_block(one)
-
-    @pl.when(c == pl.num_programs(0) - 1)
-    def _():
-        gc_out[...] = gc_t[...].astype(BF16)
+    if given:
+        gc_t[...] = given[3][...]
+
+    def make(k):
+        here = at_block(k, bs)
+        gy = jnp.where(flags[1] == 1, seeded_block(cot, live, here), moved[:, here])
+        gy_out[:, here] = gy
+        put_split(stage, flags, own, k, dot(cp_t[here, :], gy, 1, 0))
+        return rounded(dot(fac[0, k], gy, 1, 1))
+
+    scattered(make, perm, (pl.program_id(0) + skipped) * STEP, gc_t, even, odd, bs)
+    keep[...] = stage[0]
+    send[...] = stage[1]
 
 
 def back_two_one(
-    own, perm, flags, gc_t, h_t, ap_t, slope_t, fac_two, fac_one, keep_two, send_two, keep_one, send_one, ga_out, ga_t, gpre, rows
+    own, perm, flags, gc_t, h_t, ap_t, slope_t, fac_two, fac_one, keep_two, send_two, keep_one, send_one, ga_out, ga_t, twos, ones, even, odd
 ):
     c = pl.program_id(0)
     bs = fac_two.shape[2]
-    twos, ones = (keep_two, send_two), (keep_one, send_one)
-
-    def one(k, u):
+
+    def make(k):
         here = at_block(k, bs)
-        gh = dot(fac_two[0, k], gc_t[here, :], 1, 0)
-        gpre[here, :] = (gh * slope_t[here, :]).astype(BF16)
-        rows[u] = rounded(dot(fac_one[0, k], gpre[here, :], 1, 0))
-        scatter_rows(perm, (c * STEP + k) * bs, rows.at[u], ga_t, bs)
-
-    each_block(one)
-
-    def grads(goes, k, block):
-        at = at_block(block, bs)
-        twos[goes][k] = dot(h_t[at, :], gc_t[at, :], 1, 1).astype(BF16)
-        ones[goes][k] = dot(ap_t[at, :], gpre[at, :], 1, 1).astype(BF16)
-
-    each_split(flags, own, grads)
+        gc = gc_t[here, :].astype(BF16)
+        gh = dot(fac_two[0, k], gc, 1, 0)
+        gpre = (gh * slope_t[here, :]).astype(BF16)
+        put_split(twos, flags, own, k, dot(h_t[here, :], gc, 1, 1))
+        put_split(ones, flags, own, k, dot(ap_t[here, :], gpre, 1, 1))
+        return rounded(dot(fac_one[0, k], gpre, 1, 0))
+
+    scattered(make, perm, c * STEP, ga_t, even, odd, bs)
+    keep_two[...], send_two[...] = twos[0], twos[1]
+    keep_one[...], send_one[...] = ones[0], ones[1]
 
     @pl.when(c == pl.num_programs(0) - 1)
     def _():
@@ -267,14 +305,13 @@
         inner[...] = jnp.broadcast_to(mean, inner.shape)
 
 
-def back_last(flags, gn, cot, live, moved, x, scale, gamma, inner, grad_x):
-    bs = live.shape[1]
+def back_last(gy, gn, x, scale, gamma, inner, grad_x):
+    bs = scale.shape[1]
 
     def one(k, u):
         cols = at_block(k, bs)
         z = zed_block(x, scale, cols)
-        gy = chosen_gy(flags, cot, live, moved, cols)
-        grad_x[:, cols] = gradient(gy, gn[:, cols], gamma[:, cols], z, scale, inner)
+        grad_x[:, cols] = gradient(gy[:, cols], gn[:, cols], gamma[:, cols], z, scale, inner)
 
     each_block(one, unroll=4)
 
@@ -368,6 +405,9 @@
     two_at = pl.BlockSpec((2, STEP // 2, bs, bs), lambda c, *_: (0, c, 0, 0))
     big = pltpu.VMEM((width, tokens), F32)
     rows = pltpu.VMEM((UNROLL, bs, tokens), F32)
+    block = pltpu.VMEM((bs, tokens), F32)
+    stage = pltpu.VMEM((2, STEP // 2, bs, bs), BF16)
+    part = (steps - 1) * STEP * bs
     last = steps - 1
 
     def phased(*picks):
@@ -384,7 +424,7 @@
     b_which, b_at = pick((3, 2, 2)), phased(None, None, last, last)
     cot_at, out_at, mid_at = phased(None, last, last, None), phased(0, 0, 0, None), phased(0, None, last, last)
     mid = pl.BlockSpec(chunk, lambda ph, c, *_: (mid_at(ph, c), 0))
-    ap_t, h_t, slope_t, scale, grad_x = call(
+    ap_t, h_t, slope_t, scale, *grad_x = call(
         first_pass,
         "first_pass",
         (4, steps),
@@ -396,12 +436,19 @@
             pl.BlockSpec(fblock, lambda ph, c, *_: (a_which(ph), a_at(ph, c), 0, 0)),
             pl.BlockSpec(fblock, lambda ph, c, *_: (b_which(ph), b_at(ph, c), 0, 0)),
         ],
-        [mid, mid, mid, sca, pl.BlockSpec(wide, lambda ph, c, *_: (0, out_at(ph, c)))],
-        [feat(BF16), feat(BF16), feat(F32), small, row(BF16)],
-        [big, big, big, pltpu.VMEM((tokens, width), F32), pltpu.VMEM((tokens, bs), F32), rows, rows],
+        [mid, mid, mid, sca, pl.BlockSpec(wide, lambda ph, c, *_: (0, jnp.minimum(out_at(ph, c), last - 1))), whole(*wide)],
+        [
+            feat(BF16),
+            feat(BF16),
+            feat(F32),
+            small,
+            jax.ShapeDtypeStruct((tokens, part), BF16),
+            jax.ShapeDtypeStruct(wide, BF16),
+        ],
+        [big, big, big, pltpu.VMEM((tokens, width), F32), pltpu.VMEM((tokens, bs), F32)] + [block] * 4,
         vmem=50,
     )(perm, x, cotangent, live, gamma, fac, fac)
-    moved = lax.ppermute(grad_x, "section", [(i, i - 1) for i in range(1, sections)])
+    moved = [lax.ppermute(piece, "section", [(i, i - 1) for i in range(1, sections)]) for piece in grad_x]
 
     early, rest = phased(None, last), phased(0, None)
     cp_t = call(
@@ -418,28 +465,33 @@
     )(perm, h_t, fac)
 
     start = lambda keep, send, order: Halving(keep, send, order, own, me, replicas)
-    keep, send = call(
-        functools.partial(grad_three, own),
-        "grad_three",
-        (steps,),
-        [w_at, sca, w_at, c_at],
-        [half_at, half_at],
-        [half(), half()],
-    )(flags, cotangent, live, moved, cp_t)
-    three = start(keep, send, bits).go()
-    gc_t = call(
-        back_three,
-        "back_three",
-        (steps,),
-        [w_at, sca, w_at, f_at(3)],
-        whole(width, tokens),
-        feat(BF16),
-        [big, rows],
+    shapes = [half(), half(), row(BF16), feat(F32)]
+    scratch = [stage, block, block]
+    partial = call(
+        functools.partial(back_three, own, 0),
+        "back_three_early",
+        (steps - 1,),
+        [w_at, sca, w_at, c_at, f_at(3)],
+        [half_at, half_at, w_at, whole(width, tokens)],
+        shapes,
+        scratch,
         prefetch=2,
-    )(perm, flags, cotangent, live, moved, fac)
-    (gc_t,) = met(three, then=[gc_t])
-    three.add()
-    (gc_t,) = met(three, then=[gc_t])
+    )(perm, flags, cotangent, live, moved[0], cp_t, fac)
+    shift = lambda spec: pl.BlockSpec(spec.block_shape, lambda c, *_: spec.index_map(c + last))
+    held = pl.BlockSpec(memory_space=pl.ANY)
+    partial, moved[1] = lax.optimization_barrier((partial, moved[1]))
+    keep, send, gy, gc_t = call(
+        functools.partial(back_three, own, steps - 1),
+        "back_three_late",
+        (1,),
+        [shift(w_at), sca, w_at, shift(c_at), shift(f_at(3)), held, held, held, whole(width, tokens)],
+        [shift(half_at), shift(half_at), shift(w_at), whole(width, tokens)],
+        shapes,
+        scratch,
+        prefetch=2,
+        aliases={7: 0, 8: 1, 9: 2, 10: 3},
+    )(perm, flags, cotangent, live, moved[1], cp_t, fac, *partial)
+    three = start(keep, send, bits)
     three.go()
     keep_two, send_two, keep_one, send_one, ga_t = call(
         functools.partial(back_two_one, own),
@@ -448,7 +500,7 @@
         [c_at, c_at, c_at, c_at, f_at(2), f_at(1)],
         [half_at] * 4 + [whole(width, tokens)],
         [half()] * 4 + [feat(BF16)],
-        [big, pltpu.VMEM(chunk, BF16), rows],
+        [big, stage, stage, block, block],
         prefetch=2,
     )(perm, flags, gc_t, h_t, ap_t, slope_t, fac, fac)
     two, one = start(keep_two, send_two, other), start(keep_one, send_one, bits)
@@ -468,25 +520,29 @@
         [pltpu.VMEM((tokens, bs), F32)],
     )(flags, ga_t, x, scale, gamma, fac)
     zero = start(keep_zero, send_zero, bits)
-    gn, zero.keep, zero.send = met(one, two, three, then=[gn, zero.keep, zero.send])
+    gn, zero.keep, zero.send = met(one, two, then=[gn, zero.keep, zero.send])
     zero.go()
-    for each in (one, two, three):
-        each.add()
-    (gn,) = met(one, two, three, then=[gn])
-    for each in (one, two, three):
-        each.go()
+    one.add()
+    two.add()
+    (gn,) = met(one, two, then=[gn])
+    one.go()
+    two.go()
+    (gn,) = met(zero, three, then=[gn])
+    zero.add()
+    three.add()
+    (gn,) = met(zero, three, then=[gn])
+    zero.go()
+    three.go()
     out_grad = call(
         back_last,
         "back_last",
         (steps,),
-        [w_at, w_at, sca, w_at, w_at, sca, g_at, sca],
+        [w_at, w_at, w_at, sca, g_at, sca],
         w_at,
         row(BF16),
-    )(flags, gn, cotangent, live, moved, x, scale, gamma, inner)
-    (out_grad,) = met(zero, then=[out_grad])
-    zero.add()
-    (out_grad,) = met(zero, one, two, three, then=[out_grad])
-    zero.go()
+        prefetch=0,
+    )(gy, gn, x, scale, gamma, inner)
+    (out_grad,) = met(one, two, three, then=[out_grad])
     for each in (one, two, three):
         each.add()
     total = [each.finish() for each in (zero, one, two, three)]

time: 221 us -> 214 us (0.968)
  waiting for transfers between devices: 68.8 us -> 47.6 us
  Pallas kernels: 112 us -> 122 us
  other arithmetic: 10.6 us -> 17.2 us
    ppermute x1 -> x2, waiting for transfers between devices: 34.4 us -> 22.5 us  [on_device(): lax.ppermute(piece, 'section', [(i, i - 1) for i in range(1, sections)])]
    ppermute x16, waiting for transfers between devices: 34.4 us -> 25.1 us  [go(): lax.ppermute(self.send, 'dp', [(i, i ^ 1 << bit) for i in range(self.repl...]
    convert_element_type x9, other arithmetic: 8.47 us -> 15.1 us  [part(): total = (a.astype(F32) + b.astype(F32)).astype(self.keep.dtype)]
    pallas_call x1, Pallas kernels: 19.3 us -> 25.1 us  [on_device(): call(functools.partial(back_two_one, own), 'back_two_one', (steps,), [c_a...]
    pallas_call x3, Pallas kernels: 26 us -> 30 us  [the longest x1 15.4 us: on_device(): call(functools.partial(back_three, own, 0), 'back_three_early', (steps -...]
    ppermute x16, starting transfers between devices: 20.8 us -> 18.2 us  [go(): lax.ppermute(self.send, 'dp', [(i, i ^ 1 << bit) for i in range(self.repl...]
    unnamed x18 -> x26, local copies, waits for them, and re-layouts: 5.62 us -> 3.95 us
  transfers between devices with their start and end apart: 17 -> 18, of which waited for: 7 -> 8; matrix products, arithmetic and copies ran while one was open for 3% -> 7% of each run, Pallas kernels for 28% -> 32%
where the time goes in v4:
time: 214 us; the launch traced here: 213 us
  Pallas kernels  122 us (57%)
  waiting for transfers between devices  47.6 us (22%)
  starting transfers between devices  20.9 us (10%)
  other arithmetic  17.2 us (8%)
  local copies, waits for them, and re-layouts  4.62 us (2%)
    pallas_call x1, Pallas kernels, on_device(): call(first_pass, 'first_pass', (4, steps), [tok, pl.BlockSpec(wide, lambd...  46.2 us
    ppermute x16, waiting for transfers between devices, go(): lax.ppermute(self.send, 'dp', [(i, i ^ 1 << bit) for i in range(self.repl...  25.1 us
    pallas_call x1, Pallas kernels, on_device(): call(functools.partial(back_two_one, own), 'back_two_one', (steps,), [c_a...  25.1 us
    ppermute x2, waiting for transfers between devices, on_device(): lax.ppermute(piece, 'section', [(i, i - 1) for i in range(1, sections)])  22.5 us
    ppermute x16, starting transfers between devices, go(): lax.ppermute(self.send, 'dp', [(i, i ^ 1 << bit) for i in range(self.repl...  18.2 us
    pallas_call x1, Pallas kernels, on_device(): call(functools.partial(back_three, own, 0), 'back_three_early', (steps -...  15.4 us
    convert_element_type x9, other arithmetic, part(): total = (a.astype(F32) + b.astype(F32)).astype(self.keep.dtype)  15.1 us
    pallas_call x1, Pallas kernels, on_device(): call(forward_second, 'forward_second', (2, steps), [pl.BlockSpec(chunk, l...  12.9 us
  transfers between devices with their start and end apart: 18, of which 8 were waited for; matrix products, arithmetic and copies ran while one was open for 7% of the time, Pallas kernels for 32%

profile of v4, /device:TPU:0, one launch (start us, length us, event | category | flops | bytes accessed | tf_op | source)
XLA Modules:
  0.0 213.1 jit_solution(14036081721510095623)
XLA Ops:
  2.9 46.2 %first_pass.1 = (bf16[8192,128]{1,0:T(8,128)(2,1)}, bf16[8192,128]{1,0:T(8,128)(2,1)}, f32[8192,128]{1,0:T(8,128)}, f32[128,128]{1,0:T(8,128)S(1)}, bf16[128,614...) custom-call(s32[8192]{0:T(1024)S(1)} %bitcast.92, bf16[128,8192]{1,0:T(8,128)(2,1)} %bitcast.105, bf16[128,8192]{1,0:T(8,128)(2,1)} %cot.5, ...), custom_call_target="tpu_custom_call" | custom-call | tf_op jit(solution)/shard_map/first_pass/pallas_call | solution.py:427
  51.9 12.9 %forward_second.1.cp_t = bf16[8192,128]{1,0:T(8,128)(2,1)S(1)} custom-call(s32[8192]{0:T(1024)S(1)} %bitcast.93, bf16[8192,128]{1,0:T(8,128)(2,1)} %get-tuple-element.71.h_t, bf16[4,64,128,128]{3,2,1,0:T(8,128)(2,1)} %bitcast.99), custom_call_target="tpu_custom_call" | custom-call | tf_op jit(solution)/shard_map/forward_second/pallas_call | solution.py:454
  66.2 22.5 %collective-permute-done.moved = bf16[128,6144]{1,0:T(8,128)(2,1)S(1)} collective-permute-done((bf16[128,6144]{1,0:T(8,128)(2,1)}, bf16[128,6144]{1,0:T(8,128)(2,1)S(1)}, u32[]{:S(2)}, u32[]{:S(2)}) %collective-permute-start) | collective-permute-done | bytes 1572896 | tf_op jit(solution)/shard_map/ppermute | solution.py:451
  88.7 15.4 %back_three_early.1 = (bf16[32,128,128]{2,1,0:T(8,128)(2,1)S(1)}, bf16[32,128,128]{2,1,0:T(8,128)(2,1)S(1)}, bf16[128,8192]{1,0:T(8,128)(2,1)}, f32[8192,128]{1,0:T(8,128)}) custom-call(s32[8192]{0:T(1024)S(1)} %bitcast.94, s32[2]{0:T(128)S(1)} %pad_add_fusion.flags, bf16[128,8192]{1,0:T(8,128)(2,1)} %cot.5, f32[128,128]{1,0:T(8,128)S(1)} %broadcast_in_dim.12.live, ...), custom_call_target="tpu_custom_call" | custom-call | tf_op jit(solution)/shard_map/back_three_early/pallas_call | solution.py:470
  104.1 8.6 %back_three_late.1 = (bf16[32,128,128]{2,1,0:T(8,128)(2,1)S(1)}, bf16[32,128,128]{2,1,0:T(8,128)(2,1)S(1)}, bf16[128,8192]{1,0:T(8,128)(2,1)}, f32[8192,128]{1,0:T(8,128)}) custom-call(s32[8192]{0:T(1024)S(1)} %bitcast.95, s32[2]{0:T(128)S(1)} %pad_add_fusion.flags, ...), custom_call_target="tpu_custom_call", output_to_operand_aliasing={{0}: (7, {}), {1}: (8, {}), {2}: (9, {}), {3}: (10, {})} | custom-call | tf_op jit(solution)/shard_map/back_three_late/pallas_call | solution.py:483
  112.7 25.1 %back_two_one.1 = (bf16[32,128,128]{2,1,0:T(8,128)(2,1)S(1)}, bf16[32,128,128]{2,1,0:T(8,128)(2,1)}, bf16[32,128,128]{2,1,0:T(8,128)(2,1)S(1)}, bf16[32,128,128]{2,1,0:T(8,128)(2,1)}, bf16[8192,128]{1,0:T(8,128)(2,1)}) custom-call(s32[8192]{0:T(1024)S(1)} %bitcast.96, s32[2]{0:T(128)S(1)} %pad_add_fusion.flags, f32[8192,128]{1,0:T(8,128)} %get-tuple-element.84.gc_t, ...), custom_call_target="tpu_custom_call" | custom-call | tf_op jit(solution)/shard_map/back_two_one/pallas_call | solution.py:496
  139.4 2.5 %add_convert_fusion.6 = (bf16[4,1,4,128,128]{4,3,2,1,0:T(8,128)(2,1)}, bf16[4,1,4,128,128]{4,3,2,1,0:T(8,128)(2,1)}) fusion(bf16[4,2,4,128,128]{4,3,2,1,0:T(8,128)(2,1)} %bitcast.6, s32[]{:T(128)S(6)} %select_n.68, bf16[4,2,4,128,128]{4,3,2,1,0:T(8,128)(2,1)S(1)} %bitcast.88, s32[]{:T(128)S(6)} %select_n.67), kind=kLoop, calls=%fused_computation.7 | loop fusion | flops 2097152 | bytes 3145736 | tf_op jit(solution)/shard_map/convert_element_type | solution.py:345
  141.9 7.8 %back_zero.1 = (bf16[32,144,128]{2,1,0:T(8,128)(2,1)S(1)}, bf16[32,144,128]{2,1,0:T(8,128)(2,1)}, f32[128,8192]{1,0:T(8,128)}, f32[128,128]{1,0:T(8,128)S(1)}) custom-call(s32[2]{0:T(128)S(1)} %pad_add_fusion.flags, bf16[8192,128]{1,0:T(8,128)(2,1)} %get-tuple-element.99.ga_t, bf16[128,8192]{1,0:T(8,128)(2,1)} %bitcast.106, ...), custom_call_target="tpu_custom_call" | custom-call | tf_op jit(solution)/shard_map/back_zero/pallas_call | solution.py:513
  150.2 2.7 %collective-permute-start.8 = (bf16[16,128,128]{2,1,0:T(8,128)(2,1)}, bf16[16,128,128]{2,1,0:T(8,128)(2,1)}, u32[]{:S(2)}, u32[]{:S(2)}) collective-permute-start(bf16[16,128,128]{2,1,0:T(8,128)(2,1)} %bitcast.8), channel_id=1, source_target_pairs={{0,2},{1,3},{2,0},{3,1},{4,6},{5,7},{6,4},{7,5},{8,10},{9,11},{10,... | collective-permute-start | bytes 1572872 | tf_op jit(solution)/shard_map/ppermute | solution.py:329
  152.9 2.6 %add_convert_fusion.4 = (bf16[4,1,4,128,128]{4,3,2,1,0:T(8,128)(2,1)}, bf16[4,1,4,128,128]{4,3,2,1,0:T(8,128)(2,1)}) fusion(bf16[4,2,4,128,128]{4,3,2,1,0:T(8,128)(2,1)} %bitcast.10, s32[]{:T(128)S(6)} %select_n.68, bf16[4,2,4,128,128]{4,3,2,1,0:T(8,128)(2,1)S(1)} %bitcast.91, s32[]{:T(128)S(6)} %select_n.67), kind=kLoop, calls=%fused_computation.5 | loop fusion | flops 2097152 | bytes 3145736 | tf_op jit(solution)/shard_map/convert_element_type | solution.py:345
  155.4 2.6 %add_convert_fusion.2 = (bf16[2,1,8,128,128]{4,3,2,1,0:T(8,128)(2,1)}, bf16[2,1,8,128,128]{4,3,2,1,0:T(8,128)(2,1)}) fusion(bf16[2,2,8,128,128]{4,3,2,1,0:T(8,128)(2,1)} %bitcast.14, s32[]{:T(128)S(6)} %select_n.70, bf16[2,2,8,128,128]{4,3,2,1,0:T(8,128)(2,1)S(1)} %bitcast.90, s32[]{:T(128)S(6)} %select_n.69), kind=kLoop, calls=%fused_computation.3 | loop fusion | flops 2097152 | bytes 3145736 | tf_op jit(solution)/shard_map/convert_element_type | solution.py:345
  158.1 2.1 collective-permute-start.6
  160.2 5.7 %collective-permute-done.8 = bf16[16,128,128]{2,1,0:T(8,128)(2,1)} collective-permute-done((bf16[16,128,128]{2,1,0:T(8,128)(2,1)}, bf16[16,128,128]{2,1,0:T(8,128)(2,1)}, u32[]{:S(2)}, u32[]{:S(2)}) %collective-permute-start.8) | collective-permute-done | bytes 524320 | tf_op jit(solution)/shard_map/ppermute | solution.py:329
  165.9 2.0 add_convert_fusion.14
  167.9 2.7 %add_convert_fusion = (bf16[4,1,4,144,128]{4,3,2,1,0:T(8,128)(2,1)}, bf16[4,1,4,144,128]{4,3,2,1,0:T(8,128)(2,1)}) fusion(bf16[4,2,4,144,128]{4,3,2,1,0:T(8,128)(2,1)} %bitcast.18, s32[]{:T(128)S(6)} %select_n.68, bf16[4,2,4,144,128]{4,3,2,1,0:T(8,128)(2,1)S(1)} %bitcast.89, s32[]{:T(128)S(6)} %select_n.67), kind=kLoop, calls=%fused_computation | loop fusion | flops 2359296 | bytes 3538952 | tf_op jit(solution)/shard_map/convert_element_type | solution.py:345
  170.6 2.2 %collective-permute-start.9 = (bf16[8,128,128]{2,1,0:T(8,128)(2,1)}, bf16[8,128,128]{2,1,0:T(8,128)(2,1)S(1)}, u32[]{:S(2)}, u32[]{:S(2)}) collective-permute-start(bf16[8,128,128]{2,1,0:T(8,128)(2,1)} %bitcast.24), channel_id=1, source_target_pairs={{0,4},{1,5},{2,6},{3,7},{4,0},{5,1},{6,2},{7,3},{8,12},{9,13},{10,... | collective-permute-start | bytes 786440 | tf_op jit(solution)/shard_map/ppermute | solution.py:329
  172.8 1.5 collective-permute-start.10
  174.3 6.1 %back_last.1 = bf16[128,8192]{1,0:T(8,128)(2,1)} custom-call(bf16[128,8192]{1,0:T(8,128)(2,1)S(1)} %copy-done.1, f32[128,8192]{1,0:T(8,128)} %get-tuple-element.126.gn, bf16[128,8192]{1,0:T(8,128)(2,1)} %bitcast.107, f32[128,128]{1,0:T(8,128)S(1)} %get-tuple-element.100.scale, f32[1,8192]{1,0:T(1,128)S(1)} %copy-done.7, f32[128,128]{1,0:T(8,128)S(1)} %get-tuple-element.127.inner), custom_call_target="tpu_custom_call" | custom-call | tf_op jit(solution)/shard_map/back_last/pallas_call | solution.py:536
  180.4 2.7 %collective-permute-start.17 = (bf16[4,128,128]{2,1,0:T(8,128)(2,1)S(1)}, bf16[4,128,128]{2,1,0:T(8,128)(2,1)S(1)}, u32[]{:S(2)}, u32[]{:S(2)}) collective-permute-start(bf16[4,128,128]{2,1,0:T(8,128)(2,1)S(1)} %fusion.10), channel_id=1, source_target_pairs={{0,8},{1,9},{2,10},{3,11},{4,12},{5,13},{6,14},{7,15},{8,0},{9,1},... | collective-permute-start | bytes 393224 | tf_op jit(solution)/shard_map/ppermute | solution.py:329
  187.8 3.7 %collective-permute-done.13 = bf16[8,128,128]{2,1,0:T(8,128)(2,1)S(1)} collective-permute-done((bf16[8,128,128]{2,1,0:T(8,128)(2,1)S(1)}, bf16[8,128,128]{2,1,0:T(8,128)(2,1)S(1)}, u32[]{:S(2)}, u32[]{:S(2)}) %collective-permute-start.13) | collective-permute-done | bytes 262176 | tf_op jit(solution)/shard_map/ppermute | solution.py:329
  194.8 2.9 %collective-permute-start.16 = (bf16[4,128,128]{2,1,0:T(8,128)(2,1)S(1)}, bf16[4,128,128]{2,1,0:T(8,128)(2,1)S(1)}, u32[]{:S(2)}, u32[]{:S(2)}) collective-permute-start(bf16[4,128,128]{2,1,0:T(8,128)(2,1)S(1)} %fusion.14), channel_id=1, source_target_pairs={{0,8},{1,9},{2,10},{3,11},{4,12},{5,13},{6,14},{7,15},{8,0},{9,1},... | collective-permute-start | bytes 393224 | tf_op jit(solution)/shard_map/ppermute | solution.py:329
  197.7 1.7 collective-permute-done.14
  199.5 5.0 %collective-permute-done.11 = bf16[8,144,128]{2,1,0:T(8,128)(2,1)S(1)} collective-permute-done((bf16[8,144,128]{2,1,0:T(8,128)(2,1)S(1)}, bf16[8,144,128]{2,1,0:T(8,128)(2,1)S(1)}, u32[]{:S(2)}, u32[]{:S(2)}) %collective-permute-start.11) | collective-permute-done | bytes 294944 | tf_op jit(solution)/shard_map/ppermute | solution.py:329
  204.7 6.7 %collective-permute-done.12 = bf16[4,144,128]{2,1,0:T(8,128)(2,1)S(1)} collective-permute-done((bf16[4,144,128]{2,1,0:T(8,128)(2,1)S(1)}, bf16[4,144,128]{2,1,0:T(8,128)(2,1)S(1)}, u32[]{:S(2)}, u32[]{:S(2)}) %collective-permute-start.12) | collective-permute-done | bytes 147488 | tf_op jit(solution)/shard_map/ppermute | solution.py:329
  (67 shorter events, 18.7 us)
Async XLA Ops:
  49.1 39.6 %collective-permute-start = (bf16[128,6144]{1,0:T(8,128)(2,1)}, bf16[128,6144]{1,0:T(8,128)(2,1)S(1)}, u32[]{:S(2)}, u32[]{:S(2)}) collective-permute-start(bf16[128,6144]{1,0:T(8,128)(2,1)} %get-tuple-element.70), channel_id=1, source_target_pairs={{16,0},{17,1},{18,2},{19,3},{20,4},{21,5},{22,6},{23,7},{24,8},{25... | collective-permute-start | bytes 4718600 | tf_op jit(solution)/shard_map/ppermute | solution.py:451
  50.4 53.8 %collective-permute-start.1 = (bf16[128,2048]{1,0:T(8,128)(2,1)}, bf16[128,2048]{1,0:T(8,128)(2,1)S(1)}, u32[]{:S(2)}, u32[]{:S(2)}) collective-permute-start(bf16[128,2048]{1,0:T(8,128)(2,1)} %get-tuple-element.76), channel_id=1, source_target_pairs={{16,0},{17,1},{18,2},{19,3},{20,4},{21,5},{22,6},{23,7},{24,8},{25... | collective-permute-start | bytes 1572872 | tf_op jit(solution)/shard_map/ppermute | solution.py:451
  51.8 36.9 %copy-start.5 = (s32[1,8192]{1,0:T(1,128)S(1)}, s32[1,8192]{1,0:T(1,128)}, u32[]{:S(2)}) copy-start(s32[1,8192]{1,0:T(1,128)} %param.11) | copy-start | bytes 98308
  112.7 26.1 %collective-permute-start.2 = (bf16[32,128,128]{2,1,0:T(8,128)(2,1)S(1)}, bf16[32,128,128]{2,1,0:T(8,128)(2,1)}, u32[]{:S(2)}, u32[]{:S(2)}) collective-permute-start(bf16[32,128,128]{2,1,0:T(8,128)(2,1)S(1)} %get-tuple-element.83), channel_id=1, source_target_pairs={{0,1},{1,0},{2,3},{3,2},{4,5},{5,4},{6,7},{7,6},{8,9},{9,8},{10,11... | collective-permute-start | bytes 3145736 | tf_op jit(solution)/shard_map/ppermute | solution.py:329
  138.8 10.9 %collective-permute-start.3 = (bf16[32,128,128]{2,1,0:T(8,128)(2,1)}, bf16[32,128,128]{2,1,0:T(8,128)(2,1)}, u32[]{:S(2)}, u32[]{:S(2)}) collective-permute-start(bf16[32,128,128]{2,1,0:T(8,128)(2,1)} %get-tuple-element.93), channel_id=1, source_target_pairs={{0,1},{1,0},{2,3},{3,2},{4,5},{5,4},{6,7},{7,6},{8,9},{9,8},{10,11... | collective-permute-start | bytes 3145736 | tf_op jit(solution)/shard_map/ppermute | solution.py:329
  139.3 10.4 %collective-permute-start.4 = (bf16[32,128,128]{2,1,0:T(8,128)(2,1)}, bf16[32,128,128]{2,1,0:T(8,128)(2,1)}, u32[]{:S(2)}, u32[]{:S(2)}) collective-permute-start(bf16[32,128,128]{2,1,0:T(8,128)(2,1)} %get-tuple-element.95), channel_id=1, source_target_pairs={{0,1},{1,0},{2,3},{3,2},{4,5},{5,4},{6,7},{7,6},{8,9},{9,8},{10,11... | collective-permute-start | bytes 3145736 | tf_op jit(solution)/shard_map/ppermute | solution.py:329
  141.9 10.9 %copy-start.3 = (bf16[32,128,128]{2,1,0:T(8,128)(2,1)S(1)}, bf16[32,128,128]{2,1,0:T(8,128)(2,1)}, u32[]{:S(2)}) copy-start(bf16[32,128,128]{2,1,0:T(8,128)(2,1)} %copy-done.2) | copy-start | bytes 3145732
  149.7 16.2 %collective-permute-start.7 = (bf16[32,144,128]{2,1,0:T(8,128)(2,1)}, bf16[32,144,128]{2,1,0:T(8,128)(2,1)}, u32[]{:S(2)}, u32[]{:S(2)}) collective-permute-start(bf16[32,144,128]{2,1,0:T(8,128)(2,1)} %get-tuple-element.114), channel_id=1, source_target_pairs={{0,1},{1,0},{2,3},{3,2},{4,5},{5,4},{6,7},{7,6},{8,9},{9,8},{10,11... | collective-permute-start | bytes 3538952 | tf_op jit(solution)/shard_map/ppermute | solution.py:329
  150.2 15.7 %collective-permute-start.8 = (bf16[16,128,128]{2,1,0:T(8,128)(2,1)}, bf16[16,128,128]{2,1,0:T(8,128)(2,1)}, u32[]{:S(2)}, u32[]{:S(2)}) collective-permute-start(bf16[16,128,128]{2,1,0:T(8,128)(2,1)} %bitcast.8), channel_id=1, source_target_pairs={{0,2},{1,3},{2,0},{3,1},{4,6},{5,7},{6,4},{7,5},{8,10},{9,11},{10,... | collective-permute-start | bytes 1572872 | tf_op jit(solution)/shard_map/ppermute | solution.py:329
  155.4 10.5 %copy-start.11 = (bf16[4,1,4,128,128]{4,3,2,1,0:T(8,128)(2,1)S(1)}, bf16[4,1,4,128,128]{4,3,2,1,0:T(8,128)(2,1)}, u32[]{:S(2)}) copy-start(bf16[4,1,4,128,128]{4,3,2,1,0:T(8,128)(2,1)} %get-tuple-element.144) | copy-start | bytes 1572868
  158.1 22.3 %collective-permute-start.5 = (bf16[16,128,128]{2,1,0:T(8,128)(2,1)}, bf16[16,128,128]{2,1,0:T(8,128)(2,1)}, u32[]{:S(2)}, u32[]{:S(2)}) collective-permute-start(bf16[16,128,128]{2,1,0:T(8,128)(2,1)} %bitcast.12), channel_id=1, source_target_pairs={{0,2},{1,3},{2,0},{3,1},{4,6},{5,7},{6,4},{7,5},{8,10},{9,11},{10,... | collective-permute-start | bytes 1572872 | tf_op jit(solution)/shard_map/ppermute | solution.py:329
  158.1 22.3 %collective-permute-start.6 = (bf16[16,128,128]{2,1,0:T(8,128)(2,1)}, bf16[16,128,128]{2,1,0:T(8,128)(2,1)}, u32[]{:S(2)}, u32[]{:S(2)}) collective-permute-start(bf16[16,128,128]{2,1,0:T(8,128)(2,1)} %bitcast.16), channel_id=1, source_target_pairs={{0,4},{1,5},{2,6},{3,7},{4,0},{5,1},{6,2},{7,3},{8,12},{9,13},{10,... | collective-permute-start | bytes 1572872 | tf_op jit(solution)/shard_map/ppermute | solution.py:329
  167.9 6.4 %copy-start.1 = (bf16[128,8192]{1,0:T(8,128)(2,1)S(1)}, bf16[128,8192]{1,0:T(8,128)(2,1)}, u32[]{:S(2)}) copy-start(bf16[128,8192]{1,0:T(8,128)(2,1)} %get-tuple-element.125.gy) | copy-start | bytes 6291460
  170.6 9.7 %collective-permute-start.9 = (bf16[8,128,128]{2,1,0:T(8,128)(2,1)}, bf16[8,128,128]{2,1,0:T(8,128)(2,1)S(1)}, u32[]{:S(2)}, u32[]{:S(2)}) collective-permute-start(bf16[8,128,128]{2,1,0:T(8,128)(2,1)} %bitcast.24), channel_id=1, source_target_pairs={{0,4},{1,5},{2,6},{3,7},{4,0},{5,1},{6,2},{7,3},{8,12},{9,13},{10,... | collective-permute-start | bytes 786440 | tf_op jit(solution)/shard_map/ppermute | solution.py:329
  172.8 19.2 %collective-permute-start.10 = (bf16[16,144,128]{2,1,0:T(8,128)(2,1)}, bf16[16,144,128]{2,1,0:T(8,128)(2,1)S(1)}, u32[]{:S(2)}, u32[]{:S(2)}) collective-permute-start(bf16[16,144,128]{2,1,0:T(8,128)(2,1)} %bitcast.116), channel_id=1, source_target_pairs={{0,2},{1,3},{2,0},{3,1},{4,6},{5,7},{6,4},{7,5},{8,10},{9,11},{10,... | collective-permute-start | bytes 1769480 | tf_op jit(solution)/shard_map/ppermute | solution.py:329
  174.3 8.8 %copy-start.10 = (bf16[4,1,4,128,128]{4,3,2,1,0:T(8,128)(2,1)S(1)}, bf16[4,1,4,128,128]{4,3,2,1,0:T(8,128)(2,1)}, u32[]{:S(2)}) copy-start(bf16[4,1,4,128,128]{4,3,2,1,0:T(8,128)(2,1)} %get-tuple-element.142) | copy-start | bytes 1572868
  180.4 7.4 %collective-permute-start.17 = (bf16[4,128,128]{2,1,0:T(8,128)(2,1)S(1)}, bf16[4,128,128]{2,1,0:T(8,128)(2,1)S(1)}, u32[]{:S(2)}, u32[]{:S(2)}) collective-permute-start(bf16[4,128,128]{2,1,0:T(8,128)(2,1)S(1)} %fusion.10), channel_id=1, source_target_pairs={{0,8},{1,9},{2,10},{3,11},{4,12},{5,13},{6,14},{7,15},{8,0},{9,1},... | collective-permute-start | bytes 393224 | tf_op jit(solution)/shard_map/ppermute | solution.py:329
  183.1 8.9 %copy-start.8 = (bf16[4,1,4,144,128]{4,3,2,1,0:T(8,128)(2,1)S(1)}, bf16[4,1,4,144,128]{4,3,2,1,0:T(8,128)(2,1)}, u32[]{:S(2)}) copy-start(bf16[4,1,4,144,128]{4,3,2,1,0:T(8,128)(2,1)} %get-tuple-element.138) | copy-start | bytes 1769476
  184.3 7.2 %collective-permute-start.13 = (bf16[8,128,128]{2,1,0:T(8,128)(2,1)S(1)}, bf16[8,128,128]{2,1,0:T(8,128)(2,1)S(1)}, u32[]{:S(2)}, u32[]{:S(2)}) collective-permute-start(bf16[8,128,128]{2,1,0:T(8,128)(2,1)S(1)} %bitcast.127), channel_id=1, source_target_pairs={{0,4},{1,5},{2,6},{3,7},{4,0},{5,1},{6,2},{7,3},{8,12},{9,13},{10,... | collective-permute-start | bytes 786440 | tf_op jit(solution)/shard_map/ppermute | solution.py:329
  186.0 8.7 %collective-permute-start.15 = (bf16[8,128,128]{2,1,0:T(8,128)(2,1)S(1)}, bf16[8,128,128]{2,1,0:T(8,128)(2,1)S(1)}, u32[]{:S(2)}, u32[]{:S(2)}) collective-permute-start(bf16[8,128,128]{2,1,0:T(8,128)(2,1)S(1)} %bitcast.126), channel_id=1, source_target_pairs={{0,2},{1,3},{2,0},{3,1},{4,6},{5,7},{6,4},{7,5},{8,10},{9,11},{10,... | collective-permute-start | bytes 786440 | tf_op jit(solution)/shard_map/ppermute | solution.py:329
  191.6 7.9 %collective-permute-start.14 = (bf16[4,128,128]{2,1,0:T(8,128)(2,1)S(1)}, bf16[4,128,128]{2,1,0:T(8,128)(2,1)S(1)}, u32[]{:S(2)}, u32[]{:S(2)}) collective-permute-start(bf16[4,128,128]{2,1,0:T(8,128)(2,1)S(1)} %fusion.12), channel_id=1, source_target_pairs={{0,8},{1,9},{2,10},{3,11},{4,12},{5,13},{6,14},{7,15},{8,0},{9,1},... | collective-permute-start | bytes 393224 | tf_op jit(solution)/shard_map/ppermute | solution.py:329
  192.1 12.3 %collective-permute-start.11 = (bf16[8,144,128]{2,1,0:T(8,128)(2,1)S(1)}, bf16[8,144,128]{2,1,0:T(8,128)(2,1)S(1)}, u32[]{:S(2)}, u32[]{:S(2)}) collective-permute-start(bf16[8,144,128]{2,1,0:T(8,128)(2,1)S(1)} %bitcast.119), channel_id=1, source_target_pairs={{0,4},{1,5},{2,6},{3,7},{4,0},{5,1},{6,2},{7,3},{8,12},{9,13},{10,... | collective-permute-start | bytes 884744 | tf_op jit(solution)/shard_map/ppermute | solution.py:329
  194.8 9.9 %collective-permute-start.16 = (bf16[4,128,128]{2,1,0:T(8,128)(2,1)S(1)}, bf16[4,128,128]{2,1,0:T(8,128)(2,1)S(1)}, u32[]{:S(2)}, u32[]{:S(2)}) collective-permute-start(bf16[4,128,128]{2,1,0:T(8,128)(2,1)S(1)} %fusion.14), channel_id=1, source_target_pairs={{0,8},{1,9},{2,10},{3,11},{4,12},{5,13},{6,14},{7,15},{8,0},{9,1},... | collective-permute-start | bytes 393224 | tf_op jit(solution)/shard_map/ppermute | solution.py:329
  204.5 6.9 %collective-permute-start.12 = (bf16[4,144,128]{2,1,0:T(8,128)(2,1)S(1)}, bf16[4,144,128]{2,1,0:T(8,128)(2,1)S(1)}, u32[]{:S(2)}, u32[]{:S(2)}) collective-permute-start(bf16[4,144,128]{2,1,0:T(8,128)(2,1)S(1)} %fusion.8), channel_id=1, source_target_pairs={{0,8},{1,9},{2,10},{3,11},{4,12},{5,13},{6,14},{7,15},{8,0},{9,1},... | collective-permute-start | bytes 442376 | tf_op jit(solution)/shard_map/ppermute | solution.py:329
  (7 other events, 17.6 us)

commit v5 on v4

--- a/solution.py
+++ b/solution.py
@@ -51,7 +51,7 @@
 
 
 def at_block(k, bs):
-    return pl.ds(pl.multiple_of(k * bs, bs), bs)
+    return pl.ds(k * bs, bs) if isinstance(k, int) else pl.ds(pl.multiple_of(k * bs, bs), bs)
 
 
 def rounded(v):
@@ -77,19 +77,11 @@
         scatter_rows(perm, (first + k) * bs, source, target, bs)
 
     even[...] = make(0)
-
-    def pair(i, carry):
-        k = 2 * i
-        odd[...] = make(k + 1)
-        move(k, even)
-        even[...] = make(k + 2)
-        move(k + 1, odd)
-        return carry
-
-    lax.fori_loop(0, STEP // 2 - 1, pair, 0)
-    odd[...] = make(STEP - 1)
-    move(STEP - 2, even)
-    move(STEP - 1, odd)
+    for k in range(STEP):
+        now, then = (even, odd) if k % 2 == 0 else (odd, even)
+        if k + 1 < STEP:
+            then[...] = make(k + 1)
+        move(k, now)
 
 
 def gathered_scattered(make, perm, first, source, target, even_in, odd_in, even_out, odd_out, bs):
@@ -99,30 +91,16 @@
     def move(k, out):
         scatter_rows(perm, (first + k) * bs, out, target, bs)
 
-    fetch(0, even_in)
-    fetch(1, odd_in)
-    even_out[...] = make(0, even_in)
-
-    def pair(i, carry):
-        k = 2 * i
-        odd_out[...] = make(k + 1, odd_in)
-        fetch(k + 2, even_in)
-        move(k, even_out)
-        even_out[...] = make(k + 2, even_in)
-        fetch(k + 3, odd_in)
-        move(k + 1, odd_out)
-        return carry
-
-    lax.fori_loop(0, STEP // 2 - 1, pair, 0)
-    odd_out[...] = make(STEP - 1, odd_in)
-    move(STEP - 2, even_out)
-    move(STEP - 1, odd_out)
-
-
-def put_split(stage, flags, own, k, value):
-    device = lax.div(k, own)
-    goes = lax.bitwise_xor(lax.bitwise_and(device, 1), flags[0])
-    stage[goes, lax.div(device, 2) * own + lax.rem(k, own)] = value.astype(BF16)
+    for k in range(STEP):
+        into, out = (even_in, even_out) if k % 2 == 0 else (odd_in, odd_out)
+        fetch(k, into)
+        out[...] = make(k, into)
+        move(k, out)
+
+
+def gelu_parts(pre):
+    cdf = 0.5 * (1.0 + lax.erf(pre * inv_sqrt_two))
+    return (pre * cdf).astype(BF16), cdf + pre * jnp.exp(-0.5 * pre * pre) * inv_sqrt_two_pi
 
 
 def seeded_block(cot, live, cols):
@@ -134,7 +112,7 @@
 
 
 def first_pass(
-    perm, x, cot, live, gamma, fac_a, fac_b, ap_t, h_t, slope_t, scale, grad_a, grad_b, a_t, gc_t, ga_t, gn, acc, r0, r1, r2, r3
+    perm, x, cot, live, gamma, fac_a, fac_b, ap_t, scale, grad_a, grad_b, a_t, gc_t, ga_t, gn, acc, r0, r1, r2, r3
 ):
     phase, c = pl.program_id(0), pl.program_id(1)
     bs = fac_a.shape[2]
@@ -167,11 +145,7 @@
             here = at_block(k, bs)
             ap = rows[...].astype(BF16)
             ap_t[here, :] = ap
-            pre = dot(fac_a[0, k], ap, 0, 0)
-            cdf = 0.5 * (1.0 + lax.erf(pre * inv_sqrt_two))
-            h_t[here, :] = (pre * cdf).astype(BF16)
-            slope = cdf + pre * jnp.exp(-0.5 * pre * pre) * inv_sqrt_two_pi
-            slope_t[here, :] = slope
+            _, slope = gelu_parts(dot(fac_a[0, k], ap, 0, 0))
             gh = dot(fac_b[0, k], gc_t[at_block(c * STEP + k, bs), :].astype(BF16), 1, 0)
             return rounded(dot(fac_a[0, k], (gh * slope).astype(BF16), 1, 0))
 
@@ -206,17 +180,17 @@
     pl.when(jnp.logical_and(phase == 3, c == last))(lambda: emit(grad_b))
 
 
-def forward_second(perm, h_t, fac, cp_t, c_t, rows):
+def forward_second(perm, ap_t, fac_one, fac_two, cp_t, c_t, rows):
     phase, c = pl.program_id(0), pl.program_id(1)
-    bs = fac.shape[2]
+    bs = fac_two.shape[2]
 
     @pl.when(phase == 0)
     def _():
-        each_block(
-            lambda k, u: c_t.__setitem__(
-                (at_block(c * STEP + k, bs), slice(None)), rounded(dot(fac[0, k], h_t[at_block(k, bs), :], 0, 0))
-            )
-        )
+        def one(k, u):
+            h, _ = gelu_parts(dot(fac_one[0, k], ap_t[at_block(k, bs), :], 0, 0))
+            c_t[at_block(c * STEP + k, bs), :] = rounded(dot(fac_two[0, k], h, 0, 0))
+
+        each_block(one)
 
     @pl.when(phase == 1)
     def _():
@@ -236,8 +210,9 @@
 
 
 def back_three(own, skipped, perm, flags, cot, live, moved, cp_t, fac, *refs):
-    *given, keep, send, gy_out, gc_t, stage, even, odd = refs
+    *given, keep, send, gy_out, gc_t, even, odd = refs
     bs = fac.shape[2]
+    outs = (keep, send)
     if given:
         gc_t[...] = given[3][...]
 
@@ -245,32 +220,39 @@
         here = at_block(k, bs)
         gy = jnp.where(flags[1] == 1, seeded_block(cot, live, here), moved[:, here])
         gy_out[:, here] = gy
-        put_split(stage, flags, own, k, dot(cp_t[here, :], gy, 1, 0))
         return rounded(dot(fac[0, k], gy, 1, 1))
 
+    def grads(goes, k, block):
+        at = at_block(block, bs)
+        outs[goes][k] = dot(cp_t[at, :], gy_out[:, at], 1, 0).astype(BF16)
+
     scattered(make, perm, (pl.program_id(0) + skipped) * STEP, gc_t, even, odd, bs)
-    keep[...] = stage[0]
-    send[...] = stage[1]
+    each_split(flags, own, grads)
 
 
 def back_two_one(
-    own, perm, flags, gc_t, h_t, ap_t, slope_t, fac_two, fac_one, keep_two, send_two, keep_one, send_one, ga_out, ga_t, twos, ones, even, odd
+    own, perm, flags, gc_t, ap_t, fac_two, fac_one, keep_two, send_two, keep_one, send_one, ga_out, ga_t, h_t, gpre_t, gc_b, even, odd
 ):
     c = pl.program_id(0)
     bs = fac_two.shape[2]
+    twos, ones = (keep_two, send_two), (keep_one, send_one)
 
     def make(k):
         here = at_block(k, bs)
+        h_t[here, :], slope = gelu_parts(dot(fac_one[0, k], ap_t[here, :], 0, 0))
         gc = gc_t[here, :].astype(BF16)
-        gh = dot(fac_two[0, k], gc, 1, 0)
-        gpre = (gh * slope_t[here, :]).astype(BF16)
-        put_split(twos, flags, own, k, dot(h_t[here, :], gc, 1, 1))
-        put_split(ones, flags, own, k, dot(ap_t[here, :], gpre, 1, 1))
+        gc_b[here, :] = gc
+        gpre = (dot(fac_two[0, k], gc, 1, 0) * slope).astype(BF16)
+        gpre_t[here, :] = gpre
         return rounded(dot(fac_one[0, k], gpre, 1, 0))
 
+    def grads(goes, k, block):
+        at = at_block(block, bs)
+        twos[goes][k] = dot(h_t[at, :], gc_b[at, :], 1, 1).astype(BF16)
+        ones[goes][k] = dot(ap_t[at, :], gpre_t[at, :], 1, 1).astype(BF16)
+
     scattered(make, perm, c * STEP, ga_t, even, odd, bs)
-    keep_two[...], send_two[...] = twos[0], twos[1]
-    keep_one[...], send_one[...] = ones[0], ones[1]
+    each_split(flags, own, grads)
 
     @pl.when(c == pl.num_programs(0) - 1)
     def _():
@@ -406,7 +388,7 @@
     big = pltpu.VMEM((width, tokens), F32)
     rows = pltpu.VMEM((UNROLL, bs, tokens), F32)
     block = pltpu.VMEM((bs, tokens), F32)
-    stage = pltpu.VMEM((2, STEP // 2, bs, bs), BF16)
+    part_t = pltpu.VMEM(chunk, BF16)
     part = (steps - 1) * STEP * bs
     last = steps - 1
 
@@ -424,7 +406,7 @@
     b_which, b_at = pick((3, 2, 2)), phased(None, None, last, last)
     cot_at, out_at, mid_at = phased(None, last, last, None), phased(0, 0, 0, None), phased(0, None, last, last)
     mid = pl.BlockSpec(chunk, lambda ph, c, *_: (mid_at(ph, c), 0))
-    ap_t, h_t, slope_t, scale, *grad_x = call(
+    ap_t, scale, *grad_x = call(
         first_pass,
         "first_pass",
         (4, steps),
@@ -436,11 +418,9 @@
             pl.BlockSpec(fblock, lambda ph, c, *_: (a_which(ph), a_at(ph, c), 0, 0)),
             pl.BlockSpec(fblock, lambda ph, c, *_: (b_which(ph), b_at(ph, c), 0, 0)),
         ],
-        [mid, mid, mid, sca, pl.BlockSpec(wide, lambda ph, c, *_: (0, jnp.minimum(out_at(ph, c), last - 1))), whole(*wide)],
+        [mid, sca, pl.BlockSpec(wide, lambda ph, c, *_: (0, jnp.minimum(out_at(ph, c), last - 1))), whole(*wide)],
         [
             feat(BF16),
-            feat(BF16),
-            feat(F32),
             small,
             jax.ShapeDtypeStruct((tokens, part), BF16),
             jax.ShapeDtypeStruct(wide, BF16),
@@ -457,16 +437,17 @@
         (2, steps),
         [
             pl.BlockSpec(chunk, lambda ph, c, *_: (early(ph, c), 0)),
+            pl.BlockSpec(fblock, lambda ph, c, *_: (1, early(ph, c), 0, 0)),
             pl.BlockSpec(fblock, lambda ph, c, *_: (2, early(ph, c), 0, 0)),
         ],
         pl.BlockSpec(chunk, lambda ph, c, *_: (rest(ph, c), 0)),
         feat(BF16),
         [big, rows],
-    )(perm, h_t, fac)
+    )(perm, ap_t, fac, fac)
 
     start = lambda keep, send, order: Halving(keep, send, order, own, me, replicas)
     shapes = [half(), half(), row(BF16), feat(F32)]
-    scratch = [stage, block, block]
+    scratch = [block, block]
     partial = call(
         functools.partial(back_three, own, 0),
         "back_three_early",
@@ -497,12 +478,12 @@
         functools.partial(back_two_one, own),
         "back_two_one",
         (steps,),
-        [c_at, c_at, c_at, c_at, f_at(2), f_at(1)],
+        [c_at, c_at, f_at(2), f_at(1)],
         [half_at] * 4 + [whole(width, tokens)],
         [half()] * 4 + [feat(BF16)],
-        [big, stage, stage, block, block],
+        [big, part_t, part_t, part_t, block, block],
         prefetch=2,
-    )(perm, flags, gc_t, h_t, ap_t, slope_t, fac, fac)
+    )(perm, flags, gc_t, ap_t, fac, fac)
     two, one = start(keep_two, send_two, other), start(keep_one, send_one, bits)
     ga_t, one.keep, one.send, two.keep, two.send = met(three, then=[ga_t, one.keep, one.send, two.keep, two.send])
     three.add()
@@ -520,19 +501,16 @@
         [pltpu.VMEM((tokens, bs), F32)],
     )(flags, ga_t, x, scale, gamma, fac)
     zero = start(keep_zero, send_zero, bits)
-    gn, zero.keep, zero.send = met(one, two, then=[gn, zero.keep, zero.send])
+    gn, zero.keep, zero.send = met(one, two, three, then=[gn, zero.keep, zero.send])
     zero.go()
-    one.add()
-    two.add()
-    (gn,) = met(one, two, then=[gn])
-    one.go()
-    two.go()
-    (gn,) = met(zero, three, then=[gn])
+    for each in (one, two, three):
+        each.add()
+    (gn,) = met(zero, one, two, three, then=[gn])
+    for each in (one, two, three):
+        each.go()
     zero.add()
-    three.add()
-    (gn,) = met(zero, three, then=[gn])
+    (gn,) = met(zero, then=[gn])
     zero.go()
-    three.go()
     out_grad = call(
         back_last,
         "back_last",

time: 214 us -> 205 us (0.958)
  Pallas kernels: 122 us -> 107 us
  waiting for transfers between devices: 47.6 us -> 53.5 us
    ppermute x16, waiting for transfers between devices: 25.1 us -> 32.5 us  [go(): lax.ppermute(self.send, 'dp', [(i, i ^ 1 << bit) for i in range(self.repl...]
    pallas_call x1, Pallas kernels: 25.1 us -> 19.1 us  [on_device(): call(functools.partial(back_two_one, own), 'back_two_one', (steps,), [c_a...]
    pallas_call x1, Pallas kernels: 46.2 us -> 40.8 us  [on_device(): call(first_pass, 'first_pass', (4, steps), [tok, pl.BlockSpec(wide, lambd...]
    pallas_call x1, Pallas kernels: 15.4 us -> 10.9 us  [on_device(): call(functools.partial(back_three, own, 0), 'back_three_early', (steps -...]
  transfers between devices with their start and end apart: 18 -> 18, of which waited for: 8 -> 7; matrix products, arithmetic and copies ran while one was open for 7% -> 8% of each run, Pallas kernels for 32% -> 28%
where the time goes in v5:
time: 205 us; the launch traced here: 204 us
  Pallas kernels  107 us (52%)
  waiting for transfers between devices  53.5 us (26%)
  starting transfers between devices  19.9 us (10%)
  other arithmetic  19 us (9%)
  local copies, waits for them, and re-layouts  4.55 us (2%)
    pallas_call x1, Pallas kernels, on_device(): call(first_pass, 'first_pass', (4, steps), [tok, pl.BlockSpec(wide, lambd...  40.8 us
    ppermute x16, waiting for transfers between devices, go(): lax.ppermute(self.send, 'dp', [(i, i ^ 1 << bit) for i in range(self.repl...  32.5 us
    ppermute x2, waiting for transfers between devices, on_device(): lax.ppermute(piece, 'section', [(i, i - 1) for i in range(1, sections)])  21 us
    pallas_call x1, Pallas kernels, on_device(): call(functools.partial(back_two_one, own), 'back_two_one', (steps,), [c_a...  19.1 us
    ppermute x16, starting transfers between devices, go(): lax.ppermute(self.send, 'dp', [(i, i ^ 1 << bit) for i in range(self.repl...  17.2 us
    convert_element_type x9, other arithmetic, part(): total = (a.astype(F32) + b.astype(F32)).astype(self.keep.dtype)  15.9 us
    pallas_call x1, Pallas kernels, on_device(): call(forward_second, 'forward_second', (2, steps), [pl.BlockSpec(chunk, l...  14.4 us
    pallas_call x1, Pallas kernels, on_device(): call(functools.partial(back_three, own, 0), 'back_three_early', (steps -...  10.9 us
  transfers between devices with their start and end apart: 18, of which 7 were waited for; matrix products, arithmetic and copies ran while one was open for 8% of the time, Pallas kernels for 28%

profile of v5, /device:TPU:0, one launch (start us, length us, event | category | flops | bytes accessed | tf_op | source)
XLA Modules:
  0.0 204.4 jit_solution(421310037208429527)
XLA Ops:
  2.9 40.8 %first_pass.1 = (bf16[8192,128]{1,0:T(8,128)(2,1)}, f32[128,128]{1,0:T(8,128)S(1)}, bf16[128,6144]{1,0:T(8,128)(2,1)}, bf16[128,2048]{1,0:T(8,128)(2,1)}) custom-call(s32[8192]{0:T(1024)S(1)} %bitcast.92, bf16[128,8192]{1,0:T(8,128)(2,1)} %bitcast.106, bf16[128,8192]{1,0:T(8,128)(2,1)} %cot.5, f32[128,128]{1,0:T(8,128)S(1)} %broadcast_in_dim.12.live, ...), custom_call_target="tpu_custom_call" | custom-call | tf_op jit(solution)/shard_map/first_pass/pallas_call | solution.py:409
  46.5 14.4 %forward_second.1.cp_t = bf16[8192,128]{1,0:T(8,128)(2,1)S(1)} custom-call(s32[8192]{0:T(1024)S(1)} %bitcast.93, bf16[8192,128]{1,0:T(8,128)(2,1)} %get-tuple-element.68.ap_t, bf16[4,64,128,128]{3,2,1,0:T(8,128)(2,1)} %bitcast.99, bf16[4,64,128,128]{3,2,1,0:T(8,128)(2,1)} %bitcast.100), custom_call_target="tpu_custom_call" | custom-call | tf_op jit(solution)/shard_map/forward_second/pallas_call | solution.py:434
  62.3 21.0 %collective-permute-done.moved = bf16[128,6144]{1,0:T(8,128)(2,1)S(1)} collective-permute-done((bf16[128,6144]{1,0:T(8,128)(2,1)}, bf16[128,6144]{1,0:T(8,128)(2,1)S(1)}, u32[]{:S(2)}, u32[]{:S(2)}) %collective-permute-start) | collective-permute-done | bytes 1572896 | tf_op jit(solution)/shard_map/ppermute | solution.py:431
  83.3 10.9 %back_three_early.1 = (bf16[32,128,128]{2,1,0:T(8,128)(2,1)S(1)}, bf16[32,128,128]{2,1,0:T(8,128)(2,1)S(1)}, bf16[128,8192]{1,0:T(8,128)(2,1)}, f32[8192,128]{1,0:T(8,128)}) custom-call(s32[8192]{0:T(1024)S(1)} %bitcast.94, s32[2]{0:T(128)S(1)} %pad_add_fusion.flags, bf16[128,8192]{1,0:T(8,128)(2,1)} %cot.5, f32[128,128]{1,0:T(8,128)S(1)} %broadcast_in_dim.12.live, ...), custom_call_target="tpu_custom_call" | custom-call | tf_op jit(solution)/shard_map/back_three_early/pallas_call | solution.py:451
  94.2 7.7 %back_three_late.1 = (bf16[32,128,128]{2,1,0:T(8,128)(2,1)S(1)}, bf16[32,128,128]{2,1,0:T(8,128)(2,1)S(1)}, bf16[128,8192]{1,0:T(8,128)(2,1)}, f32[8192,128]{1,0:T(8,128)}) custom-call(s32[8192]{0:T(1024)S(1)} %bitcast.95, s32[2]{0:T(128)S(1)} %pad_add_fusion.flags, ...), custom_call_target="tpu_custom_call", output_to_operand_aliasing={{0}: (7, {}), {1}: (8, {}), {2}: (9, {}), {3}: (10, {})} | custom-call | tf_op jit(solution)/shard_map/back_three_late/pallas_call | solution.py:464
  101.9 19.1 %back_two_one.1 = (bf16[32,128,128]{2,1,0:T(8,128)(2,1)S(1)}, bf16[32,128,128]{2,1,0:T(8,128)(2,1)}, bf16[32,128,128]{2,1,0:T(8,128)(2,1)S(1)}, bf16[32,128,128]{2,1,0:T(8,128)(2,1)}, bf16[8192,128]{1,0:T(8,128)(2,1)}) custom-call(s32[8192]{0:T(1024)S(1)} %bitcast.96, s32[2]{0:T(128)S(1)} %pad_add_fusion.flags, f32[8192,128]{1,0:T(8,128)} %get-tuple-element.81.gc_t, ...), custom_call_target="tpu_custom_call" | custom-call | tf_op jit(solution)/shard_map/back_two_one/pallas_call | solution.py:477
  122.5 2.4 %add_convert_fusion.6 = (bf16[4,1,4,128,128]{4,3,2,1,0:T(8,128)(2,1)S(1)}, bf16[4,1,4,128,128]{4,3,2,1,0:T(8,128)(2,1)}) fusion(bf16[4,2,4,128,128]{4,3,2,1,0:T(8,128)(2,1)} %bitcast.6, s32[]{:T(128)S(6)} %select_n.68, bf16[4,2,4,128,128]{4,3,2,1,0:T(8,128)(2,1)S(1)} %bitcast.88, s32[]{:T(128)S(6)} %select_n.67), kind=kLoop, calls=%fused_computation.7 | loop fusion | flops 2097152 | bytes 3145736 | tf_op jit(solution)/shard_map/convert_element_type | solution.py:327
  124.9 2.7 %collective-permute-start.5 = (bf16[16,128,128]{2,1,0:T(8,128)(2,1)S(1)}, bf16[16,128,128]{2,1,0:T(8,128)(2,1)}, u32[]{:S(2)}, u32[]{:S(2)}) collective-permute-start(bf16[16,128,128]{2,1,0:T(8,128)(2,1)S(1)} %bitcast.117), channel_id=1, source_target_pairs={{0,2},{1,3},{2,0},{3,1},{4,6},{5,7},{6,4},{7,5},{8,10},{9,11},{10,... | collective-permute-start | bytes 1572872 | tf_op jit(solution)/shard_map/ppermute | solution.py:311
  127.6 7.8 %back_zero.1 = (bf16[32,144,128]{2,1,0:T(8,128)(2,1)S(1)}, bf16[32,144,128]{2,1,0:T(8,128)(2,1)}, f32[128,8192]{1,0:T(8,128)}, f32[128,128]{1,0:T(8,128)S(1)}) custom-call(s32[2]{0:T(128)S(1)} %pad_add_fusion.flags, bf16[8192,128]{1,0:T(8,128)(2,1)} %get-tuple-element.96.ga_t, bf16[128,8192]{1,0:T(8,128)(2,1)} %bitcast.107, ...), custom_call_target="tpu_custom_call" | custom-call | tf_op jit(solution)/shard_map/back_zero/pallas_call | solution.py:494
  135.4 4.9 %collective-permute-done.5 = bf16[16,128,128]{2,1,0:T(8,128)(2,1)} collective-permute-done((bf16[16,128,128]{2,1,0:T(8,128)(2,1)S(1)}, bf16[16,128,128]{2,1,0:T(8,128)(2,1)}, u32[]{:S(2)}, u32[]{:S(2)}) %collective-permute-start.5) | collective-permute-done | bytes 524320 | tf_op jit(solution)/shard_map/ppermute | solution.py:311
  140.3 2.2 %add_convert_fusion.14 = (bf16[2,1,4,128,128]{4,3,2,0,1:T(8,128)(2,1)}, bf16[2,1,4,128,128]{4,3,2,0,1:T(8,128)(2,1)}) fusion(bf16[2,2,4,128,128]{4,3,2,1,0:T(8,128)(2,1)} %bitcast.18, s32[]{:T(128)S(6)} %select_n.70, bf16[2,2,4,128,128]{4,3,2,1,0:T(8,128)(2,1)} %bitcast.113, s32[]{:T(128)S(6)} %select_n.69), kind=kLoop, calls=%fused_computation.15 | loop fusion | flops 1048576 | bytes 1572872 | tf_op jit(solution)/shard_map/convert_element_type | solution.py:327
  142.5 2.6 %add_convert_fusion.2 = (bf16[2,1,8,128,128]{4,3,2,1,0:T(8,128)(2,1)}, bf16[2,1,8,128,128]{4,3,2,1,0:T(8,128)(2,1)}) fusion(bf16[2,2,8,128,128]{4,3,2,1,0:T(8,128)(2,1)} %bitcast.14, s32[]{:T(128)S(6)} %select_n.70, bf16[2,2,8,128,128]{4,3,2,1,0:T(8,128)(2,1)S(1)} %bitcast.91, s32[]{:T(128)S(6)} %select_n.69), kind=kLoop, calls=%fused_computation.3 | loop fusion | flops 2097152 | bytes 3145736 | tf_op jit(solution)/shard_map/convert_element_type | solution.py:327
  145.0 2.6 %add_convert_fusion.4 = (bf16[4,1,4,128,128]{4,3,2,1,0:T(8,128)(2,1)}, bf16[4,1,4,128,128]{4,3,2,1,0:T(8,128)(2,1)}) fusion(bf16[4,2,4,128,128]{4,3,2,1,0:T(8,128)(2,1)} %bitcast.10, s32[]{:T(128)S(6)} %select_n.68, bf16[4,2,4,128,128]{4,3,2,1,0:T(8,128)(2,1)S(1)} %bitcast.90, s32[]{:T(128)S(6)} %select_n.67), kind=kLoop, calls=%fused_computation.5 | loop fusion | flops 2097152 | bytes 3145736 | tf_op jit(solution)/shard_map/convert_element_type | solution.py:327
  147.6 1.7 collective-permute-start.7
  151.4 2.7 %add_convert_fusion = (bf16[4,1,4,144,128]{4,3,2,1,0:T(8,128)(2,1)}, bf16[4,1,4,144,128]{4,3,2,1,0:T(8,128)(2,1)}) fusion(bf16[4,2,4,144,128]{4,3,2,1,0:T(8,128)(2,1)} %bitcast.22, s32[]{:T(128)S(6)} %select_n.68, bf16[4,2,4,144,128]{4,3,2,1,0:T(8,128)(2,1)S(1)} %bitcast.89, s32[]{:T(128)S(6)} %select_n.67), kind=kLoop, calls=%fused_computation | loop fusion | flops 2359296 | bytes 3538952 | tf_op jit(solution)/shard_map/convert_element_type | solution.py:327
  154.4 6.0 %back_last.1 = bf16[128,8192]{1,0:T(8,128)(2,1)} custom-call(bf16[128,8192]{1,0:T(8,128)(2,1)S(1)} %copy-done.1, f32[128,8192]{1,0:T(8,128)} %get-tuple-element.120.gn, bf16[128,8192]{1,0:T(8,128)(2,1)} %bitcast.108, f32[128,128]{1,0:T(8,128)S(1)} %get-tuple-element.97.scale, f32[1,8192]{1,0:T(1,128)S(1)} %copy-done.7, f32[128,128]{1,0:T(8,128)S(1)} %get-tuple-element.121.inner), custom_call_target="tpu_custom_call" | custom-call | tf_op jit(solution)/shard_map/back_last/pallas_call | solution.py:514
  160.3 9.0 %collective-permute-done.9 = bf16[8,128,128]{2,1,0:T(8,128)(2,1)} collective-permute-done((bf16[8,128,128]{2,1,0:T(8,128)(2,1)}, bf16[8,128,128]{2,1,0:T(8,128)(2,1)}, u32[]{:S(2)}, u32[]{:S(2)}) %collective-permute-start.9) | collective-permute-done | bytes 262176 | tf_op jit(solution)/shard_map/ppermute | solution.py:311
  170.6 1.6 collective-permute-start.13
  173.2 2.6 %collective-permute-start.17 = (bf16[4,128,128]{2,1,0:T(8,128)(2,1)S(1)}, bf16[4,128,128]{2,1,0:T(8,128)(2,1)S(1)}, u32[]{:S(2)}, u32[]{:S(2)}) collective-permute-start(bf16[4,128,128]{2,1,0:T(8,128)(2,1)S(1)} %fusion.10), channel_id=1, source_target_pairs={{0,8},{1,9},{2,10},{3,11},{4,12},{5,13},{6,14},{7,15},{8,0},{9,1},... | collective-permute-start | bytes 393224 | tf_op jit(solution)/shard_map/ppermute | solution.py:311
  178.3 3.5 %collective-permute-done.17 = bf16[4,128,128]{2,1,0:T(8,128)(2,1)S(1)} collective-permute-done((bf16[4,128,128]{2,1,0:T(8,128)(2,1)S(1)}, bf16[4,128,128]{2,1,0:T(8,128)(2,1)S(1)}, u32[]{:S(2)}, u32[]{:S(2)}) %collective-permute-start.17) | collective-permute-done | bytes 131104 | tf_op jit(solution)/shard_map/ppermute | solution.py:311
  182.8 3.4 %collective-permute-start.14 = (bf16[4,128,128]{2,1,0:T(8,128)(2,1)S(1)}, bf16[4,128,128]{2,1,0:T(8,128)(2,1)S(1)}, u32[]{:S(2)}, u32[]{:S(2)}) collective-permute-start(bf16[4,128,128]{2,1,0:T(8,128)(2,1)S(1)} %fusion.12), channel_id=1, source_target_pairs={{0,8},{1,9},{2,10},{3,11},{4,12},{5,13},{6,14},{7,15},{8,0},{9,1},... | collective-permute-start | bytes 393224 | tf_op jit(solution)/shard_map/ppermute | solution.py:311
  186.4 5.4 %collective-permute-done.11 = bf16[8,144,128]{2,1,0:T(8,128)(2,1)S(1)} collective-permute-done((bf16[8,144,128]{2,1,0:T(8,128)(2,1)S(1)}, bf16[8,144,128]{2,1,0:T(8,128)(2,1)S(1)}, u32[]{:S(2)}, u32[]{:S(2)}) %collective-permute-start.11) | collective-permute-done | bytes 294944 | tf_op jit(solution)/shard_map/ppermute | solution.py:311
  192.9 7.8 %collective-permute-done.16 = bf16[4,128,128]{2,1,0:T(8,128)(2,1)S(1)} collective-permute-done((bf16[4,128,128]{2,1,0:T(8,128)(2,1)S(1)}, bf16[4,128,128]{2,1,0:T(8,128)(2,1)S(1)}, u32[]{:S(2)}, u32[]{:S(2)}) %collective-permute-start.16) | collective-permute-done | bytes 131104 | tf_op jit(solution)/shard_map/ppermute | solution.py:311
  200.7 1.9 collective-permute-done.12
  (65 shorter events, 18.9 us)
Async XLA Ops:
  43.7 39.6 %collective-permute-start = (bf16[128,6144]{1,0:T(8,128)(2,1)}, bf16[128,6144]{1,0:T(8,128)(2,1)S(1)}, u32[]{:S(2)}, u32[]{:S(2)}) collective-permute-start(bf16[128,6144]{1,0:T(8,128)(2,1)} %get-tuple-element.67), channel_id=1, source_target_pairs={{16,0},{17,1},{18,2},{19,3},{20,4},{21,5},{22,6},{23,7},{24,8},{25... | collective-permute-start | bytes 4718600 | tf_op jit(solution)/shard_map/ppermute | solution.py:431
  45.0 49.2 %collective-permute-start.1 = (bf16[128,2048]{1,0:T(8,128)(2,1)}, bf16[128,2048]{1,0:T(8,128)(2,1)S(1)}, u32[]{:S(2)}, u32[]{:S(2)}) collective-permute-start(bf16[128,2048]{1,0:T(8,128)(2,1)} %get-tuple-element.73), channel_id=1, source_target_pairs={{16,0},{17,1},{18,2},{19,3},{20,4},{21,5},{22,6},{23,7},{24,8},{25... | collective-permute-start | bytes 1572872 | tf_op jit(solution)/shard_map/ppermute | solution.py:431
  46.5 36.9 %copy-start.5 = (s32[1,8192]{1,0:T(1,128)S(1)}, s32[1,8192]{1,0:T(1,128)}, u32[]{:S(2)}) copy-start(s32[1,8192]{1,0:T(1,128)} %param.11) | copy-start | bytes 98308
  101.9 20.1 %collective-permute-start.2 = (bf16[32,128,128]{2,1,0:T(8,128)(2,1)S(1)}, bf16[32,128,128]{2,1,0:T(8,128)(2,1)}, u32[]{:S(2)}, u32[]{:S(2)}) collective-permute-start(bf16[32,128,128]{2,1,0:T(8,128)(2,1)S(1)} %get-tuple-element.80), channel_id=1, source_target_pairs={{0,1},{1,0},{2,3},{3,2},{4,5},{5,4},{6,7},{7,6},{8,9},{9,8},{10,11... | collective-permute-start | bytes 3145736 | tf_op jit(solution)/shard_map/ppermute | solution.py:311
  122.0 18.3 %collective-permute-start.3 = (bf16[32,128,128]{2,1,0:T(8,128)(2,1)}, bf16[32,128,128]{2,1,0:T(8,128)(2,1)}, u32[]{:S(2)}, u32[]{:S(2)}) collective-permute-start(bf16[32,128,128]{2,1,0:T(8,128)(2,1)} %get-tuple-element.88), channel_id=1, source_target_pairs={{0,1},{1,0},{2,3},{3,2},{4,5},{5,4},{6,7},{7,6},{8,9},{9,8},{10,11... | collective-permute-start | bytes 3145736 | tf_op jit(solution)/shard_map/ppermute | solution.py:311
  122.5 17.8 %collective-permute-start.4 = (bf16[32,128,128]{2,1,0:T(8,128)(2,1)}, bf16[32,128,128]{2,1,0:T(8,128)(2,1)}, u32[]{:S(2)}, u32[]{:S(2)}) collective-permute-start(bf16[32,128,128]{2,1,0:T(8,128)(2,1)} %get-tuple-element.90), channel_id=1, source_target_pairs={{0,1},{1,0},{2,3},{3,2},{4,5},{5,4},{6,7},{7,6},{8,9},{9,8},{10,11... | collective-permute-start | bytes 3145736 | tf_op jit(solution)/shard_map/ppermute | solution.py:311
  124.9 15.4 %collective-permute-start.5 = (bf16[16,128,128]{2,1,0:T(8,128)(2,1)S(1)}, bf16[16,128,128]{2,1,0:T(8,128)(2,1)}, u32[]{:S(2)}, u32[]{:S(2)}) collective-permute-start(bf16[16,128,128]{2,1,0:T(8,128)(2,1)S(1)} %bitcast.117), channel_id=1, source_target_pairs={{0,2},{1,3},{2,0},{3,1},{4,6},{5,7},{6,4},{7,5},{8,10},{9,11},{10,... | collective-permute-start | bytes 1572872 | tf_op jit(solution)/shard_map/ppermute | solution.py:311
  135.4 7.1 %copy-start.3 = (bf16[32,128,128]{2,1,0:T(8,128)(2,1)S(1)}, bf16[32,128,128]{2,1,0:T(8,128)(2,1)}, u32[]{:S(2)}) copy-start(bf16[32,128,128]{2,1,0:T(8,128)(2,1)} %copy-done.2) | copy-start | bytes 3145732
  140.3 7.3 %collective-permute-start.6 = (bf16[32,144,128]{2,1,0:T(8,128)(2,1)}, bf16[32,144,128]{2,1,0:T(8,128)(2,1)}, u32[]{:S(2)}, u32[]{:S(2)}) collective-permute-start(bf16[32,144,128]{2,1,0:T(8,128)(2,1)} %get-tuple-element.102), channel_id=1, source_target_pairs={{0,1},{1,0},{2,3},{3,2},{4,5},{5,4},{6,7},{7,6},{8,9},{9,8},{10,11... | collective-permute-start | bytes 3538952 | tf_op jit(solution)/shard_map/ppermute | solution.py:311
  147.6 21.7 %collective-permute-start.7 = (bf16[16,128,128]{2,1,0:T(8,128)(2,1)}, bf16[16,128,128]{2,1,0:T(8,128)(2,1)}, u32[]{:S(2)}, u32[]{:S(2)}) collective-permute-start(bf16[16,128,128]{2,1,0:T(8,128)(2,1)} %bitcast.12), channel_id=1, source_target_pairs={{0,2},{1,3},{2,0},{3,1},{4,6},{5,7},{6,4},{7,5},{8,10},{9,11},{10,... | collective-permute-start | bytes 1572872 | tf_op jit(solution)/shard_map/ppermute | solution.py:311
  149.3 20.0 %collective-permute-start.8 = (bf16[16,128,128]{2,1,0:T(8,128)(2,1)}, bf16[16,128,128]{2,1,0:T(8,128)(2,1)}, u32[]{:S(2)}, u32[]{:S(2)}) collective-permute-start(bf16[16,128,128]{2,1,0:T(8,128)(2,1)} %bitcast.16), channel_id=1, source_target_pairs={{0,4},{1,5},{2,6},{3,7},{4,0},{5,1},{6,2},{7,3},{8,12},{9,13},{10,... | collective-permute-start | bytes 1572872 | tf_op jit(solution)/shard_map/ppermute | solution.py:311
  150.9 18.4 %collective-permute-start.9 = (bf16[8,128,128]{2,1,0:T(8,128)(2,1)}, bf16[8,128,128]{2,1,0:T(8,128)(2,1)}, u32[]{:S(2)}, u32[]{:S(2)}) collective-permute-start(bf16[8,128,128]{2,1,0:T(8,128)(2,1)} %bitcast.20), channel_id=1, source_target_pairs={{0,4},{1,5},{2,6},{3,7},{4,0},{5,1},{6,2},{7,3},{8,12},{9,13},{10,... | collective-permute-start | bytes 786440 | tf_op jit(solution)/shard_map/ppermute | solution.py:311
  154.1 23.5 %collective-permute-start.10 = (bf16[16,144,128]{2,1,0:T(8,128)(2,1)}, bf16[16,144,128]{2,1,0:T(8,128)(2,1)S(1)}, u32[]{:S(2)}, u32[]{:S(2)}) collective-permute-start(bf16[16,144,128]{2,1,0:T(8,128)(2,1)} %bitcast.24), channel_id=1, source_target_pairs={{0,2},{1,3},{2,0},{3,1},{4,6},{5,7},{6,4},{7,5},{8,10},{9,11},{10,... | collective-permute-start | bytes 1769480 | tf_op jit(solution)/shard_map/ppermute | solution.py:311
  154.4 14.9 %copy-start.10 = (bf16[4,1,4,128,128]{4,3,2,1,0:T(8,128)(2,1)S(1)}, bf16[4,1,4,128,128]{4,3,2,1,0:T(8,128)(2,1)}, u32[]{:S(2)}) copy-start(bf16[4,1,4,128,128]{4,3,2,1,0:T(8,128)(2,1)} %get-tuple-element.136) | copy-start | bytes 1572868
  160.3 11.9 %copy-start.11 = (bf16[2,1,4,128,128]{4,3,2,0,1:T(8,128)(2,1)S(1)}, bf16[2,1,4,128,128]{4,3,2,0,1:T(8,128)(2,1)}, u32[]{:S(2)}) copy-start(bf16[2,1,4,128,128]{4,3,2,0,1:T(8,128)(2,1)} %get-tuple-element.146) | copy-start | bytes 786436
  160.3 15.5 %copy-start.9 = (bf16[2,1,8,128,128]{4,3,2,1,0:T(8,128)(2,1)S(1)}, bf16[2,1,8,128,128]{4,3,2,1,0:T(8,128)(2,1)}, u32[]{:S(2)}) copy-start(bf16[2,1,8,128,128]{4,3,2,1,0:T(8,128)(2,1)} %get-tuple-element.134) | copy-start | bytes 1572868
  169.3 8.3 %copy-start.8 = (bf16[4,1,4,144,128]{4,3,2,1,0:T(8,128)(2,1)S(1)}, bf16[4,1,4,144,128]{4,3,2,1,0:T(8,128)(2,1)}, u32[]{:S(2)}) copy-start(bf16[4,1,4,144,128]{4,3,2,1,0:T(8,128)(2,1)} %get-tuple-element.132) | copy-start | bytes 1769476
  170.6 12.2 %collective-permute-start.13 = (bf16[8,128,128]{2,1,0:T(8,128)(2,1)S(1)}, bf16[8,128,128]{2,1,0:T(8,128)(2,1)S(1)}, u32[]{:S(2)}, u32[]{:S(2)}) collective-permute-start(bf16[8,128,128]{2,1,0:T(8,128)(2,1)S(1)} %bitcast.125), channel_id=1, source_target_pairs={{0,4},{1,5},{2,6},{3,7},{4,0},{5,1},{6,2},{7,3},{8,12},{9,13},{10,... | collective-permute-start | bytes 786440 | tf_op jit(solution)/shard_map/ppermute | solution.py:311
  173.2 8.6 %collective-permute-start.17 = (bf16[4,128,128]{2,1,0:T(8,128)(2,1)S(1)}, bf16[4,128,128]{2,1,0:T(8,128)(2,1)S(1)}, u32[]{:S(2)}, u32[]{:S(2)}) collective-permute-start(bf16[4,128,128]{2,1,0:T(8,128)(2,1)S(1)} %fusion.10), channel_id=1, source_target_pairs={{0,8},{1,9},{2,10},{3,11},{4,12},{5,13},{6,14},{7,15},{8,0},{9,1},... | collective-permute-start | bytes 393224 | tf_op jit(solution)/shard_map/ppermute | solution.py:311
  177.0 9.3 %collective-permute-start.15 = (bf16[8,128,128]{2,1,0:T(8,128)(2,1)S(1)}, bf16[8,128,128]{2,1,0:T(8,128)(2,1)S(1)}, u32[]{:S(2)}, u32[]{:S(2)}) collective-permute-start(bf16[8,128,128]{2,1,0:T(8,128)(2,1)S(1)} %bitcast.126), channel_id=1, source_target_pairs={{0,2},{1,3},{2,0},{3,1},{4,6},{5,7},{6,4},{7,5},{8,10},{9,11},{10,... | collective-permute-start | bytes 786440 | tf_op jit(solution)/shard_map/ppermute | solution.py:311
  177.8 14.0 %collective-permute-start.11 = (bf16[8,144,128]{2,1,0:T(8,128)(2,1)S(1)}, bf16[8,144,128]{2,1,0:T(8,128)(2,1)S(1)}, u32[]{:S(2)}, u32[]{:S(2)}) collective-permute-start(bf16[8,144,128]{2,1,0:T(8,128)(2,1)S(1)} %bitcast.120), channel_id=1, source_target_pairs={{0,4},{1,5},{2,6},{3,7},{4,0},{5,1},{6,2},{7,3},{8,12},{9,13},{10,... | collective-permute-start | bytes 884744 | tf_op jit(solution)/shard_map/ppermute | solution.py:311
  182.8 10.0 %collective-permute-start.14 = (bf16[4,128,128]{2,1,0:T(8,128)(2,1)S(1)}, bf16[4,128,128]{2,1,0:T(8,128)(2,1)S(1)}, u32[]{:S(2)}, u32[]{:S(2)}) collective-permute-start(bf16[4,128,128]{2,1,0:T(8,128)(2,1)S(1)} %fusion.12), channel_id=1, source_target_pairs={{0,8},{1,9},{2,10},{3,11},{4,12},{5,13},{6,14},{7,15},{8,0},{9,1},... | collective-permute-start | bytes 393224 | tf_op jit(solution)/shard_map/ppermute | solution.py:311
  186.3 14.4 %collective-permute-start.16 = (bf16[4,128,128]{2,1,0:T(8,128)(2,1)S(1)}, bf16[4,128,128]{2,1,0:T(8,128)(2,1)S(1)}, u32[]{:S(2)}, u32[]{:S(2)}) collective-permute-start(bf16[4,128,128]{2,1,0:T(8,128)(2,1)S(1)} %fusion.14), channel_id=1, source_target_pairs={{0,8},{1,9},{2,10},{3,11},{4,12},{5,13},{6,14},{7,15},{8,0},{9,1},... | collective-permute-start | bytes 393224 | tf_op jit(solution)/shard_map/ppermute | solution.py:311
  191.8 10.8 %collective-permute-start.12 = (bf16[4,144,128]{2,1,0:T(8,128)(2,1)S(1)}, bf16[4,144,128]{2,1,0:T(8,128)(2,1)S(1)}, u32[]{:S(2)}, u32[]{:S(2)}) collective-permute-start(bf16[4,144,128]{2,1,0:T(8,128)(2,1)S(1)} %fusion.8), channel_id=1, source_target_pairs={{0,8},{1,9},{2,10},{3,11},{4,12},{5,13},{6,14},{7,15},{8,0},{9,1},... | collective-permute-start | bytes 442376 | tf_op jit(solution)/shard_map/ppermute | solution.py:311
  (6 other events, 11.9 us)

commit v6 on v5

--- a/solution.py
+++ b/solution.py
@@ -259,43 +259,41 @@
         ga_out[...] = ga_t[...].astype(BF16)
 
 
-def back_zero(own, flags, ga_t, x, scale, gamma, fac, keep, send, gn, inner, acc):
-    c = pl.program_id(0)
+def back_zero(own, flags, ga_t, gy, x, scale, gamma, fac, keep, send, grad_x, gn, acc):
+    phase, c = pl.program_id(0), pl.program_id(1)
     bs = fac.shape[2]
     outs = (keep, send)
 
-    @pl.when(c == 0)
+    @pl.when(jnp.logical_and(phase == 0, c == 0))
     def _():
         acc[...] = jnp.zeros(acc.shape, F32)
 
-    def one(goes, k, block):
-        at = at_block(block, bs)
-        z = zed_block(x, scale, at)
-        zg = z * gamma[:, at]
-        outs[goes][k, pl.ds(0, bs), :] = dot(zg.astype(BF16), ga_t[at, :], 0, 1).astype(BF16)
-        value = dot(ga_t[at, :], fac[0, block], 0, 1)
-        gn[:, at] = value
-        total = jnp.sum(value * z, axis=0, keepdims=True)
-        outs[goes][k, pl.ds(bs, EXTRA), :] = jnp.broadcast_to(total, (EXTRA, bs)).astype(BF16)
-        acc[...] += value * zg
-
-    each_split(flags, own, one)
-
-    @pl.when(c == pl.num_programs(0) - 1)
-    def _():
-        mean = jnp.sum(acc[...], axis=1, keepdims=True) / (x.shape[1] * pl.num_programs(0))
-        inner[...] = jnp.broadcast_to(mean, inner.shape)
-
-
-def back_last(gy, gn, x, scale, gamma, inner, grad_x):
-    bs = scale.shape[1]
-
-    def one(k, u):
-        cols = at_block(k, bs)
-        z = zed_block(x, scale, cols)
-        grad_x[:, cols] = gradient(gy[:, cols], gn[:, cols], gamma[:, cols], z, scale, inner)
-
-    each_block(one, unroll=4)
+    @pl.when(phase == 0)
+    def _():
+        def one(goes, k, block):
+            at = at_block(block, bs)
+            z = zed_block(x, scale, at)
+            zg = z * gamma[:, at]
+            outs[goes][k, pl.ds(0, bs), :] = dot(zg.astype(BF16), ga_t[at, :], 0, 1).astype(BF16)
+            value = dot(ga_t[at, :], fac[0, block], 0, 1)
+            gn[:, at_block(c * STEP + block, bs)] = value
+            total = jnp.sum(value * z, axis=0, keepdims=True)
+            outs[goes][k, pl.ds(bs, EXTRA), :] = jnp.broadcast_to(total, (EXTRA, bs)).astype(BF16)
+            acc[...] += value * zg
+
+        each_split(flags, own, one)
+
+    @pl.when(jnp.logical_and(phase == 0, c == pl.num_programs(1) - 1))
+    def _():
+        mean = jnp.sum(acc[...], axis=1, keepdims=True) / gn.shape[1]
+        acc[...] = jnp.broadcast_to(mean, acc.shape)
+
+    @pl.when(phase == 1)
+    def _():
+        for k in range(STEP):
+            cols = at_block(k, bs)
+            z = zed_block(x, scale, cols)
+            grad_x[:, cols] = gradient(gy[:, cols], gn[:, at_block(c * STEP + k, bs)], gamma[:, cols], z, scale, acc)
 
 
 class Halving:
@@ -350,6 +348,13 @@
         else:
             h.came = rest
     return then
+
+
+def behind(first, *others):
+    state = [(h.keep, h.came) for h in others]
+    first.keep, state = lax.optimization_barrier((first.keep, state))
+    for h, (keep, came) in zip(others, state):
+        h.keep, h.came = keep, came
 
 
 def on_device(replicas, sections, activations, cotangent, token_ids, gains, factors, monarch_perm):
@@ -426,7 +431,7 @@
             jax.ShapeDtypeStruct(wide, BF16),
         ],
         [big, big, big, pltpu.VMEM((tokens, width), F32), pltpu.VMEM((tokens, bs), F32)] + [block] * 4,
-        vmem=50,
+        vmem=60,
     )(perm, x, cotangent, live, gamma, fac, fac)
     moved = [lax.ppermute(piece, "section", [(i, i - 1) for i in range(1, sections)]) for piece in grad_x]
 
@@ -491,38 +496,35 @@
     one.go()
     two.go()
     three.go()
-    keep_zero, send_zero, gn, inner = call(
+    held_at = lambda shape, at, *lead: pl.BlockSpec(shape, lambda ph, c, *_: lead + (at(ph, c),) + (0,) * (len(shape) - 1 - len(lead)))
+    across = lambda shape, at: pl.BlockSpec(shape, lambda ph, c, *_: (0, at(ph, c)))
+    both = phased(None, None)
+    keep_zero, send_zero, out_grad = call(
         functools.partial(back_zero, own),
         "back_zero",
-        (steps,),
-        [c_at, w_at, sca, g_at, f_at(0)],
-        [more_at, more_at, w_at, sca],
-        [half(EXTRA), half(EXTRA), row(F32), small],
-        [pltpu.VMEM((tokens, bs), F32)],
-    )(flags, ga_t, x, scale, gamma, fac)
+        (2, steps),
+        [
+            held_at(chunk, early),
+            across(wide, rest),
+            across(wide, both),
+            sca,
+            across((1, STEP * bs), both),
+            held_at(fblock, early, 0),
+        ],
+        [held_at(more_at.block_shape, early)] * 2 + [across(wide, rest)],
+        [half(EXTRA), half(EXTRA), row(BF16)],
+        [pltpu.VMEM((tokens, width), F32), pltpu.VMEM((tokens, bs), F32)],
+    )(flags, ga_t, gy, x, scale, gamma, fac)
     zero = start(keep_zero, send_zero, bits)
-    gn, zero.keep, zero.send = met(one, two, three, then=[gn, zero.keep, zero.send])
+    out_grad, zero.keep, zero.send = met(one, two, three, then=[out_grad, zero.keep, zero.send])
     zero.go()
-    for each in (one, two, three):
-        each.add()
-    (gn,) = met(zero, one, two, three, then=[gn])
-    for each in (one, two, three):
-        each.go()
-    zero.add()
-    (gn,) = met(zero, then=[gn])
-    zero.go()
-    out_grad = call(
-        back_last,
-        "back_last",
-        (steps,),
-        [w_at, w_at, w_at, sca, g_at, sca],
-        w_at,
-        row(BF16),
-        prefetch=0,
-    )(gy, gn, x, scale, gamma, inner)
-    (out_grad,) = met(one, two, three, then=[out_grad])
-    for each in (one, two, three):
-        each.add()
+    one.add().go()
+    zero.add().go()
+    two.add().go()
+    three.add().go()
+    one.add().go()
+    zero.add().go()
+    behind(zero, one, two)
     total = [each.finish() for each in (zero, one, two, three)]
     grad_gamma = total[0][:, bs, :].reshape(1, own * bs)
     total[0] = total[0][:, :bs, :]

time: 205 us -> 202 us (0.985)
  Pallas kernels: 107 us -> 104 us
  waiting for transfers between devices: 53.5 us -> 56.3 us
  other arithmetic: 19 us -> 16.5 us
    pallas_call x2 -> x1, Pallas kernels: 13.7 us -> 10.9 us  [on_device(): call(functools.partial(back_zero, own), 'back_zero', (2, steps), [held_at...]
    ppermute x16, waiting for transfers between devices: 32.5 us -> 35.3 us  [go(): lax.ppermute(self.send, 'dp', [(i, i ^ 1 << bit) for i in range(self.repl...]
    unnamed x24 -> x22, local copies, waits for them, and re-layouts: 3.88 us -> 1.41 us
    convert_element_type x9, other arithmetic: 15.9 us -> 13.5 us  [part(): total = (a.astype(F32) + b.astype(F32)).astype(self.keep.dtype)]
  transfers between devices with their start and end apart: 18 -> 18, of which waited for: 7 -> 9; matrix products, arithmetic and copies ran while one was open for 8% -> 7% of each run, Pallas kernels for 28% -> 27%
where the time goes in v6:
time: 202 us
  Pallas kernels  104 us (51%)
  waiting for transfers between devices  56.3 us (28%)
  starting transfers between devices  21.3 us (11%)
  other arithmetic  16.5 us (8%)
  local copies, waits for them, and re-layouts  2.72 us (1%)
    pallas_call x1, Pallas kernels, on_device(): call(first_pass, 'first_pass', (4, steps), [tok, pl.BlockSpec(wide, lambd...  41.2 us
    ppermute x16, waiting for transfers between devices, go(): lax.ppermute(self.send, 'dp', [(i, i ^ 1 << bit) for i in range(self.repl...  35.3 us
    ppermute x2, waiting for transfers between devices, on_device(): lax.ppermute(piece, 'section', [(i, i - 1) for i in range(1, sections)])  21 us
    pallas_call x1, Pallas kernels, on_device(): call(functools.partial(back_two_one, own), 'back_two_one', (steps,), [c_a...  19.2 us
    ppermute x16, starting transfers between devices, go(): lax.ppermute(self.send, 'dp', [(i, i ^ 1 << bit) for i in range(self.repl...  18.5 us
    pallas_call x1, Pallas kernels, on_device(): call(forward_second, 'forward_second', (2, steps), [pl.BlockSpec(chunk, l...  14.4 us
    convert_element_type x9, other arithmetic, part(): total = (a.astype(F32) + b.astype(F32)).astype(self.keep.dtype)  13.5 us
    pallas_call x1, Pallas kernels, on_device(): call(functools.partial(back_three, own, 0), 'back_three_early', (steps -...  10.9 us
  transfers between devices with their start and end apart: 18, of which 9 were waited for; matrix products, arithmetic and copies ran while one was open for 7% of the time, Pallas kernels for 27%

profile of v6, /device:TPU:0, one launch (start us, length us, event | category | flops | bytes accessed | tf_op | source)
XLA Modules:
  0.0 201.6 jit_solution(10309811185025097228)
XLA Ops:
  2.0 41.2 %first_pass.1 = (bf16[8192,128]{1,0:T(8,128)(2,1)}, f32[128,128]{1,0:T(8,128)}, bf16[128,6144]{1,0:T(8,128)(2,1)}, bf16[128,2048]{1,0:T(8,128)(2,1)}) custom-call(s32[8192]{0:T(1024)} %bitcast.84, bf16[128,8192]{1,0:T(8,128)(2,1)} %bitcast.98, bf16[128,8192]{1,0:T(8,128)(2,1)} %cot.5, f32[128,128]{1,0:T(8,128)} %broadcast_in_dim.12.live, f32[1,8192]{1,0:T(1,128)} %gamma.3, ...), custom_call_target="tpu_custom_call" | custom-call | tf_op jit(solution)/shard_map/first_pass/pallas_call | solution.py:414
  46.0 14.4 %forward_second.1.cp_t = bf16[8192,128]{1,0:T(8,128)(2,1)S(1)} custom-call(s32[8192]{0:T(1024)S(1)} %bitcast.85, bf16[8192,128]{1,0:T(8,128)(2,1)} %get-tuple-element.53.ap_t, bf16[4,64,128,128]{3,2,1,0:T(8,128)(2,1)} %bitcast.91, bf16[4,64,128,128]{3,2,1,0:T(8,128)(2,1)} %bitcast.92), custom_call_target="tpu_custom_call" | custom-call | tf_op jit(solution)/shard_map/forward_second/pallas_call | solution.py:439
  61.8 21.0 %collective-permute-done.moved = bf16[128,6144]{1,0:T(8,128)(2,1)S(1)} collective-permute-done((bf16[128,6144]{1,0:T(8,128)(2,1)}, bf16[128,6144]{1,0:T(8,128)(2,1)S(1)}, u32[]{:S(2)}, u32[]{:S(2)}) %collective-permute-start) | collective-permute-done | bytes 1572896 | tf_op jit(solution)/shard_map/ppermute | solution.py:436
  82.9 10.9 %back_three_early.1 = (bf16[32,128,128]{2,1,0:T(8,128)(2,1)S(1)}, bf16[32,128,128]{2,1,0:T(8,128)(2,1)S(1)}, bf16[128,8192]{1,0:T(8,128)(2,1)}, f32[8192,128]{1,0:T(8,128)}) custom-call(s32[8192]{0:T(1024)S(1)} %bitcast.86, s32[2]{0:T(128)S(1)} %pad_add_fusion.flags, bf16[128,8192]{1,0:T(8,128)(2,1)} %cot.5, f32[128,128]{1,0:T(8,128)S(1)} %copy-done.1, ...), custom_call_target="tpu_custom_call" | custom-call | tf_op jit(solution)/shard_map/back_three_early/pallas_call | solution.py:456
  93.8 7.7 %back_three_late.1 = (bf16[32,128,128]{2,1,0:T(8,128)(2,1)S(1)}, bf16[32,128,128]{2,1,0:T(8,128)(2,1)S(1)}, bf16[128,8192]{1,0:T(8,128)(2,1)}, f32[8192,128]{1,0:T(8,128)}) custom-call(s32[8192]{0:T(1024)S(1)} %bitcast.87, s32[2]{0:T(128)S(1)} %pad_add_fusion.flags, ...), custom_call_target="tpu_custom_call", output_to_operand_aliasing={{0}: (7, {}), {1}: (8, {}), {2}: (9, {}), {3}: (10, {})} | custom-call | tf_op jit(solution)/shard_map/back_three_late/pallas_call | solution.py:469
  101.4 19.2 %back_two_one.1 = (bf16[32,128,128]{2,1,0:T(8,128)(2,1)S(1)}, bf16[32,128,128]{2,1,0:T(8,128)(2,1)}, bf16[32,128,128]{2,1,0:T(8,128)(2,1)S(1)}, bf16[32,128,128]{2,1,0:T(8,128)(2,1)}, bf16[8192,128]{1,0:T(8,128)(2,1)}) custom-call(s32[8192]{0:T(1024)S(1)} %bitcast.88, s32[2]{0:T(128)S(1)} %pad_add_fusion.flags, f32[8192,128]{1,0:T(8,128)} %get-tuple-element.66.gc_t, ...), custom_call_target="tpu_custom_call" | custom-call | tf_op jit(solution)/shard_map/back_two_one/pallas_call | solution.py:482
  121.2 2.4 %add_convert_fusion.6 = (bf16[4,1,4,128,128]{4,3,2,1,0:T(8,128)(2,1)S(1)}, bf16[4,1,4,128,128]{4,3,2,1,0:T(8,128)(2,1)}) fusion(bf16[4,2,4,128,128]{4,3,2,1,0:T(8,128)(2,1)} %bitcast.6, s32[]{:T(128)S(6)} %select_n.68, bf16[4,2,4,128,128]{4,3,2,1,0:T(8,128)(2,1)S(1)} %bitcast.80, s32[]{:T(128)S(6)} %select_n.67), kind=kLoop, calls=%fused_computation.7 | loop fusion | flops 2097152 | bytes 3145736 | tf_op jit(solution)/shard_map/convert_element_type | solution.py:325
  123.6 2.6 %collective-permute-start.5 = (bf16[16,128,128]{2,1,0:T(8,128)(2,1)S(1)}, bf16[16,128,128]{2,1,0:T(8,128)(2,1)S(1)}, u32[]{:S(2)}, u32[]{:S(2)}) collective-permute-start(bf16[16,128,128]{2,1,0:T(8,128)(2,1)S(1)} %bitcast.111), channel_id=1, source_target_pairs={{0,2},{1,3},{2,0},{3,1},{4,6},{5,7},{6,4},{7,5},{8,10},{9,11},{10,... | collective-permute-start | bytes 1572872 | tf_op jit(solution)/shard_map/ppermute | solution.py:309
  126.3 10.9 %back_zero.1 = (bf16[32,144,128]{2,1,0:T(8,128)(2,1)S(1)}, bf16[32,144,128]{2,1,0:T(8,128)(2,1)}, bf16[128,8192]{1,0:T(8,128)(2,1)}) custom-call(s32[2]{0:T(128)S(1)} %pad_add_fusion.flags, bf16[8192,128]{1,0:T(8,128)(2,1)} %get-tuple-element.81.ga_t, bf16[128,8192]{1,0:T(8,128)(2,1)} %get-tuple-element.82.gy, bf16[128,8192]{1,0:T(8,128)(2,1)} %bitcast.99, ...), custom_call_target="tpu_custom_call" | custom-call | tf_op jit(solution)/shard_map/back_zero/pallas_call | solution.py:502
  137.1 1.7 collective-permute-done.5
  138.9 2.7 %add_convert_fusion.5 = (bf16[4,1,4,128,128]{4,3,2,1,0:T(8,128)(2,1)}, bf16[4,1,4,128,128]{4,3,2,1,0:T(8,128)(2,1)}) fusion(bf16[4,2,4,128,128]{4,3,2,1,0:T(8,128)(2,1)} %bitcast.17, s32[]{:T(128)S(6)} %select_n.67, bf16[4,2,4,128,128]{4,3,2,1,0:T(8,128)(2,1)S(1)} %bitcast.83, s32[]{:T(128)S(6)} %select_n.68), kind=kLoop, calls=%fused_computation.6 | loop fusion | flops 2097152 | bytes 3145736 | tf_op jit(solution)/shard_map/convert_element_type | solution.py:325
  141.6 1.8 collective-permute-start.8
  143.3 2.4 %add_convert_fusion.1 = (bf16[4,1,4,144,128]{4,3,2,1,0:T(8,128)(2,1)S(1)}, bf16[4,1,4,144,128]{4,3,2,1,0:T(8,128)(2,1)}) fusion(bf16[4,2,4,144,128]{4,3,2,1,0:T(8,128)(2,1)} %bitcast.11, s32[]{:T(128)S(6)} %select_n.67, bf16[4,2,4,144,128]{4,3,2,1,0:T(8,128)(2,1)S(1)} %bitcast.81, s32[]{:T(128)S(6)} %select_n.68), kind=kLoop, calls=%fused_computation.1 | loop fusion | flops 2359296 | bytes 3538952 | tf_op jit(solution)/shard_map/convert_element_type | solution.py:325
  146.2 2.5 %add_convert_fusion.2 = (bf16[2,1,8,128,128]{4,3,2,1,0:T(8,128)(2,1)}, bf16[2,1,8,128,128]{4,3,2,1,0:T(8,128)(2,1)S(1)}) fusion(bf16[2,2,8,128,128]{4,3,2,1,0:T(8,128)(2,1)} %bitcast.24, s32[]{:T(128)S(6)} %select_n.70, bf16[2,2,8,128,128]{4,3,2,1,0:T(8,128)(2,1)S(1)} %bitcast.82, s32[]{:T(128)S(6)} %select_n.69), kind=kLoop, calls=%fused_computation.3 | loop fusion | flops 2097152 | bytes 3145736 | tf_op jit(solution)/shard_map/convert_element_type | solution.py:325
  150.3 6.3 %collective-permute-done.8 = bf16[16,128,128]{2,1,0:T(8,128)(2,1)} collective-permute-done((bf16[16,128,128]{2,1,0:T(8,128)(2,1)}, bf16[16,128,128]{2,1,0:T(8,128)(2,1)}, u32[]{:S(2)}, u32[]{:S(2)}) %collective-permute-start.8) | collective-permute-done | bytes 524320 | tf_op jit(solution)/shard_map/ppermute | solution.py:309
  156.7 2.2 %add_convert_fusion.11 = (bf16[2,1,4,128,128]{4,3,2,1,0:T(8,128)(2,1)S(1)}, bf16[2,1,4,128,128]{4,3,2,1,0:T(8,128)(2,1)}, bf16[2,1,4,128,128]{4,3,2,1,0:T(8,128)(2,1)S(1)}, bf16[2,1,4,128,128]{4,3,2,1,0:T(8,128)(2,1)}) fusion(bf16[2,2,4,128,128]{4,3,2,1,0:T(8,128)(2,1)S(1)} %bitcast.109, s32[]{:T(128)S(6)} %select_n.69, ...), kind=kLoop, calls=%fused_computation.12 | loop fusion | flops 2097152 | bytes 3145736 | tf_op jit(solution)/shard_map/convert_element_type | solution.py:325
  158.9 1.8 collective-permute-start.16
  160.9 8.4 %collective-permute-done.16 = bf16[8,128,128]{2,1,0:T(8,128)(2,1)S(1)} collective-permute-done((bf16[8,128,128]{2,1,0:T(8,128)(2,1)}, bf16[8,128,128]{2,1,0:T(8,128)(2,1)S(1)}, u32[]{:S(2)}, u32[]{:S(2)}) %collective-permute-start.16) | collective-permute-done | bytes 262176 | tf_op jit(solution)/shard_map/ppermute | solution.py:309
  169.4 2.7 %collective-permute-start.17 = (bf16[4,128,128]{2,1,0:T(8,128)(2,1)S(1)}, bf16[4,128,128]{2,1,0:T(8,128)(2,1)S(1)}, u32[]{:S(2)}, u32[]{:S(2)}) collective-permute-start(bf16[4,128,128]{2,1,0:T(8,128)(2,1)S(1)} %fusion.14), channel_id=1, source_target_pairs={{0,8},{1,9},{2,10},{3,11},{4,12},{5,13},{6,14},{7,15},{8,0},{9,1},... | collective-permute-start | bytes 393224 | tf_op jit(solution)/shard_map/ppermute | solution.py:309
  172.3 4.5 %collective-permute-done.9 = bf16[8,128,128]{2,1,0:T(8,128)(2,1)} collective-permute-done((bf16[8,128,128]{2,1,0:T(8,128)(2,1)}, bf16[8,128,128]{2,1,0:T(8,128)(2,1)}, u32[]{:S(2)}, u32[]{:S(2)}) %collective-permute-start.9) | collective-permute-done | bytes 262176 | tf_op jit(solution)/shard_map/ppermute | solution.py:309
  180.5 2.4 %collective-permute-start.11 = (bf16[8,144,128]{2,1,0:T(8,128)(2,1)S(1)}, bf16[8,144,128]{2,1,0:T(8,128)(2,1)S(1)}, u32[]{:S(2)}, u32[]{:S(2)}) collective-permute-start(bf16[8,144,128]{2,1,0:T(8,128)(2,1)S(1)} %bitcast.114), channel_id=1, source_target_pairs={{0,4},{1,5},{2,6},{3,7},{4,0},{5,1},{6,2},{7,3},{8,12},{9,13},{10,... | collective-permute-start | bytes 884744 | tf_op jit(solution)/shard_map/ppermute | solution.py:309
  184.5 3.2 %collective-permute-done.13 = bf16[4,128,128]{2,1,0:T(8,128)(2,1)S(1)} collective-permute-done((bf16[4,128,128]{2,1,0:T(8,128)(2,1)S(1)}, bf16[4,128,128]{2,1,0:T(8,128)(2,1)S(1)}, u32[]{:S(2)}, u32[]{:S(2)}) %collective-permute-start.13) | collective-permute-done | bytes 131104 | tf_op jit(solution)/shard_map/ppermute | solution.py:309
  188.6 3.8 %collective-permute-done.11 = bf16[8,144,128]{2,1,0:T(8,128)(2,1)S(1)} collective-permute-done((bf16[8,144,128]{2,1,0:T(8,128)(2,1)S(1)}, bf16[8,144,128]{2,1,0:T(8,128)(2,1)S(1)}, u32[]{:S(2)}, u32[]{:S(2)}) %collective-permute-start.11) | collective-permute-done | bytes 294944 | tf_op jit(solution)/shard_map/ppermute | solution.py:309
  193.3 6.6 %collective-permute-done.12 = bf16[4,144,128]{2,1,0:T(8,128)(2,1)S(1)} collective-permute-done((bf16[4,144,128]{2,1,0:T(8,128)(2,1)S(1)}, bf16[4,144,128]{2,1,0:T(8,128)(2,1)S(1)}, u32[]{:S(2)}, u32[]{:S(2)}) %collective-permute-start.12) | collective-permute-done | bytes 147488 | tf_op jit(solution)/shard_map/ppermute | solution.py:309
  (61 shorter events, 17.8 us)
Async XLA Ops:
  2.0 44.0 %copy-start.2 = (s32[1,8192]{1,0:T(1,128)S(1)}, s32[1,8192]{1,0:T(1,128)}, u32[]{:S(2)}) copy-start(s32[1,8192]{1,0:T(1,128)} %param.11) | copy-start | bytes 98308
  43.2 39.7 %collective-permute-start = (bf16[128,6144]{1,0:T(8,128)(2,1)}, bf16[128,6144]{1,0:T(8,128)(2,1)S(1)}, u32[]{:S(2)}, u32[]{:S(2)}) collective-permute-start(bf16[128,6144]{1,0:T(8,128)(2,1)} %get-tuple-element.52), channel_id=1, source_target_pairs={{16,0},{17,1},{18,2},{19,3},{20,4},{21,5},{22,6},{23,7},{24,8},{25... | collective-permute-start | bytes 4718600 | tf_op jit(solution)/shard_map/ppermute | solution.py:436
  44.5 49.3 %collective-permute-start.1 = (bf16[128,2048]{1,0:T(8,128)(2,1)}, bf16[128,2048]{1,0:T(8,128)(2,1)S(1)}, u32[]{:S(2)}, u32[]{:S(2)}) collective-permute-start(bf16[128,2048]{1,0:T(8,128)(2,1)} %get-tuple-element.58), channel_id=1, source_target_pairs={{16,0},{17,1},{18,2},{19,3},{20,4},{21,5},{22,6},{23,7},{24,8},{25... | collective-permute-start | bytes 1572872 | tf_op jit(solution)/shard_map/ppermute | solution.py:436
  46.0 36.9 %copy-start.1 = (f32[128,128]{1,0:T(8,128)S(1)}, f32[128,128]{1,0:T(8,128)}, u32[]{:S(2)}) copy-start(f32[128,128]{1,0:T(8,128)} %broadcast_in_dim.12.live) | copy-start | bytes 196612
  101.4 19.2 %collective-permute-start.2 = (bf16[32,128,128]{2,1,0:T(8,128)(2,1)S(1)}, bf16[32,128,128]{2,1,0:T(8,128)(2,1)}, u32[]{:S(2)}, u32[]{:S(2)}) collective-permute-start(bf16[32,128,128]{2,1,0:T(8,128)(2,1)S(1)} %get-tuple-element.65), channel_id=1, source_target_pairs={{0,1},{1,0},{2,3},{3,2},{4,5},{5,4},{6,7},{7,6},{8,9},{9,8},{10,11... | collective-permute-start | bytes 3145736 | tf_op jit(solution)/shard_map/ppermute | solution.py:309
  120.6 18.2 %collective-permute-start.3 = (bf16[32,128,128]{2,1,0:T(8,128)(2,1)}, bf16[32,128,128]{2,1,0:T(8,128)(2,1)}, u32[]{:S(2)}, u32[]{:S(2)}) collective-permute-start(bf16[32,128,128]{2,1,0:T(8,128)(2,1)} %get-tuple-element.73), channel_id=1, source_target_pairs={{0,1},{1,0},{2,3},{3,2},{4,5},{5,4},{6,7},{7,6},{8,9},{9,8},{10,11... | collective-permute-start | bytes 3145736 | tf_op jit(solution)/shard_map/ppermute | solution.py:309
  121.2 17.6 %collective-permute-start.4 = (bf16[32,128,128]{2,1,0:T(8,128)(2,1)}, bf16[32,128,128]{2,1,0:T(8,128)(2,1)}, u32[]{:S(2)}, u32[]{:S(2)}) collective-permute-start(bf16[32,128,128]{2,1,0:T(8,128)(2,1)} %get-tuple-element.75), channel_id=1, source_target_pairs={{0,1},{1,0},{2,3},{3,2},{4,5},{5,4},{6,7},{7,6},{8,9},{9,8},{10,11... | collective-permute-start | bytes 3145736 | tf_op jit(solution)/shard_map/ppermute | solution.py:309
  123.6 15.2 %collective-permute-start.5 = (bf16[16,128,128]{2,1,0:T(8,128)(2,1)S(1)}, bf16[16,128,128]{2,1,0:T(8,128)(2,1)S(1)}, u32[]{:S(2)}, u32[]{:S(2)}) collective-permute-start(bf16[16,128,128]{2,1,0:T(8,128)(2,1)S(1)} %bitcast.111), channel_id=1, source_target_pairs={{0,2},{1,3},{2,0},{3,1},{4,6},{5,7},{6,4},{7,5},{8,10},{9,11},{10,... | collective-permute-start | bytes 1572872 | tf_op jit(solution)/shard_map/ppermute | solution.py:309
  138.8 4.5 %collective-permute-start.6 = (bf16[32,144,128]{2,1,0:T(8,128)(2,1)}, bf16[32,144,128]{2,1,0:T(8,128)(2,1)}, u32[]{:S(2)}, u32[]{:S(2)}) collective-permute-start(bf16[32,144,128]{2,1,0:T(8,128)(2,1)} %get-tuple-element.89), channel_id=1, source_target_pairs={{0,1},{1,0},{2,3},{3,2},{4,5},{5,4},{6,7},{7,6},{8,9},{9,8},{10,11... | collective-permute-start | bytes 3538952 | tf_op jit(solution)/shard_map/ppermute | solution.py:309
  141.6 15.1 %collective-permute-start.8 = (bf16[16,128,128]{2,1,0:T(8,128)(2,1)}, bf16[16,128,128]{2,1,0:T(8,128)(2,1)}, u32[]{:S(2)}, u32[]{:S(2)}) collective-permute-start(bf16[16,128,128]{2,1,0:T(8,128)(2,1)} %bitcast.19), channel_id=1, source_target_pairs={{0,2},{1,3},{2,0},{3,1},{4,6},{5,7},{6,4},{7,5},{8,10},{9,11},{10,... | collective-permute-start | bytes 1572872 | tf_op jit(solution)/shard_map/ppermute | solution.py:309
  145.7 26.4 %collective-permute-start.7 = (bf16[16,144,128]{2,1,0:T(8,128)(2,1)}, bf16[16,144,128]{2,1,0:T(8,128)(2,1)S(1)}, u32[]{:S(2)}, u32[]{:S(2)}) collective-permute-start(bf16[16,144,128]{2,1,0:T(8,128)(2,1)} %bitcast.13), channel_id=1, source_target_pairs={{0,2},{1,3},{2,0},{3,1},{4,6},{5,7},{6,4},{7,5},{8,10},{9,11},{10,... | collective-permute-start | bytes 1769480 | tf_op jit(solution)/shard_map/ppermute | solution.py:309
  146.2 10.5 %copy-start.5 = (bf16[4,1,4,128,128]{4,3,2,1,0:T(8,128)(2,1)S(1)}, bf16[4,1,4,128,128]{4,3,2,1,0:T(8,128)(2,1)}, u32[]{:S(2)}) copy-start(bf16[4,1,4,128,128]{4,3,2,1,0:T(8,128)(2,1)} %get-tuple-element.108) | copy-start | bytes 1572868
  146.2 10.5 %copy-start.6 = (bf16[4,1,4,128,128]{4,3,2,1,0:T(8,128)(2,1)S(1)}, bf16[4,1,4,128,128]{4,3,2,1,0:T(8,128)(2,1)}, u32[]{:S(2)}) copy-start(bf16[4,1,4,128,128]{4,3,2,1,0:T(8,128)(2,1)} %get-tuple-element.105) | copy-start | bytes 1572868
  146.2 10.5 %copy-start.8 = (bf16[16,128,128]{2,1,0:T(8,128)(2,1)S(1)}, bf16[16,128,128]{2,1,0:T(8,128)(2,1)}, u32[]{:S(2)}) copy-start(bf16[16,128,128]{2,1,0:T(8,128)(2,1)} %copy-done.7) | copy-start | bytes 1572868
  148.7 23.6 %collective-permute-start.10 = (bf16[16,128,128]{2,1,0:T(8,128)(2,1)}, bf16[16,128,128]{2,1,0:T(8,128)(2,1)S(1)}, u32[]{:S(2)}, u32[]{:S(2)}) collective-permute-start(bf16[16,128,128]{2,1,0:T(8,128)(2,1)} %bitcast.26), channel_id=1, source_target_pairs={{0,4},{1,5},{2,6},{3,7},{4,0},{5,1},{6,2},{7,3},{8,12},{9,13},{10,... | collective-permute-start | bytes 1572872 | tf_op jit(solution)/shard_map/ppermute | solution.py:309
  158.9 10.5 %collective-permute-start.16 = (bf16[8,128,128]{2,1,0:T(8,128)(2,1)}, bf16[8,128,128]{2,1,0:T(8,128)(2,1)S(1)}, u32[]{:S(2)}, u32[]{:S(2)}) collective-permute-start(bf16[8,128,128]{2,1,0:T(8,128)(2,1)} %bitcast.47), channel_id=1, source_target_pairs={{0,4},{1,5},{2,6},{3,7},{4,0},{5,1},{6,2},{7,3},{8,12},{9,13},{10,... | collective-permute-start | bytes 786440 | tf_op jit(solution)/shard_map/ppermute | solution.py:309
  160.7 16.0 %collective-permute-start.9 = (bf16[8,128,128]{2,1,0:T(8,128)(2,1)}, bf16[8,128,128]{2,1,0:T(8,128)(2,1)}, u32[]{:S(2)}, u32[]{:S(2)}) collective-permute-start(bf16[8,128,128]{2,1,0:T(8,128)(2,1)} %bitcast.22), channel_id=1, source_target_pairs={{0,4},{1,5},{2,6},{3,7},{4,0},{5,1},{6,2},{7,3},{8,12},{9,13},{10,... | collective-permute-start | bytes 786440 | tf_op jit(solution)/shard_map/ppermute | solution.py:309
  169.4 11.1 %collective-permute-start.17 = (bf16[4,128,128]{2,1,0:T(8,128)(2,1)S(1)}, bf16[4,128,128]{2,1,0:T(8,128)(2,1)S(1)}, u32[]{:S(2)}, u32[]{:S(2)}) collective-permute-start(bf16[4,128,128]{2,1,0:T(8,128)(2,1)S(1)} %fusion.14), channel_id=1, source_target_pairs={{0,8},{1,9},{2,10},{3,11},{4,12},{5,13},{6,14},{7,15},{8,0},{9,1},... | collective-permute-start | bytes 393224 | tf_op jit(solution)/shard_map/ppermute | solution.py:309
  172.1 8.3 %copy-start.10 = (bf16[8,128,128]{2,1,0:T(8,128)(2,1)S(1)}, bf16[8,128,128]{2,1,0:T(8,128)(2,1)}, u32[]{:S(2)}) copy-start(bf16[8,128,128]{2,1,0:T(8,128)(2,1)} %copy-done.9) | copy-start | bytes 786436
  176.9 6.8 %collective-permute-start.14 = (bf16[8,128,128]{2,1,0:T(8,128)(2,1)S(1)}, bf16[8,128,128]{2,1,0:T(8,128)(2,1)S(1)}, u32[]{:S(2)}, u32[]{:S(2)}) collective-permute-start(bf16[8,128,128]{2,1,0:T(8,128)(2,1)S(1)} %bitcast.119), channel_id=1, source_target_pairs={{0,2},{1,3},{2,0},{3,1},{4,6},{5,7},{6,4},{7,5},{8,10},{9,11},{10,... | collective-permute-start | bytes 786440 | tf_op jit(solution)/shard_map/ppermute | solution.py:309
  179.4 8.3 %collective-permute-start.13 = (bf16[4,128,128]{2,1,0:T(8,128)(2,1)S(1)}, bf16[4,128,128]{2,1,0:T(8,128)(2,1)S(1)}, u32[]{:S(2)}, u32[]{:S(2)}) collective-permute-start(bf16[4,128,128]{2,1,0:T(8,128)(2,1)S(1)} %fusion.10), channel_id=1, source_target_pairs={{0,8},{1,9},{2,10},{3,11},{4,12},{5,13},{6,14},{7,15},{8,0},{9,1},... | collective-permute-start | bytes 393224 | tf_op jit(solution)/shard_map/ppermute | solution.py:309
  180.5 12.0 %collective-permute-start.11 = (bf16[8,144,128]{2,1,0:T(8,128)(2,1)S(1)}, bf16[8,144,128]{2,1,0:T(8,128)(2,1)S(1)}, u32[]{:S(2)}, u32[]{:S(2)}) collective-permute-start(bf16[8,144,128]{2,1,0:T(8,128)(2,1)S(1)} %bitcast.114), channel_id=1, source_target_pairs={{0,4},{1,5},{2,6},{3,7},{4,0},{5,1},{6,2},{7,3},{8,12},{9,13},{10,... | collective-permute-start | bytes 884744 | tf_op jit(solution)/shard_map/ppermute | solution.py:309
  183.8 9.5 %collective-permute-start.15 = (bf16[4,128,128]{2,1,0:T(8,128)(2,1)S(1)}, bf16[4,128,128]{2,1,0:T(8,128)(2,1)S(1)}, u32[]{:S(2)}, u32[]{:S(2)}) collective-permute-start(bf16[4,128,128]{2,1,0:T(8,128)(2,1)S(1)} %fusion.12), channel_id=1, source_target_pairs={{0,8},{1,9},{2,10},{3,11},{4,12},{5,13},{6,14},{7,15},{8,0},{9,1},... | collective-permute-start | bytes 393224 | tf_op jit(solution)/shard_map/ppermute | solution.py:309
  192.5 7.4 %collective-permute-start.12 = (bf16[4,144,128]{2,1,0:T(8,128)(2,1)S(1)}, bf16[4,144,128]{2,1,0:T(8,128)(2,1)S(1)}, u32[]{:S(2)}, u32[]{:S(2)}) collective-permute-start(bf16[4,144,128]{2,1,0:T(8,128)(2,1)S(1)} %fusion.8), channel_id=1, source_target_pairs={{0,8},{1,9},{2,10},{3,11},{4,12},{5,13},{6,14},{7,15},{8,0},{9,1},... | collective-permute-start | bytes 442376 | tf_op jit(solution)/shard_map/ppermute | solution.py:309
  (5 other events, 17.0 us)

commit v7 on v6

--- a/solution.py
+++ b/solution.py
@@ -210,11 +210,14 @@
 
 
 def back_three(own, skipped, perm, flags, cot, live, moved, cp_t, fac, *refs):
-    *given, keep, send, gy_out, gc_t, even, odd = refs
+    if len(refs) > 6:
+        _, _, _, gc_in, keep, send, gy_out, gc_out, gc_t, even, odd = refs
+        gc_t[...] = gc_in[...]
+    else:
+        keep, send, gy_out, gc_t, even, odd = refs
+        gc_out = None
     bs = fac.shape[2]
     outs = (keep, send)
-    if given:
-        gc_t[...] = given[3][...]
 
     def make(k):
         here = at_block(k, bs)
@@ -228,10 +231,12 @@
 
     scattered(make, perm, (pl.program_id(0) + skipped) * STEP, gc_t, even, odd, bs)
     each_split(flags, own, grads)
+    if gc_out is not None:
+        gc_out[...] = gc_t[...].astype(BF16)
 
 
 def back_two_one(
-    own, perm, flags, gc_t, ap_t, fac_two, fac_one, keep_two, send_two, keep_one, send_one, ga_out, ga_t, h_t, gpre_t, gc_b, even, odd
+    own, perm, flags, gc_t, ap_t, fac_two, fac_one, keep_two, send_two, keep_one, send_one, ga_out, ga_t, h_t, gpre_t, even, odd
 ):
     c = pl.program_id(0)
     bs = fac_two.shape[2]
@@ -240,15 +245,13 @@
     def make(k):
         here = at_block(k, bs)
         h_t[here, :], slope = gelu_parts(dot(fac_one[0, k], ap_t[here, :], 0, 0))
-        gc = gc_t[here, :].astype(BF16)
-        gc_b[here, :] = gc
-        gpre = (dot(fac_two[0, k], gc, 1, 0) * slope).astype(BF16)
+        gpre = (dot(fac_two[0, k], gc_t[here, :], 1, 0) * slope).astype(BF16)
         gpre_t[here, :] = gpre
         return rounded(dot(fac_one[0, k], gpre, 1, 0))
 
     def grads(goes, k, block):
         at = at_block(block, bs)
-        twos[goes][k] = dot(h_t[at, :], gc_b[at, :], 1, 1).astype(BF16)
+        twos[goes][k] = dot(h_t[at, :], gc_t[at, :], 1, 1).astype(BF16)
         ones[goes][k] = dot(ap_t[at, :], gpre_t[at, :], 1, 1).astype(BF16)
 
     scattered(make, perm, c * STEP, ga_t, even, odd, bs)
@@ -472,10 +475,10 @@
         (1,),
         [shift(w_at), sca, w_at, shift(c_at), shift(f_at(3)), held, held, held, whole(width, tokens)],
         [shift(half_at), shift(half_at), shift(w_at), whole(width, tokens)],
-        shapes,
-        scratch,
+        shapes[:3] + [feat(BF16)],
+        [big] + scratch,
         prefetch=2,
-        aliases={7: 0, 8: 1, 9: 2, 10: 3},
+        aliases={7: 0, 8: 1, 9: 2},
     )(perm, flags, cotangent, live, moved[1], cp_t, fac, *partial)
     three = start(keep, send, bits)
     three.go()
@@ -486,7 +489,7 @@
         [c_at, c_at, f_at(2), f_at(1)],
         [half_at] * 4 + [whole(width, tokens)],
         [half()] * 4 + [feat(BF16)],
-        [big, part_t, part_t, part_t, block, block],
+        [big, part_t, part_t, block, block],
         prefetch=2,
     )(perm, flags, gc_t, ap_t, fac, fac)
     two, one = start(keep_two, send_two, other), start(keep_one, send_one, bits)

time: 202 us -> 202 us (level)
  no operation moved by 1% of the time
where the time goes in v7:
time: 202 us; the launch traced here: 201 us
  Pallas kernels  103 us (51%)
  waiting for transfers between devices  56.3 us (28%)
  starting transfers between devices  21.3 us (11%)
  other arithmetic  16.5 us (8%)
  local copies, waits for them, and re-layouts  2.72 us (1%)
    pallas_call x1, Pallas kernels, on_device(): call(first_pass, 'first_pass', (4, steps), [tok, pl.BlockSpec(wide, lambd...  41.2 us
    ppermute x16, waiting for transfers between devices, go(): lax.ppermute(self.send, 'dp', [(i, i ^ 1 << bit) for i in range(self.repl...  35.2 us
    ppermute x2, waiting for transfers between devices, on_device(): lax.ppermute(piece, 'section', [(i, i - 1) for i in range(1, sections)])  21 us
    pallas_call x1, Pallas kernels, on_device(): call(functools.partial(back_two_one, own), 'back_two_one', (steps,), [c_a...  18.7 us
    ppermute x16, starting transfers between devices, go(): lax.ppermute(self.send, 'dp', [(i, i ^ 1 << bit) for i in range(self.repl...  18.5 us
    pallas_call x1, Pallas kernels, on_device(): call(forward_second, 'forward_second', (2, steps), [pl.BlockSpec(chunk, l...  14.4 us
    convert_element_type x9, other arithmetic, part(): total = (a.astype(F32) + b.astype(F32)).astype(self.keep.dtype)  13.5 us
    pallas_call x1, Pallas kernels, on_device(): call(functools.partial(back_three, own, 0), 'back_three_early', (steps -...  10.9 us
  transfers between devices with their start and end apart: 18, of which 9 were waited for; matrix products, arithmetic and copies ran while one was open for 7% of the time, Pallas kernels for 27%

profile of v7, /device:TPU:0, one launch (start us, length us, event | category | flops | bytes accessed | tf_op | source)
XLA Modules:
  0.0 200.8 jit_solution(12875842638903935935)
XLA Ops:
  2.0 41.2 %first_pass.1 = (bf16[8192,128]{1,0:T(8,128)(2,1)}, f32[128,128]{1,0:T(8,128)}, bf16[128,6144]{1,0:T(8,128)(2,1)}, bf16[128,2048]{1,0:T(8,128)(2,1)}) custom-call(s32[8192]{0:T(1024)} %bitcast.84, bf16[128,8192]{1,0:T(8,128)(2,1)} %bitcast.98, bf16[128,8192]{1,0:T(8,128)(2,1)} %cot.5, f32[128,128]{1,0:T(8,128)} %broadcast_in_dim.12.live, f32[1,8192]{1,0:T(1,128)} %gamma.3, ...), custom_call_target="tpu_custom_call" | custom-call | tf_op jit(solution)/shard_map/first_pass/pallas_call | solution.py:417
  46.0 14.4 %forward_second.1.cp_t = bf16[8192,128]{1,0:T(8,128)(2,1)S(1)} custom-call(s32[8192]{0:T(1024)S(1)} %bitcast.85, bf16[8192,128]{1,0:T(8,128)(2,1)} %get-tuple-element.53.ap_t, bf16[4,64,128,128]{3,2,1,0:T(8,128)(2,1)} %bitcast.91, bf16[4,64,128,128]{3,2,1,0:T(8,128)(2,1)} %bitcast.92), custom_call_target="tpu_custom_call" | custom-call | tf_op jit(solution)/shard_map/forward_second/pallas_call | solution.py:442
  61.8 21.0 %collective-permute-done.moved = bf16[128,6144]{1,0:T(8,128)(2,1)S(1)} collective-permute-done((bf16[128,6144]{1,0:T(8,128)(2,1)}, bf16[128,6144]{1,0:T(8,128)(2,1)S(1)}, u32[]{:S(2)}, u32[]{:S(2)}) %collective-permute-start) | collective-permute-done | bytes 1572896 | tf_op jit(solution)/shard_map/ppermute | solution.py:439
  82.9 10.9 %back_three_early.1 = (bf16[32,128,128]{2,1,0:T(8,128)(2,1)S(1)}, bf16[32,128,128]{2,1,0:T(8,128)(2,1)S(1)}, bf16[128,8192]{1,0:T(8,128)(2,1)}, f32[8192,128]{1,0:T(8,128)}) custom-call(s32[8192]{0:T(1024)S(1)} %bitcast.86, s32[2]{0:T(128)S(1)} %pad_add_fusion.flags, bf16[128,8192]{1,0:T(8,128)(2,1)} %cot.5, f32[128,128]{1,0:T(8,128)S(1)} %copy-done.1, ...), custom_call_target="tpu_custom_call" | custom-call | tf_op jit(solution)/shard_map/back_three_early/pallas_call | solution.py:459
  93.7 7.2 %back_three_late.1 = (bf16[32,128,128]{2,1,0:T(8,128)(2,1)S(1)}, bf16[32,128,128]{2,1,0:T(8,128)(2,1)S(1)}, bf16[128,8192]{1,0:T(8,128)(2,1)}, bf16[8192,128]{1,0:T(8,128)(2,1)}) custom-call(s32[8192]{0:T(1024)S(1)} %bitcast.87, s32[2]{0:T(128)S(1)} %pad_add_fusion.flags, ...), custom_call_target="tpu_custom_call", output_to_operand_aliasing={{0}: (7, {}), {1}: (8, {}), {2}: (9, {})} | custom-call | tf_op jit(solution)/shard_map/back_three_late/pallas_call | solution.py:472
  101.0 18.7 %back_two_one.1 = (bf16[32,128,128]{2,1,0:T(8,128)(2,1)S(1)}, bf16[32,128,128]{2,1,0:T(8,128)(2,1)}, bf16[32,128,128]{2,1,0:T(8,128)(2,1)S(1)}, bf16[32,128,128]{2,1,0:T(8,128)(2,1)}, bf16[8192,128]{1,0:T(8,128)(2,1)}) custom-call(s32[8192]{0:T(1024)S(1)} %bitcast.88, s32[2]{0:T(128)S(1)} %pad_add_fusion.flags, bf16[8192,128]{1,0:T(8,128)(2,1)} %get-tuple-element.66.gc_t, ...), custom_call_target="tpu_custom_call" | custom-call | tf_op jit(solution)/shard_map/back_two_one/pallas_call | solution.py:485
  120.3 2.4 %add_convert_fusion.6 = (bf16[4,1,4,128,128]{4,3,2,1,0:T(8,128)(2,1)S(1)}, bf16[4,1,4,128,128]{4,3,2,1,0:T(8,128)(2,1)}) fusion(bf16[4,2,4,128,128]{4,3,2,1,0:T(8,128)(2,1)} %bitcast.6, s32[]{:T(128)S(6)} %select_n.68, bf16[4,2,4,128,128]{4,3,2,1,0:T(8,128)(2,1)S(1)} %bitcast.80, s32[]{:T(128)S(6)} %select_n.67), kind=kLoop, calls=%fused_computation.7 | loop fusion | flops 2097152 | bytes 3145736 | tf_op jit(solution)/shard_map/convert_element_type | solution.py:328
  122.7 2.7 %collective-permute-start.5 = (bf16[16,128,128]{2,1,0:T(8,128)(2,1)S(1)}, bf16[16,128,128]{2,1,0:T(8,128)(2,1)S(1)}, u32[]{:S(2)}, u32[]{:S(2)}) collective-permute-start(bf16[16,128,128]{2,1,0:T(8,128)(2,1)S(1)} %bitcast.111), channel_id=1, source_target_pairs={{0,2},{1,3},{2,0},{3,1},{4,6},{5,7},{6,4},{7,5},{8,10},{9,11},{10,... | collective-permute-start | bytes 1572872 | tf_op jit(solution)/shard_map/ppermute | solution.py:312
  125.4 10.8 %back_zero.1 = (bf16[32,144,128]{2,1,0:T(8,128)(2,1)S(1)}, bf16[32,144,128]{2,1,0:T(8,128)(2,1)}, bf16[128,8192]{1,0:T(8,128)(2,1)}) custom-call(s32[2]{0:T(128)S(1)} %pad_add_fusion.flags, bf16[8192,128]{1,0:T(8,128)(2,1)} %get-tuple-element.81.ga_t, bf16[128,8192]{1,0:T(8,128)(2,1)} %get-tuple-element.82.gy, bf16[128,8192]{1,0:T(8,128)(2,1)} %bitcast.99, ...), custom_call_target="tpu_custom_call" | custom-call | tf_op jit(solution)/shard_map/back_zero/pallas_call | solution.py:505
  136.2 1.7 collective-permute-done.5
  138.0 2.7 %add_convert_fusion.5 = (bf16[4,1,4,128,128]{4,3,2,1,0:T(8,128)(2,1)}, bf16[4,1,4,128,128]{4,3,2,1,0:T(8,128)(2,1)}) fusion(bf16[4,2,4,128,128]{4,3,2,1,0:T(8,128)(2,1)} %bitcast.17, s32[]{:T(128)S(6)} %select_n.67, bf16[4,2,4,128,128]{4,3,2,1,0:T(8,128)(2,1)S(1)} %bitcast.83, s32[]{:T(128)S(6)} %select_n.68), kind=kLoop, calls=%fused_computation.6 | loop fusion | flops 2097152 | bytes 3145736 | tf_op jit(solution)/shard_map/convert_element_type | solution.py:328
  140.7 1.8 collective-permute-start.8
  142.5 2.4 %add_convert_fusion.1 = (bf16[4,1,4,144,128]{4,3,2,1,0:T(8,128)(2,1)S(1)}, bf16[4,1,4,144,128]{4,3,2,1,0:T(8,128)(2,1)}) fusion(bf16[4,2,4,144,128]{4,3,2,1,0:T(8,128)(2,1)} %bitcast.11, s32[]{:T(128)S(6)} %select_n.67, bf16[4,2,4,144,128]{4,3,2,1,0:T(8,128)(2,1)S(1)} %bitcast.81, s32[]{:T(128)S(6)} %select_n.68), kind=kLoop, calls=%fused_computation.1 | loop fusion | flops 2359296 | bytes 3538952 | tf_op jit(solution)/shard_map/convert_element_type | solution.py:328
  145.3 2.5 %add_convert_fusion.2 = (bf16[2,1,8,128,128]{4,3,2,1,0:T(8,128)(2,1)}, bf16[2,1,8,128,128]{4,3,2,1,0:T(8,128)(2,1)S(1)}) fusion(bf16[2,2,8,128,128]{4,3,2,1,0:T(8,128)(2,1)} %bitcast.24, s32[]{:T(128)S(6)} %select_n.70, bf16[2,2,8,128,128]{4,3,2,1,0:T(8,128)(2,1)S(1)} %bitcast.82, s32[]{:T(128)S(6)} %select_n.69), kind=kLoop, calls=%fused_computation.3 | loop fusion | flops 2097152 | bytes 3145736 | tf_op jit(solution)/shard_map/convert_element_type | solution.py:328
  149.4 6.3 %collective-permute-done.8 = bf16[16,128,128]{2,1,0:T(8,128)(2,1)} collective-permute-done((bf16[16,128,128]{2,1,0:T(8,128)(2,1)}, bf16[16,128,128]{2,1,0:T(8,128)(2,1)}, u32[]{:S(2)}, u32[]{:S(2)}) %collective-permute-start.8) | collective-permute-done | bytes 524320 | tf_op jit(solution)/shard_map/ppermute | solution.py:312
  155.8 2.2 %add_convert_fusion.11 = (bf16[2,1,4,128,128]{4,3,2,1,0:T(8,128)(2,1)S(1)}, bf16[2,1,4,128,128]{4,3,2,1,0:T(8,128)(2,1)}, bf16[2,1,4,128,128]{4,3,2,1,0:T(8,128)(2,1)S(1)}, bf16[2,1,4,128,128]{4,3,2,1,0:T(8,128)(2,1)}) fusion(bf16[2,2,4,128,128]{4,3,2,1,0:T(8,128)(2,1)S(1)} %bitcast.109, s32[]{:T(128)S(6)} %select_n.69, ...), kind=kLoop, calls=%fused_computation.12 | loop fusion | flops 2097152 | bytes 3145736 | tf_op jit(solution)/shard_map/convert_element_type | solution.py:328
  158.0 1.8 collective-permute-start.16
  160.0 8.4 %collective-permute-done.16 = bf16[8,128,128]{2,1,0:T(8,128)(2,1)S(1)} collective-permute-done((bf16[8,128,128]{2,1,0:T(8,128)(2,1)}, bf16[8,128,128]{2,1,0:T(8,128)(2,1)S(1)}, u32[]{:S(2)}, u32[]{:S(2)}) %collective-permute-start.16) | collective-permute-done | bytes 262176 | tf_op jit(solution)/shard_map/ppermute | solution.py:312
  168.5 2.7 %collective-permute-start.17 = (bf16[4,128,128]{2,1,0:T(8,128)(2,1)S(1)}, bf16[4,128,128]{2,1,0:T(8,128)(2,1)S(1)}, u32[]{:S(2)}, u32[]{:S(2)}) collective-permute-start(bf16[4,128,128]{2,1,0:T(8,128)(2,1)S(1)} %fusion.14), channel_id=1, source_target_pairs={{0,8},{1,9},{2,10},{3,11},{4,12},{5,13},{6,14},{7,15},{8,0},{9,1},... | collective-permute-start | bytes 393224 | tf_op jit(solution)/shard_map/ppermute | solution.py:312
  171.4 4.4 %collective-permute-done.9 = bf16[8,128,128]{2,1,0:T(8,128)(2,1)} collective-permute-done((bf16[8,128,128]{2,1,0:T(8,128)(2,1)}, bf16[8,128,128]{2,1,0:T(8,128)(2,1)}, u32[]{:S(2)}, u32[]{:S(2)}) %collective-permute-start.9) | collective-permute-done | bytes 262176 | tf_op jit(solution)/shard_map/ppermute | solution.py:312
  179.6 2.4 %collective-permute-start.11 = (bf16[8,144,128]{2,1,0:T(8,128)(2,1)S(1)}, bf16[8,144,128]{2,1,0:T(8,128)(2,1)S(1)}, u32[]{:S(2)}, u32[]{:S(2)}) collective-permute-start(bf16[8,144,128]{2,1,0:T(8,128)(2,1)S(1)} %bitcast.114), channel_id=1, source_target_pairs={{0,4},{1,5},{2,6},{3,7},{4,0},{5,1},{6,2},{7,3},{8,12},{9,13},{10,... | collective-permute-start | bytes 884744 | tf_op jit(solution)/shard_map/ppermute | solution.py:312
  183.6 3.2 %collective-permute-done.13 = bf16[4,128,128]{2,1,0:T(8,128)(2,1)S(1)} collective-permute-done((bf16[4,128,128]{2,1,0:T(8,128)(2,1)S(1)}, bf16[4,128,128]{2,1,0:T(8,128)(2,1)S(1)}, u32[]{:S(2)}, u32[]{:S(2)}) %collective-permute-start.13) | collective-permute-done | bytes 131104 | tf_op jit(solution)/shard_map/ppermute | solution.py:312
  187.7 3.8 %collective-permute-done.11 = bf16[8,144,128]{2,1,0:T(8,128)(2,1)S(1)} collective-permute-done((bf16[8,144,128]{2,1,0:T(8,128)(2,1)S(1)}, bf16[8,144,128]{2,1,0:T(8,128)(2,1)S(1)}, u32[]{:S(2)}, u32[]{:S(2)}) %collective-permute-start.11) | collective-permute-done | bytes 294944 | tf_op jit(solution)/shard_map/ppermute | solution.py:312
  192.5 6.6 %collective-permute-done.12 = bf16[4,144,128]{2,1,0:T(8,128)(2,1)S(1)} collective-permute-done((bf16[4,144,128]{2,1,0:T(8,128)(2,1)S(1)}, bf16[4,144,128]{2,1,0:T(8,128)(2,1)S(1)}, u32[]{:S(2)}, u32[]{:S(2)}) %collective-permute-start.12) | collective-permute-done | bytes 147488 | tf_op jit(solution)/shard_map/ppermute | solution.py:312
  (61 shorter events, 17.8 us)
Async XLA Ops:
  2.0 44.0 %copy-start.2 = (s32[1,8192]{1,0:T(1,128)S(1)}, s32[1,8192]{1,0:T(1,128)}, u32[]{:S(2)}) copy-start(s32[1,8192]{1,0:T(1,128)} %param.11) | copy-start | bytes 98308
  43.2 39.7 %collective-permute-start = (bf16[128,6144]{1,0:T(8,128)(2,1)}, bf16[128,6144]{1,0:T(8,128)(2,1)S(1)}, u32[]{:S(2)}, u32[]{:S(2)}) collective-permute-start(bf16[128,6144]{1,0:T(8,128)(2,1)} %get-tuple-element.52), channel_id=1, source_target_pairs={{16,0},{17,1},{18,2},{19,3},{20,4},{21,5},{22,6},{23,7},{24,8},{25... | collective-permute-start | bytes 4718600 | tf_op jit(solution)/shard_map/ppermute | solution.py:439
  44.5 49.2 %collective-permute-start.1 = (bf16[128,2048]{1,0:T(8,128)(2,1)}, bf16[128,2048]{1,0:T(8,128)(2,1)S(1)}, u32[]{:S(2)}, u32[]{:S(2)}) collective-permute-start(bf16[128,2048]{1,0:T(8,128)(2,1)} %get-tuple-element.58), channel_id=1, source_target_pairs={{16,0},{17,1},{18,2},{19,3},{20,4},{21,5},{22,6},{23,7},{24,8},{25... | collective-permute-start | bytes 1572872 | tf_op jit(solution)/shard_map/ppermute | solution.py:439
  46.0 36.9 %copy-start.1 = (f32[128,128]{1,0:T(8,128)S(1)}, f32[128,128]{1,0:T(8,128)}, u32[]{:S(2)}) copy-start(f32[128,128]{1,0:T(8,128)} %broadcast_in_dim.12.live) | copy-start | bytes 196612
  101.0 18.7 %collective-permute-start.2 = (bf16[32,128,128]{2,1,0:T(8,128)(2,1)S(1)}, bf16[32,128,128]{2,1,0:T(8,128)(2,1)}, u32[]{:S(2)}, u32[]{:S(2)}) collective-permute-start(bf16[32,128,128]{2,1,0:T(8,128)(2,1)S(1)} %get-tuple-element.65), channel_id=1, source_target_pairs={{0,1},{1,0},{2,3},{3,2},{4,5},{5,4},{6,7},{7,6},{8,9},{9,8},{10,11... | collective-permute-start | bytes 3145736 | tf_op jit(solution)/shard_map/ppermute | solution.py:312
  119.6 18.3 %collective-permute-start.3 = (bf16[32,128,128]{2,1,0:T(8,128)(2,1)}, bf16[32,128,128]{2,1,0:T(8,128)(2,1)}, u32[]{:S(2)}, u32[]{:S(2)}) collective-permute-start(bf16[32,128,128]{2,1,0:T(8,128)(2,1)} %get-tuple-element.73), channel_id=1, source_target_pairs={{0,1},{1,0},{2,3},{3,2},{4,5},{5,4},{6,7},{7,6},{8,9},{9,8},{10,11... | collective-permute-start | bytes 3145736 | tf_op jit(solution)/shard_map/ppermute | solution.py:312
  120.2 17.7 %collective-permute-start.4 = (bf16[32,128,128]{2,1,0:T(8,128)(2,1)}, bf16[32,128,128]{2,1,0:T(8,128)(2,1)}, u32[]{:S(2)}, u32[]{:S(2)}) collective-permute-start(bf16[32,128,128]{2,1,0:T(8,128)(2,1)} %get-tuple-element.75), channel_id=1, source_target_pairs={{0,1},{1,0},{2,3},{3,2},{4,5},{5,4},{6,7},{7,6},{8,9},{9,8},{10,11... | collective-permute-start | bytes 3145736 | tf_op jit(solution)/shard_map/ppermute | solution.py:312
  122.7 15.2 %collective-permute-start.5 = (bf16[16,128,128]{2,1,0:T(8,128)(2,1)S(1)}, bf16[16,128,128]{2,1,0:T(8,128)(2,1)S(1)}, u32[]{:S(2)}, u32[]{:S(2)}) collective-permute-start(bf16[16,128,128]{2,1,0:T(8,128)(2,1)S(1)} %bitcast.111), channel_id=1, source_target_pairs={{0,2},{1,3},{2,0},{3,1},{4,6},{5,7},{6,4},{7,5},{8,10},{9,11},{10,... | collective-permute-start | bytes 1572872 | tf_op jit(solution)/shard_map/ppermute | solution.py:312
  137.9 4.6 %collective-permute-start.6 = (bf16[32,144,128]{2,1,0:T(8,128)(2,1)}, bf16[32,144,128]{2,1,0:T(8,128)(2,1)}, u32[]{:S(2)}, u32[]{:S(2)}) collective-permute-start(bf16[32,144,128]{2,1,0:T(8,128)(2,1)} %get-tuple-element.89), channel_id=1, source_target_pairs={{0,1},{1,0},{2,3},{3,2},{4,5},{5,4},{6,7},{7,6},{8,9},{9,8},{10,11... | collective-permute-start | bytes 3538952 | tf_op jit(solution)/shard_map/ppermute | solution.py:312
  140.7 15.1 %collective-permute-start.8 = (bf16[16,128,128]{2,1,0:T(8,128)(2,1)}, bf16[16,128,128]{2,1,0:T(8,128)(2,1)}, u32[]{:S(2)}, u32[]{:S(2)}) collective-permute-start(bf16[16,128,128]{2,1,0:T(8,128)(2,1)} %bitcast.19), channel_id=1, source_target_pairs={{0,2},{1,3},{2,0},{3,1},{4,6},{5,7},{6,4},{7,5},{8,10},{9,11},{10,... | collective-permute-start | bytes 1572872 | tf_op jit(solution)/shard_map/ppermute | solution.py:312
  144.8 26.4 %collective-permute-start.7 = (bf16[16,144,128]{2,1,0:T(8,128)(2,1)}, bf16[16,144,128]{2,1,0:T(8,128)(2,1)S(1)}, u32[]{:S(2)}, u32[]{:S(2)}) collective-permute-start(bf16[16,144,128]{2,1,0:T(8,128)(2,1)} %bitcast.13), channel_id=1, source_target_pairs={{0,2},{1,3},{2,0},{3,1},{4,6},{5,7},{6,4},{7,5},{8,10},{9,11},{10,... | collective-permute-start | bytes 1769480 | tf_op jit(solution)/shard_map/ppermute | solution.py:312
  145.3 10.5 %copy-start.5 = (bf16[4,1,4,128,128]{4,3,2,1,0:T(8,128)(2,1)S(1)}, bf16[4,1,4,128,128]{4,3,2,1,0:T(8,128)(2,1)}, u32[]{:S(2)}) copy-start(bf16[4,1,4,128,128]{4,3,2,1,0:T(8,128)(2,1)} %get-tuple-element.108) | copy-start | bytes 1572868
  145.3 10.5 %copy-start.6 = (bf16[4,1,4,128,128]{4,3,2,1,0:T(8,128)(2,1)S(1)}, bf16[4,1,4,128,128]{4,3,2,1,0:T(8,128)(2,1)}, u32[]{:S(2)}) copy-start(bf16[4,1,4,128,128]{4,3,2,1,0:T(8,128)(2,1)} %get-tuple-element.105) | copy-start | bytes 1572868
  145.3 10.5 %copy-start.8 = (bf16[16,128,128]{2,1,0:T(8,128)(2,1)S(1)}, bf16[16,128,128]{2,1,0:T(8,128)(2,1)}, u32[]{:S(2)}) copy-start(bf16[16,128,128]{2,1,0:T(8,128)(2,1)} %copy-done.7) | copy-start | bytes 1572868
  147.8 23.6 %collective-permute-start.10 = (bf16[16,128,128]{2,1,0:T(8,128)(2,1)}, bf16[16,128,128]{2,1,0:T(8,128)(2,1)S(1)}, u32[]{:S(2)}, u32[]{:S(2)}) collective-permute-start(bf16[16,128,128]{2,1,0:T(8,128)(2,1)} %bitcast.26), channel_id=1, source_target_pairs={{0,4},{1,5},{2,6},{3,7},{4,0},{5,1},{6,2},{7,3},{8,12},{9,13},{10,... | collective-permute-start | bytes 1572872 | tf_op jit(solution)/shard_map/ppermute | solution.py:312
  158.0 10.4 %collective-permute-start.16 = (bf16[8,128,128]{2,1,0:T(8,128)(2,1)}, bf16[8,128,128]{2,1,0:T(8,128)(2,1)S(1)}, u32[]{:S(2)}, u32[]{:S(2)}) collective-permute-start(bf16[8,128,128]{2,1,0:T(8,128)(2,1)} %bitcast.47), channel_id=1, source_target_pairs={{0,4},{1,5},{2,6},{3,7},{4,0},{5,1},{6,2},{7,3},{8,12},{9,13},{10,... | collective-permute-start | bytes 786440 | tf_op jit(solution)/shard_map/ppermute | solution.py:312
  159.8 16.0 %collective-permute-start.9 = (bf16[8,128,128]{2,1,0:T(8,128)(2,1)}, bf16[8,128,128]{2,1,0:T(8,128)(2,1)}, u32[]{:S(2)}, u32[]{:S(2)}) collective-permute-start(bf16[8,128,128]{2,1,0:T(8,128)(2,1)} %bitcast.22), channel_id=1, source_target_pairs={{0,4},{1,5},{2,6},{3,7},{4,0},{5,1},{6,2},{7,3},{8,12},{9,13},{10,... | collective-permute-start | bytes 786440 | tf_op jit(solution)/shard_map/ppermute | solution.py:312
  168.5 11.1 %collective-permute-start.17 = (bf16[4,128,128]{2,1,0:T(8,128)(2,1)S(1)}, bf16[4,128,128]{2,1,0:T(8,128)(2,1)S(1)}, u32[]{:S(2)}, u32[]{:S(2)}) collective-permute-start(bf16[4,128,128]{2,1,0:T(8,128)(2,1)S(1)} %fusion.14), channel_id=1, source_target_pairs={{0,8},{1,9},{2,10},{3,11},{4,12},{5,13},{6,14},{7,15},{8,0},{9,1},... | collective-permute-start | bytes 393224 | tf_op jit(solution)/shard_map/ppermute | solution.py:312
  171.2 8.3 %copy-start.10 = (bf16[8,128,128]{2,1,0:T(8,128)(2,1)S(1)}, bf16[8,128,128]{2,1,0:T(8,128)(2,1)}, u32[]{:S(2)}) copy-start(bf16[8,128,128]{2,1,0:T(8,128)(2,1)} %copy-done.9) | copy-start | bytes 786436
  176.0 6.8 %collective-permute-start.14 = (bf16[8,128,128]{2,1,0:T(8,128)(2,1)S(1)}, bf16[8,128,128]{2,1,0:T(8,128)(2,1)S(1)}, u32[]{:S(2)}, u32[]{:S(2)}) collective-permute-start(bf16[8,128,128]{2,1,0:T(8,128)(2,1)S(1)} %bitcast.119), channel_id=1, source_target_pairs={{0,2},{1,3},{2,0},{3,1},{4,6},{5,7},{6,4},{7,5},{8,10},{9,11},{10,... | collective-permute-start | bytes 786440 | tf_op jit(solution)/shard_map/ppermute | solution.py:312
  178.5 8.3 %collective-permute-start.13 = (bf16[4,128,128]{2,1,0:T(8,128)(2,1)S(1)}, bf16[4,128,128]{2,1,0:T(8,128)(2,1)S(1)}, u32[]{:S(2)}, u32[]{:S(2)}) collective-permute-start(bf16[4,128,128]{2,1,0:T(8,128)(2,1)S(1)} %fusion.10), channel_id=1, source_target_pairs={{0,8},{1,9},{2,10},{3,11},{4,12},{5,13},{6,14},{7,15},{8,0},{9,1},... | collective-permute-start | bytes 393224 | tf_op jit(solution)/shard_map/ppermute | solution.py:312
  179.6 12.0 %collective-permute-start.11 = (bf16[8,144,128]{2,1,0:T(8,128)(2,1)S(1)}, bf16[8,144,128]{2,1,0:T(8,128)(2,1)S(1)}, u32[]{:S(2)}, u32[]{:S(2)}) collective-permute-start(bf16[8,144,128]{2,1,0:T(8,128)(2,1)S(1)} %bitcast.114), channel_id=1, source_target_pairs={{0,4},{1,5},{2,6},{3,7},{4,0},{5,1},{6,2},{7,3},{8,12},{9,13},{10,... | collective-permute-start | bytes 884744 | tf_op jit(solution)/shard_map/ppermute | solution.py:312
  182.9 9.5 %collective-permute-start.15 = (bf16[4,128,128]{2,1,0:T(8,128)(2,1)S(1)}, bf16[4,128,128]{2,1,0:T(8,128)(2,1)S(1)}, u32[]{:S(2)}, u32[]{:S(2)}) collective-permute-start(bf16[4,128,128]{2,1,0:T(8,128)(2,1)S(1)} %fusion.12), channel_id=1, source_target_pairs={{0,8},{1,9},{2,10},{3,11},{4,12},{5,13},{6,14},{7,15},{8,0},{9,1},... | collective-permute-start | bytes 393224 | tf_op jit(solution)/shard_map/ppermute | solution.py:312
  191.6 7.4 %collective-permute-start.12 = (bf16[4,144,128]{2,1,0:T(8,128)(2,1)S(1)}, bf16[4,144,128]{2,1,0:T(8,128)(2,1)S(1)}, u32[]{:S(2)}, u32[]{:S(2)}) collective-permute-start(bf16[4,144,128]{2,1,0:T(8,128)(2,1)S(1)} %fusion.8), channel_id=1, source_target_pairs={{0,8},{1,9},{2,10},{3,11},{4,12},{5,13},{6,14},{7,15},{8,0},{9,1},... | collective-permute-start | bytes 442376 | tf_op jit(solution)/shard_map/ppermute | solution.py:312
  (5 other events, 17.1 us)

commit v8 on v7

--- a/solution.py
+++ b/solution.py
@@ -523,8 +523,9 @@
     zero.go()
     one.add().go()
     zero.add().go()
+    three.add().go()
+    behind(three, two)
     two.add().go()
-    three.add().go()
     one.add().go()
     zero.add().go()
     behind(zero, one, two)

time: 202 us -> 204 us (level)
  waiting for transfers between devices: 56.3 us -> 59.7 us
    ppermute x16, waiting for transfers between devices: 35.2 us -> 38.7 us  [go(): lax.ppermute(self.send, 'dp', [(i, i ^ 1 << bit) for i in range(self.repl...]
    convert_element_type x9 -> x11, other arithmetic: 13.5 us -> 12.9 us  [part(): total = (a.astype(F32) + b.astype(F32)).astype(self.keep.dtype)]
where the time goes in v8:
time: 204 us; the launch traced here: 203 us
  Pallas kernels  103 us (50%)
  waiting for transfers between devices  59.7 us (29%)
  starting transfers between devices  20.8 us (10%)
  other arithmetic  15.8 us (8%)
  local copies, waits for them, and re-layouts  2.7 us (1%)
    pallas_call x1, Pallas kernels, on_device(): call(first_pass, 'first_pass', (4, steps), [tok, pl.BlockSpec(wide, lambd...  41.2 us
    ppermute x16, waiting for transfers between devices, go(): lax.ppermute(self.send, 'dp', [(i, i ^ 1 << bit) for i in range(self.repl...  38.7 us
    ppermute x2, waiting for transfers between devices, on_device(): lax.ppermute(piece, 'section', [(i, i - 1) for i in range(1, sections)])  21 us
    pallas_call x1, Pallas kernels, on_device(): call(functools.partial(back_two_one, own), 'back_two_one', (steps,), [c_a...  18.7 us
    ppermute x16, starting transfers between devices, go(): lax.ppermute(self.send, 'dp', [(i, i ^ 1 << bit) for i in range(self.repl...  18.1 us
    pallas_call x1, Pallas kernels, on_device(): call(forward_second, 'forward_second', (2, steps), [pl.BlockSpec(chunk, l...  14.4 us
    convert_element_type x11, other arithmetic, part(): total = (a.astype(F32) + b.astype(F32)).astype(self.keep.dtype)  12.9 us
    pallas_call x1, Pallas kernels, on_device(): call(functools.partial(back_zero, own), 'back_zero', (2, steps), [held_at...  10.9 us
  transfers between devices with their start and end apart: 18, of which 9 were waited for; matrix products, arithmetic and copies ran while one was open for 7% of the time, Pallas kernels for 27%

profile of v8, /device:TPU:0, one launch (start us, length us, event | category | flops | bytes accessed | tf_op | source)
XLA Modules:
  0.0 203.1 jit_solution(6612122427985891678)
XLA Ops:
  2.0 41.2 %first_pass.1 = (bf16[8192,128]{1,0:T(8,128)(2,1)}, f32[128,128]{1,0:T(8,128)}, bf16[128,6144]{1,0:T(8,128)(2,1)}, bf16[128,2048]{1,0:T(8,128)(2,1)}) custom-call(s32[8192]{0:T(1024)} %bitcast.94, bf16[128,8192]{1,0:T(8,128)(2,1)} %bitcast.108, bf16[128,8192]{1,0:T(8,128)(2,1)} %cot.5, f32[128,128]{1,0:T(8,128)} %broadcast_in_dim.12.live, f32[1,8192]{1,0:T(1,128)} %gamma.3, ...), custom_call_target="tpu_custom_call" | custom-call | tf_op jit(solution)/shard_map/first_pass/pallas_call | solution.py:417
  46.0 14.4 %forward_second.1.cp_t = bf16[8192,128]{1,0:T(8,128)(2,1)S(1)} custom-call(s32[8192]{0:T(1024)S(1)} %bitcast.95, bf16[8192,128]{1,0:T(8,128)(2,1)} %get-tuple-element.56.ap_t, bf16[4,64,128,128]{3,2,1,0:T(8,128)(2,1)} %bitcast.101, bf16[4,64,128,128]{3,2,1,0:T(8,128)(2,1)} %bitcast.102), custom_call_target="tpu_custom_call" | custom-call | tf_op jit(solution)/shard_map/forward_second/pallas_call | solution.py:442
  61.8 21.0 %collective-permute-done.moved = bf16[128,6144]{1,0:T(8,128)(2,1)S(1)} collective-permute-done((bf16[128,6144]{1,0:T(8,128)(2,1)}, bf16[128,6144]{1,0:T(8,128)(2,1)S(1)}, u32[]{:S(2)}, u32[]{:S(2)}) %collective-permute-start) | collective-permute-done | bytes 1572896 | tf_op jit(solution)/shard_map/ppermute | solution.py:439
  82.9 10.8 %back_three_early.1 = (bf16[32,128,128]{2,1,0:T(8,128)(2,1)S(1)}, bf16[32,128,128]{2,1,0:T(8,128)(2,1)S(1)}, bf16[128,8192]{1,0:T(8,128)(2,1)}, f32[8192,128]{1,0:T(8,128)}) custom-call(s32[8192]{0:T(1024)S(1)} %bitcast.96, s32[2]{0:T(128)S(1)} %pad_add_fusion.flags, bf16[128,8192]{1,0:T(8,128)(2,1)} %cot.5, f32[128,128]{1,0:T(8,128)S(1)} %copy-done.1, ...), custom_call_target="tpu_custom_call" | custom-call | tf_op jit(solution)/shard_map/back_three_early/pallas_call | solution.py:459
  93.7 7.2 %back_three_late.1 = (bf16[32,128,128]{2,1,0:T(8,128)(2,1)S(1)}, bf16[32,128,128]{2,1,0:T(8,128)(2,1)S(1)}, bf16[128,8192]{1,0:T(8,128)(2,1)}, bf16[8192,128]{1,0:T(8,128)(2,1)}) custom-call(s32[8192]{0:T(1024)S(1)} %bitcast.97, s32[2]{0:T(128)S(1)} %pad_add_fusion.flags, ...), custom_call_target="tpu_custom_call", output_to_operand_aliasing={{0}: (7, {}), {1}: (8, {}), {2}: (9, {})} | custom-call | tf_op jit(solution)/shard_map/back_three_late/pallas_call | solution.py:472
  100.9 18.7 %back_two_one.1 = (bf16[32,128,128]{2,1,0:T(8,128)(2,1)S(1)}, bf16[32,128,128]{2,1,0:T(8,128)(2,1)}, bf16[32,128,128]{2,1,0:T(8,128)(2,1)S(1)}, bf16[32,128,128]{2,1,0:T(8,128)(2,1)}, bf16[8192,128]{1,0:T(8,128)(2,1)}) custom-call(s32[8192]{0:T(1024)S(1)} %bitcast.98, s32[2]{0:T(128)S(1)} %pad_add_fusion.flags, bf16[8192,128]{1,0:T(8,128)(2,1)} %get-tuple-element.69.gc_t, ...), custom_call_target="tpu_custom_call" | custom-call | tf_op jit(solution)/shard_map/back_two_one/pallas_call | solution.py:485
  120.3 2.4 %add_convert_fusion.6 = (bf16[4,1,4,128,128]{4,3,2,1,0:T(8,128)(2,1)S(1)}, bf16[4,1,4,128,128]{4,3,2,1,0:T(8,128)(2,1)}) fusion(bf16[4,2,4,128,128]{4,3,2,1,0:T(8,128)(2,1)} %bitcast.6, s32[]{:T(128)S(6)} %select_n.68, bf16[4,2,4,128,128]{4,3,2,1,0:T(8,128)(2,1)S(1)} %bitcast.90, s32[]{:T(128)S(6)} %select_n.67), kind=kLoop, calls=%fused_computation.7 | loop fusion | flops 2097152 | bytes 3145736 | tf_op jit(solution)/shard_map/convert_element_type | solution.py:328
  122.7 2.7 %collective-permute-start.5 = (bf16[16,128,128]{2,1,0:T(8,128)(2,1)S(1)}, bf16[16,128,128]{2,1,0:T(8,128)(2,1)}, u32[]{:S(2)}, u32[]{:S(2)}) collective-permute-start(bf16[16,128,128]{2,1,0:T(8,128)(2,1)S(1)} %bitcast.124), channel_id=1, source_target_pairs={{0,2},{1,3},{2,0},{3,1},{4,6},{5,7},{6,4},{7,5},{8,10},{9,11},{10,... | collective-permute-start | bytes 1572872 | tf_op jit(solution)/shard_map/ppermute | solution.py:312
  125.4 10.9 %back_zero.1 = (bf16[32,144,128]{2,1,0:T(8,128)(2,1)S(1)}, bf16[32,144,128]{2,1,0:T(8,128)(2,1)}, bf16[128,8192]{1,0:T(8,128)(2,1)}) custom-call(s32[2]{0:T(128)S(1)} %pad_add_fusion.flags, bf16[8192,128]{1,0:T(8,128)(2,1)} %get-tuple-element.84.ga_t, bf16[128,8192]{1,0:T(8,128)(2,1)} %get-tuple-element.85.gy, bf16[128,8192]{1,0:T(8,128)(2,1)} %bitcast.109, ...), custom_call_target="tpu_custom_call" | custom-call | tf_op jit(solution)/shard_map/back_zero/pallas_call | solution.py:505
  136.2 1.8 collective-permute-done.5
  139.6 1.8 collective-permute-start.8
  141.4 2.4 %add_convert_fusion.1 = (bf16[4,1,4,144,128]{4,3,2,1,0:T(8,128)(2,1)S(1)}, bf16[4,1,4,144,128]{4,3,2,1,0:T(8,128)(2,1)}) fusion(bf16[4,2,4,144,128]{4,3,2,1,0:T(8,128)(2,1)} %bitcast.11, s32[]{:T(128)S(6)} %select_n.67, bf16[4,2,4,144,128]{4,3,2,1,0:T(8,128)(2,1)S(1)} %bitcast.91, s32[]{:T(128)S(6)} %select_n.68), kind=kLoop, calls=%fused_computation.1 | loop fusion | flops 2359296 | bytes 3538952 | tf_op jit(solution)/shard_map/convert_element_type | solution.py:328
  145.4 1.9 add_convert_fusion.13
  147.3 2.4 %add_convert_fusion.2 = (bf16[2,1,8,128,128]{4,3,2,1,0:T(8,128)(2,1)}, bf16[2,1,8,128,128]{4,3,2,1,0:T(8,128)(2,1)S(1)}) fusion(bf16[2,2,8,128,128]{4,3,2,1,0:T(8,128)(2,1)} %bitcast.27, s32[]{:T(128)S(6)} %select_n.70, bf16[2,2,8,128,128]{4,3,2,1,0:T(8,128)(2,1)S(1)} %bitcast.92, s32[]{:T(128)S(6)} %select_n.69), kind=kLoop, calls=%fused_computation.3 | loop fusion | flops 2097152 | bytes 3145736 | tf_op jit(solution)/shard_map/convert_element_type | solution.py:328
  151.7 2.7 %collective-permute-done.8 = bf16[16,128,128]{2,1,0:T(8,128)(2,1)S(1)} collective-permute-done((bf16[16,128,128]{2,1,0:T(8,128)(2,1)S(1)}, bf16[16,128,128]{2,1,0:T(8,128)(2,1)S(1)}, u32[]{:S(2)}, u32[]{:S(2)}) %collective-permute-start.8) | collective-permute-done | bytes 524320 | tf_op jit(solution)/shard_map/ppermute | solution.py:312
  155.2 1.8 collective-permute-start.9
  157.1 13.2 %collective-permute-done.16 = bf16[8,128,128]{2,1,0:T(8,128)(2,1)S(1)} collective-permute-done((bf16[8,128,128]{2,1,0:T(8,128)(2,1)}, bf16[8,128,128]{2,1,0:T(8,128)(2,1)S(1)}, u32[]{:S(2)}, u32[]{:S(2)}) %collective-permute-start.16) | collective-permute-done | bytes 262176 | tf_op jit(solution)/shard_map/ppermute | solution.py:312
  170.3 2.7 %collective-permute-start.17 = (bf16[4,128,128]{2,1,0:T(8,128)(2,1)S(1)}, bf16[4,128,128]{2,1,0:T(8,128)(2,1)S(1)}, u32[]{:S(2)}, u32[]{:S(2)}) collective-permute-start(bf16[4,128,128]{2,1,0:T(8,128)(2,1)S(1)} %fusion.12), channel_id=1, source_target_pairs={{0,8},{1,9},{2,10},{3,11},{4,12},{5,13},{6,14},{7,15},{8,0},{9,1},... | collective-permute-start | bytes 393224 | tf_op jit(solution)/shard_map/ppermute | solution.py:312
  173.2 4.5 %collective-permute-done.9 = bf16[8,128,128]{2,1,0:T(8,128)(2,1)} collective-permute-done((bf16[8,128,128]{2,1,0:T(8,128)(2,1)}, bf16[8,128,128]{2,1,0:T(8,128)(2,1)}, u32[]{:S(2)}, u32[]{:S(2)}) %collective-permute-start.9) | collective-permute-done | bytes 262176 | tf_op jit(solution)/shard_map/ppermute | solution.py:312
  180.4 2.5 %collective-permute-start.11 = (bf16[8,144,128]{2,1,0:T(8,128)(2,1)S(1)}, bf16[8,144,128]{2,1,0:T(8,128)(2,1)S(1)}, u32[]{:S(2)}, u32[]{:S(2)}) collective-permute-start(bf16[8,144,128]{2,1,0:T(8,128)(2,1)S(1)} %bitcast.127), channel_id=1, source_target_pairs={{0,4},{1,5},{2,6},{3,7},{4,0},{5,1},{6,2},{7,3},{8,12},{9,13},{10,... | collective-permute-start | bytes 884744 | tf_op jit(solution)/shard_map/ppermute | solution.py:312
  182.9 1.8 collective-permute-done.14
  185.5 2.5 %collective-permute-done.13 = bf16[4,128,128]{2,1,0:T(8,128)(2,1)S(1)} collective-permute-done((bf16[4,128,128]{2,1,0:T(8,128)(2,1)S(1)}, bf16[4,128,128]{2,1,0:T(8,128)(2,1)S(1)}, u32[]{:S(2)}, u32[]{:S(2)}) %collective-permute-start.13) | collective-permute-done | bytes 131104 | tf_op jit(solution)/shard_map/ppermute | solution.py:312
  189.0 4.9 %collective-permute-done.11 = bf16[8,144,128]{2,1,0:T(8,128)(2,1)S(1)} collective-permute-done((bf16[8,144,128]{2,1,0:T(8,128)(2,1)S(1)}, bf16[8,144,128]{2,1,0:T(8,128)(2,1)S(1)}, u32[]{:S(2)}, u32[]{:S(2)}) %collective-permute-start.11) | collective-permute-done | bytes 294944 | tf_op jit(solution)/shard_map/ppermute | solution.py:312
  194.1 7.3 %collective-permute-done.12 = bf16[4,144,128]{2,1,0:T(8,128)(2,1)S(1)} collective-permute-done((bf16[4,144,128]{2,1,0:T(8,128)(2,1)S(1)}, bf16[4,144,128]{2,1,0:T(8,128)(2,1)S(1)}, u32[]{:S(2)}, u32[]{:S(2)}) %collective-permute-start.12) | collective-permute-done | bytes 147488 | tf_op jit(solution)/shard_map/ppermute | solution.py:312
  (56 shorter events, 18.8 us)
Async XLA Ops:
  2.0 44.0 %copy-start.2 = (s32[1,8192]{1,0:T(1,128)S(1)}, s32[1,8192]{1,0:T(1,128)}, u32[]{:S(2)}) copy-start(s32[1,8192]{1,0:T(1,128)} %param.11) | copy-start | bytes 98308
  43.2 39.7 %collective-permute-start = (bf16[128,6144]{1,0:T(8,128)(2,1)}, bf16[128,6144]{1,0:T(8,128)(2,1)S(1)}, u32[]{:S(2)}, u32[]{:S(2)}) collective-permute-start(bf16[128,6144]{1,0:T(8,128)(2,1)} %get-tuple-element.55), channel_id=1, source_target_pairs={{16,0},{17,1},{18,2},{19,3},{20,4},{21,5},{22,6},{23,7},{24,8},{25... | collective-permute-start | bytes 4718600 | tf_op jit(solution)/shard_map/ppermute | solution.py:439
  44.5 49.2 %collective-permute-start.1 = (bf16[128,2048]{1,0:T(8,128)(2,1)}, bf16[128,2048]{1,0:T(8,128)(2,1)S(1)}, u32[]{:S(2)}, u32[]{:S(2)}) collective-permute-start(bf16[128,2048]{1,0:T(8,128)(2,1)} %get-tuple-element.61), channel_id=1, source_target_pairs={{16,0},{17,1},{18,2},{19,3},{20,4},{21,5},{22,6},{23,7},{24,8},{25... | collective-permute-start | bytes 1572872 | tf_op jit(solution)/shard_map/ppermute | solution.py:439
  46.0 36.9 %copy-start.1 = (f32[128,128]{1,0:T(8,128)S(1)}, f32[128,128]{1,0:T(8,128)}, u32[]{:S(2)}) copy-start(f32[128,128]{1,0:T(8,128)} %broadcast_in_dim.12.live) | copy-start | bytes 196612
  100.9 18.7 %collective-permute-start.2 = (bf16[32,128,128]{2,1,0:T(8,128)(2,1)S(1)}, bf16[32,128,128]{2,1,0:T(8,128)(2,1)}, u32[]{:S(2)}, u32[]{:S(2)}) collective-permute-start(bf16[32,128,128]{2,1,0:T(8,128)(2,1)S(1)} %get-tuple-element.68), channel_id=1, source_target_pairs={{0,1},{1,0},{2,3},{3,2},{4,5},{5,4},{6,7},{7,6},{8,9},{9,8},{10,11... | collective-permute-start | bytes 3145736 | tf_op jit(solution)/shard_map/ppermute | solution.py:312
  119.6 18.4 %collective-permute-start.3 = (bf16[32,128,128]{2,1,0:T(8,128)(2,1)}, bf16[32,128,128]{2,1,0:T(8,128)(2,1)}, u32[]{:S(2)}, u32[]{:S(2)}) collective-permute-start(bf16[32,128,128]{2,1,0:T(8,128)(2,1)} %get-tuple-element.76), channel_id=1, source_target_pairs={{0,1},{1,0},{2,3},{3,2},{4,5},{5,4},{6,7},{7,6},{8,9},{9,8},{10,11... | collective-permute-start | bytes 3145736 | tf_op jit(solution)/shard_map/ppermute | solution.py:312
  120.2 17.8 %collective-permute-start.4 = (bf16[32,128,128]{2,1,0:T(8,128)(2,1)}, bf16[32,128,128]{2,1,0:T(8,128)(2,1)}, u32[]{:S(2)}, u32[]{:S(2)}) collective-permute-start(bf16[32,128,128]{2,1,0:T(8,128)(2,1)} %get-tuple-element.78), channel_id=1, source_target_pairs={{0,1},{1,0},{2,3},{3,2},{4,5},{5,4},{6,7},{7,6},{8,9},{9,8},{10,11... | collective-permute-start | bytes 3145736 | tf_op jit(solution)/shard_map/ppermute | solution.py:312
  120.3 5.1 %copy-start.3 = (f32[1,8192]{1,0:T(1,128)S(1)}, f32[1,8192]{1,0:T(1,128)}, u32[]{:S(2)}) copy-start(f32[1,8192]{1,0:T(1,128)} %gamma.3) | copy-start | bytes 98308
  120.3 5.1 %copy-start.4 = (f32[128,128]{1,0:T(8,128)S(1)}, f32[128,128]{1,0:T(8,128)}, u32[]{:S(2)}) copy-start(f32[128,128]{1,0:T(8,128)} %get-tuple-element.86.scale) | copy-start | bytes 196612
  122.7 15.3 %collective-permute-start.5 = (bf16[16,128,128]{2,1,0:T(8,128)(2,1)S(1)}, bf16[16,128,128]{2,1,0:T(8,128)(2,1)}, u32[]{:S(2)}, u32[]{:S(2)}) collective-permute-start(bf16[16,128,128]{2,1,0:T(8,128)(2,1)S(1)} %bitcast.124), channel_id=1, source_target_pairs={{0,2},{1,3},{2,0},{3,1},{4,6},{5,7},{6,4},{7,5},{8,10},{9,11},{10,... | collective-permute-start | bytes 1572872 | tf_op jit(solution)/shard_map/ppermute | solution.py:312
  138.0 3.4 %collective-permute-start.6 = (bf16[32,144,128]{2,1,0:T(8,128)(2,1)}, bf16[32,144,128]{2,1,0:T(8,128)(2,1)}, u32[]{:S(2)}, u32[]{:S(2)}) collective-permute-start(bf16[32,144,128]{2,1,0:T(8,128)(2,1)} %get-tuple-element.92), channel_id=1, source_target_pairs={{0,1},{1,0},{2,3},{3,2},{4,5},{5,4},{6,7},{7,6},{8,9},{9,8},{10,11... | collective-permute-start | bytes 3538952 | tf_op jit(solution)/shard_map/ppermute | solution.py:312
  139.6 14.8 %collective-permute-start.8 = (bf16[16,128,128]{2,1,0:T(8,128)(2,1)S(1)}, bf16[16,128,128]{2,1,0:T(8,128)(2,1)S(1)}, u32[]{:S(2)}, u32[]{:S(2)}) collective-permute-start(bf16[16,128,128]{2,1,0:T(8,128)(2,1)S(1)} %bitcast.123), channel_id=1, source_target_pairs={{0,2},{1,3},{2,0},{3,1},{4,6},{5,7},{6,4},{7,5},{8,10},{9,11},{10,... | collective-permute-start | bytes 1572872 | tf_op jit(solution)/shard_map/ppermute | solution.py:312
  141.4 4.0 %copy-start.5 = (bf16[4,1,4,128,128]{4,3,2,1,0:T(8,128)(2,1)S(1)}, bf16[4,1,4,128,128]{4,3,2,1,0:T(8,128)(2,1)}, u32[]{:S(2)}) copy-start(bf16[4,1,4,128,128]{4,3,2,1,0:T(8,128)(2,1)} %get-tuple-element.114) | copy-start | bytes 1572868
  143.8 29.1 %collective-permute-start.7 = (bf16[16,144,128]{2,1,0:T(8,128)(2,1)}, bf16[16,144,128]{2,1,0:T(8,128)(2,1)S(1)}, u32[]{:S(2)}, u32[]{:S(2)}) collective-permute-start(bf16[16,144,128]{2,1,0:T(8,128)(2,1)} %bitcast.13), channel_id=1, source_target_pairs={{0,2},{1,3},{2,0},{3,1},{4,6},{5,7},{6,4},{7,5},{8,10},{9,11},{10,... | collective-permute-start | bytes 1769480 | tf_op jit(solution)/shard_map/ppermute | solution.py:312
  149.6 23.5 %collective-permute-start.10 = (bf16[16,128,128]{2,1,0:T(8,128)(2,1)}, bf16[16,128,128]{2,1,0:T(8,128)(2,1)S(1)}, u32[]{:S(2)}, u32[]{:S(2)}) collective-permute-start(bf16[16,128,128]{2,1,0:T(8,128)(2,1)} %bitcast.29), channel_id=1, source_target_pairs={{0,4},{1,5},{2,6},{3,7},{4,0},{5,1},{6,2},{7,3},{8,12},{9,13},{10,... | collective-permute-start | bytes 1572872 | tf_op jit(solution)/shard_map/ppermute | solution.py:312
  151.2 19.1 %collective-permute-start.16 = (bf16[8,128,128]{2,1,0:T(8,128)(2,1)}, bf16[8,128,128]{2,1,0:T(8,128)(2,1)S(1)}, u32[]{:S(2)}, u32[]{:S(2)}) collective-permute-start(bf16[8,128,128]{2,1,0:T(8,128)(2,1)} %bitcast.49), channel_id=1, source_target_pairs={{0,4},{1,5},{2,6},{3,7},{4,0},{5,1},{6,2},{7,3},{8,12},{9,13},{10,... | collective-permute-start | bytes 786440 | tf_op jit(solution)/shard_map/ppermute | solution.py:312
  155.2 22.4 %collective-permute-start.9 = (bf16[8,128,128]{2,1,0:T(8,128)(2,1)}, bf16[8,128,128]{2,1,0:T(8,128)(2,1)}, u32[]{:S(2)}, u32[]{:S(2)}) collective-permute-start(bf16[8,128,128]{2,1,0:T(8,128)(2,1)} %bitcast.22), channel_id=1, source_target_pairs={{0,4},{1,5},{2,6},{3,7},{4,0},{5,1},{6,2},{7,3},{8,12},{9,13},{10,... | collective-permute-start | bytes 786440 | tf_op jit(solution)/shard_map/ppermute | solution.py:312
  170.3 10.0 %collective-permute-start.17 = (bf16[4,128,128]{2,1,0:T(8,128)(2,1)S(1)}, bf16[4,128,128]{2,1,0:T(8,128)(2,1)S(1)}, u32[]{:S(2)}, u32[]{:S(2)}) collective-permute-start(bf16[4,128,128]{2,1,0:T(8,128)(2,1)S(1)} %fusion.12), channel_id=1, source_target_pairs={{0,8},{1,9},{2,10},{3,11},{4,12},{5,13},{6,14},{7,15},{8,0},{9,1},... | collective-permute-start | bytes 393224 | tf_op jit(solution)/shard_map/ppermute | solution.py:312
  173.0 7.4 %copy-start.7 = (bf16[8,128,128]{2,1,0:T(8,128)(2,1)S(1)}, bf16[8,128,128]{2,1,0:T(8,128)(2,1)}, u32[]{:S(2)}) copy-start(bf16[8,128,128]{2,1,0:T(8,128)(2,1)} %copy-done.6) | copy-start | bytes 786436
  177.8 6.9 %collective-permute-start.14 = (bf16[8,128,128]{2,1,0:T(8,128)(2,1)S(1)}, bf16[8,128,128]{2,1,0:T(8,128)(2,1)S(1)}, u32[]{:S(2)}, u32[]{:S(2)}) collective-permute-start(bf16[8,128,128]{2,1,0:T(8,128)(2,1)S(1)} %bitcast.132), channel_id=1, source_target_pairs={{0,2},{1,3},{2,0},{3,1},{4,6},{5,7},{6,4},{7,5},{8,10},{9,11},{10,... | collective-permute-start | bytes 786440 | tf_op jit(solution)/shard_map/ppermute | solution.py:312
  179.4 8.6 %collective-permute-start.13 = (bf16[4,128,128]{2,1,0:T(8,128)(2,1)S(1)}, bf16[4,128,128]{2,1,0:T(8,128)(2,1)S(1)}, u32[]{:S(2)}, u32[]{:S(2)}) collective-permute-start(bf16[4,128,128]{2,1,0:T(8,128)(2,1)S(1)} %fusion.10), channel_id=1, source_target_pairs={{0,8},{1,9},{2,10},{3,11},{4,12},{5,13},{6,14},{7,15},{8,0},{9,1},... | collective-permute-start | bytes 393224 | tf_op jit(solution)/shard_map/ppermute | solution.py:312
  180.4 13.5 %collective-permute-start.11 = (bf16[8,144,128]{2,1,0:T(8,128)(2,1)S(1)}, bf16[8,144,128]{2,1,0:T(8,128)(2,1)S(1)}, u32[]{:S(2)}, u32[]{:S(2)}) collective-permute-start(bf16[8,144,128]{2,1,0:T(8,128)(2,1)S(1)} %bitcast.127), channel_id=1, source_target_pairs={{0,4},{1,5},{2,6},{3,7},{4,0},{5,1},{6,2},{7,3},{8,12},{9,13},{10,... | collective-permute-start | bytes 884744 | tf_op jit(solution)/shard_map/ppermute | solution.py:312
  184.8 9.2 %collective-permute-start.15 = (bf16[4,128,128]{2,1,0:T(8,128)(2,1)S(1)}, bf16[4,128,128]{2,1,0:T(8,128)(2,1)S(1)}, u32[]{:S(2)}, u32[]{:S(2)}) collective-permute-start(bf16[4,128,128]{2,1,0:T(8,128)(2,1)S(1)} %fusion.14), channel_id=1, source_target_pairs={{0,8},{1,9},{2,10},{3,11},{4,12},{5,13},{6,14},{7,15},{8,0},{9,1},... | collective-permute-start | bytes 393224 | tf_op jit(solution)/shard_map/ppermute | solution.py:312
  193.9 7.4 %collective-permute-start.12 = (bf16[4,144,128]{2,1,0:T(8,128)(2,1)S(1)}, bf16[4,144,128]{2,1,0:T(8,128)(2,1)S(1)}, u32[]{:S(2)}, u32[]{:S(2)}) collective-permute-start(bf16[4,144,128]{2,1,0:T(8,128)(2,1)S(1)} %fusion.8), channel_id=1, source_target_pairs={{0,8},{1,9},{2,10},{3,11},{4,12},{5,13},{6,14},{7,15},{8,0},{9,1},... | collective-permute-start | bytes 442376 | tf_op jit(solution)/shard_map/ppermute | solution.py:312
  (2 other events, 4.1 us)
